TPU v7x, 32 devices: a whole 2x2x4 slice. The times are simulated.
32 devices in a mesh: seq: 8 (over z, y), head: 4 (over x, core).
Axes of the slice: x: 2, y: 2, z: 4, core: 2. Of those that a mesh axis runs over, the one named last changes fastest.
Arguments:
- queries: bfloat16 [4096, 2048], P(('seq', 'head')), may hold values from -6 to 6
- output_gradient: bfloat16 [4096, 2048], P(('seq', 'head')), may hold values from -6 to 6
- outputs: bfloat16 [4096, 2048], P(('seq', 'head')), may hold values from -6 to 6
- key_vectors: bfloat16 [4096, 1024], P(('seq', 'head')), may hold values from -6 to 6
- values: bfloat16 [4096, 1024], P(('seq', 'head')), may hold values from -6 to 6
- logsum: float32 [16, 4096], P('head', 'seq'), as said below
- pair_list: int32 [20, 3], replicated, may hold values from 0 to 7, as said below
Outputs:
- grad_queries: bfloat16 [4096, 2048], P(('seq', 'head'))
- key_gradient: bfloat16 [4096, 1024], P(('seq', 'head'))
- value_gradient: bfloat16 [4096, 1024], P(('seq', 'head'))
Inputs may be any that keep to these rules, and one draw needn't show every extreme that they name: `pair_list`: every block b has the row (b, b, 1). Every other row (a, c, m) has 1 <= a - c <= 4 and m equal to 0 or 2. No pair appears twice; rows come in no particular order. A query block has between 1 and 5 rows, and block 7 has 5. `logsum`: each entry lies between ln(512) + 0.5 and ln(2560) + 0.5.
All inputs are finite; a program needn't handle non-finite values.
Results may differ from a plain program's by a relative error of at most 0.0054.
Values may be sent and summed in bfloat16 or wider, within the bound.
No kernel may reach another device: no remote copies, remote signals or barrier semaphores. Data moves between devices by JAX's collectives and lax.ppermute only.
A program may use at most 64 MiB of HBM per device.

v0:
```python
import jax
import jax.numpy as jnp
from jax import lax
from jax.sharding import PartitionSpec as P

HEAD_SIZE = 128
KEY_VALUE_HEADS = 8
QUERY_HEADS = 16
WIN = 5


def from_behind(value, axis, steps):
    count = lax.axis_size(axis)
    first, last = (max(0, -steps), min(count, count - steps))
    return lax.ppermute(value, axis, [(source, source + steps) for source in range(first, last)])


def pair_grads(q_heads, do_heads, lse_heads, delta_heads, k_block, v_block, pair_code):
    score_scale = 1.0 / jnp.sqrt(jnp.float32(HEAD_SIZE))
    blk_rows = q_heads.shape[0]
    scores = (
        jnp.einsum("qkgd,skd->kgqs", q_heads, k_block, preferred_element_type=jnp.float32)
        * score_scale
    )
    row_ids = jnp.arange(blk_rows)[:, None]
    col_ids = jnp.arange(blk_rows)[None, :]
    allowed = (
        (pair_code == 1)
        | (pair_code == 2) & (col_ids <= row_ids)
        | (pair_code == 3) & (col_ids > row_ids)
    )
    probs = jnp.where(allowed, jnp.exp(scores - lse_heads[..., None]), jnp.float32(0.0))
    probs_low = probs.astype(jnp.bfloat16)
    grad_v = jnp.einsum("kgqs,qkgd->skd", probs_low, do_heads, preferred_element_type=jnp.float32)
    dprobs = jnp.einsum("qkgd,skd->kgqs", do_heads, v_block, preferred_element_type=jnp.float32)
    dscores = (probs * (dprobs - delta_heads[..., None]) * score_scale).astype(jnp.bfloat16)
    grad_q = jnp.einsum("kgqs,skd->qkgd", dscores, k_block, preferred_element_type=jnp.float32)
    grad_k = jnp.einsum("kgqs,qkgd->skd", dscores, q_heads, preferred_element_type=jnp.float32)
    return (grad_q, jnp.stack([grad_k, grad_v], axis=0))


def shards(queries, output_gradient, outputs, key_vectors, values, logsum, pair_list):
    number_of_heads = lax.axis_size("head")
    local_q = QUERY_HEADS // number_of_heads
    resident_key_value = KEY_VALUE_HEADS // number_of_heads
    group_count = QUERY_HEADS // KEY_VALUE_HEADS
    q_cols, do_cols, o_cols, k_cols, v_cols = (
        lax.all_to_all(queries, "head", split_axis=1, concat_axis=0, tiled=True),
        lax.all_to_all(output_gradient, "head", split_axis=1, concat_axis=0, tiled=True),
        lax.all_to_all(outputs, "head", split_axis=1, concat_axis=0, tiled=True),
        lax.all_to_all(key_vectors, "head", split_axis=1, concat_axis=0, tiled=True),
        lax.all_to_all(values, "head", split_axis=1, concat_axis=0, tiled=True),
    )
    blk_rows = q_cols.shape[0]
    delta_rows = jnp.sum(
        do_cols.astype(jnp.float32).reshape(blk_rows, local_q, HEAD_SIZE)
        * o_cols.astype(jnp.float32).reshape(blk_rows, local_q, HEAD_SIZE),
        axis=-1,
    )
    q_heads = q_cols.reshape(blk_rows, resident_key_value, group_count, HEAD_SIZE)
    do_heads = do_cols.reshape(blk_rows, resident_key_value, group_count, HEAD_SIZE)
    lse_heads = logsum.reshape(resident_key_value, group_count, blk_rows)
    delta_heads = delta_rows.T.reshape(resident_key_value, group_count, blk_rows)
    own_kv = jnp.stack(
        [
            k_cols.reshape(blk_rows, resident_key_value, HEAD_SIZE),
            v_cols.reshape(blk_rows, resident_key_value, HEAD_SIZE),
        ],
        axis=0,
    )
    my_block = lax.axis_index("seq")
    zero_q = jnp.zeros((blk_rows, resident_key_value, group_count, HEAD_SIZE), jnp.float32)
    zero_kv = jnp.zeros((2, blk_rows, resident_key_value, HEAD_SIZE), jnp.float32)
    acc_q = zero_q
    travel = own_kv
    kv_parts = []
    for offset in range(WIN):
        if offset > 0:
            travel = from_behind(travel, "seq", 1)
        matches = (pair_list[:, 0] == my_block) & (pair_list[:, 1] == my_block - offset)
        pair_code = jnp.sum(jnp.where(matches, pair_list[:, 2] + 1, 0))

        def compute_pair(operand):
            return pair_grads(
                q_heads, do_heads, lse_heads, delta_heads, operand[0], operand[1], pair_code
            )

        def skip_pair(operand):
            return (zero_q, zero_kv)

        part_q, part_kv = lax.cond(pair_code > 0, compute_pair, skip_pair, travel)
        acc_q = acc_q + part_q
        kv_parts.append(part_kv)
    acc_kv = kv_parts[WIN - 1]
    for offset in range(WIN - 2, -1, -1):
        acc_kv = from_behind(acc_kv, "seq", -1) + kv_parts[offset]
    grad_q_low = acc_q.reshape(blk_rows, local_q * HEAD_SIZE).astype(jnp.bfloat16)
    grad_k_low = acc_kv[0].reshape(blk_rows, resident_key_value * HEAD_SIZE).astype(jnp.bfloat16)
    grad_v_low = acc_kv[1].reshape(blk_rows, resident_key_value * HEAD_SIZE).astype(jnp.bfloat16)
    grad_queries, key_gradient, value_gradient = (
        lax.all_to_all(grad_q_low, "head", split_axis=0, concat_axis=1, tiled=True),
        lax.all_to_all(grad_k_low, "head", split_axis=0, concat_axis=1, tiled=True),
        lax.all_to_all(grad_v_low, "head", split_axis=0, concat_axis=1, tiled=True),
    )
    return (grad_queries, key_gradient, value_gradient)


def solution(mesh):
    in_specs = (
        P(("seq", "head"), None),
        P(("seq", "head"), None),
        P(("seq", "head"), None),
        P(("seq", "head"), None),
        P(("seq", "head"), None),
        P("head", "seq"),
        P(),
    )
    out_specs = (P(("seq", "head"), None), P(("seq", "head"), None), P(("seq", "head"), None))
    return jax.shard_map(shards, mesh=mesh, in_specs=in_specs, out_specs=out_specs, check_vma=False)
```

profile of v0, /device:TPU:24, one launch (start us, length us, event | category | flops | bytes accessed | tf_op | source)
XLA Modules:
  0.0 243.2 jit_solution(16844846447018662661)
XLA Ops:
  2.5 3.4 %all-to-all-start = ((bf16[128,4,256]{0,2,1:T(8,128)(2,1)}), bf16[128,4,256]{0,2,1:T(8,128)(2,1)S(1)}, u32[]{:S(2)}, u32[]{:S(2)}) async-start(bf16[128,4,256]{0,2,1:T(8,128)(2,1)} %bitcast.82), calls=%async_computation | async-start | bytes 524288 | tf_op jit(solution)/shard_map/all_to_all | solution.py:51
  7.8 4.1 %all-to-all-done = bf16[128,4,256]{0,2,1:T(8,128)(2,1)S(1)} async-done(((bf16[128,4,256]{0,2,1:T(8,128)(2,1)}), bf16[128,4,256]{0,2,1:T(8,128)(2,1)S(1)}, u32[]{:S(2)}, u32[]{:S(2)}) %all-to-all-start) | async-done | bytes 262176 | tf_op jit(solution)/shard_map/all_to_all | solution.py:51
  11.9 3.4 %all-to-all-start.2 = ((bf16[128,4,256]{0,2,1:T(8,128)(2,1)}), bf16[128,4,256]{0,2,1:T(8,128)(2,1)S(1)}, u32[]{:S(2)}, u32[]{:S(2)}) async-start(bf16[128,4,256]{0,2,1:T(8,128)(2,1)} %bitcast.85), calls=%async_computation.2 | async-start | bytes 524288 | tf_op jit(solution)/shard_map/all_to_all | solution.py:52
  15.6 5.7 %all-to-all-done.2 = bf16[128,4,256]{0,2,1:T(8,128)(2,1)S(1)} async-done(((bf16[128,4,256]{0,2,1:T(8,128)(2,1)}), bf16[128,4,256]{0,2,1:T(8,128)(2,1)S(1)}, u32[]{:S(2)}, u32[]{:S(2)}) %all-to-all-start.2) | async-done | bytes 262176 | tf_op jit(solution)/shard_map/all_to_all | solution.py:52
  22.3 3.4 %collective-permute-start = (bf16[2,512,2,128]{3,2,1,0:T(2,128)(2,1)S(1)}, bf16[2,512,2,128]{3,2,1,0:T(2,128)(2,1)S(1)}, u32[]{:S(2)}, u32[]{:S(2)}) collective-permute-start(bf16[2,512,2,128]{3,2,1,0:T(2,128)(2,1)S(1)} %pad_maximum_fusion.5), channel_id=1, source_target_pairs={{0,4},{4,8},{8,12},{12,16},{16,20},{20,24},{24,28},{1,5},{5,9},{9,... | collective-permute-start | bytes 1572872 | tf_op jit(solution)/shard_map/ppermute | solution.py:15
  25.7 12.7 %collective-permute-done = bf16[2,512,2,128]{3,2,1,0:T(2,128)(2,1)S(1)} collective-permute-done((bf16[2,512,2,128]{3,2,1,0:T(2,128)(2,1)S(1)}, bf16[2,512,2,128]{3,2,1,0:T(2,128)(2,1)S(1)}, u32[]{:S(2)}, u32[]{:S(2)}) %collective-permute-start) | collective-permute-done | bytes 524320 | tf_op jit(solution)/shard_map/ppermute | solution.py:15
  38.4 2.5 %collective-permute-start.1 = (bf16[2,512,2,128]{3,2,1,0:T(2,128)(2,1)S(1)}, bf16[2,512,2,128]{3,2,1,0:T(2,128)(2,1)}, u32[]{:S(2)}, u32[]{:S(2)}) collective-permute-start(bf16[2,512,2,128]{3,2,1,0:T(2,128)(2,1)S(1)} %collective-permute-done), channel_id=1, source_target_pairs={{0,4},{4,8},{8,12},{12,16},{16,20},{20,24},{24,28},{1,5},{5,9},{9,... | collective-permute-start | bytes 1572872 | tf_op jit(solution)/shard_map/ppermute | solution.py:15
  41.8 3.5 %all-to-all-start.3 = ((bf16[128,4,512]{2,0,1:T(8,128)(2,1)}), bf16[128,4,512]{2,0,1:T(8,128)(2,1)S(1)}, u32[]{:S(2)}, u32[]{:S(2)}) async-start(bf16[128,4,512]{2,0,1:T(8,128)(2,1)} %bitcast.276), calls=%async_computation.3 | async-start | bytes 1048576 | tf_op jit(solution)/shard_map/all_to_all | solution.py:49
  45.3 8.5 %collective-permute-done.1 = bf16[2,512,2,128]{3,2,1,0:T(2,128)(2,1)} collective-permute-done((bf16[2,512,2,128]{3,2,1,0:T(2,128)(2,1)S(1)}, bf16[2,512,2,128]{3,2,1,0:T(2,128)(2,1)}, u32[]{:S(2)}, u32[]{:S(2)}) %collective-permute-start.1) | collective-permute-done | bytes 524320 | tf_op jit(solution)/shard_map/ppermute | solution.py:15
  53.8 1.9 collective-permute-start.2
  56.6 3.5 %all-to-all-start.4 = ((bf16[128,4,512]{2,0,1:T(8,128)(2,1)}), bf16[128,4,512]{2,0,1:T(8,128)(2,1)S(1)}, u32[]{:S(2)}, u32[]{:S(2)}) async-start(bf16[128,4,512]{2,0,1:T(8,128)(2,1)} %bitcast.275), calls=%async_computation.4 | async-start | bytes 1048576 | tf_op jit(solution)/shard_map/all_to_all | solution.py:50
  60.1 8.5 %collective-permute-done.2 = bf16[2,512,2,128]{3,2,1,0:T(2,128)(2,1)} collective-permute-done((bf16[2,512,2,128]{3,2,1,0:T(2,128)(2,1)}, bf16[2,512,2,128]{3,2,1,0:T(2,128)(2,1)}, u32[]{:S(2)}, u32[]{:S(2)}) %collective-permute-start.2) | collective-permute-done | bytes 524320 | tf_op jit(solution)/shard_map/ppermute | solution.py:15
  68.6 1.9 collective-permute-start.3
  71.4 4.3 %all-to-all-start.1 = ((bf16[128,4,512]{2,0,1:T(8,128)(2,1)}), bf16[128,4,512]{2,0,1:T(8,128)(2,1)}, u32[]{:S(2)}, u32[]{:S(2)}) async-start(bf16[128,4,512]{2,0,1:T(8,128)(2,1)} %bitcast.277), calls=%async_computation.1 | async-start | bytes 1048576 | tf_op jit(solution)/shard_map/all_to_all | solution.py:48
  78.5 6.0 %all-to-all-done.1 = bf16[128,4,512]{2,0,1:T(8,128)(2,1)} async-done(((bf16[128,4,512]{2,0,1:T(8,128)(2,1)}), bf16[128,4,512]{2,0,1:T(8,128)(2,1)}, u32[]{:S(2)}, u32[]{:S(2)}) %all-to-all-start.1) | async-done | bytes 524320 | tf_op jit(solution)/shard_map/all_to_all | solution.py:48
  86.3 14.7 %conditional.9 = (f32[512,2,2,128]{3,0,2,1:T(8,128)S(1)}, f32[2,512,2,128]{3,1,2,0:T(8,128)}) conditional(s32[]{:T(128)} %convert_element_type.82, () %tuple.56, (s32[]{:T(128)}, bf16[2,512,2,128]{3,2,1,0:T(2,128)(2,1)}, bf16[512,2,2,128]{3,2,1,0:T(2,128)(2,1)S(1)}, f32[4,512]{1,0:T(4,128)S(1)}, bf16[512,2,2,128]{3,2,1,0:T(2,128)(2,1)}, ...), branch_computations={%region_14.15_spmd, %region_15.16_spmd} | conditional | flops 1355546624 | bytes 47784068 | solution.py:91
  89.7 2.7 %fusion.113 = f32[2,512,512,2]{2,1,3,0:T(8,128)} fusion(bf16[512,2,2,128]{3,2,1,0:T(2,128)(2,1)S(1)} %get-tuple-element.210, bf16[2,512,2,128]{3,1,2,0:T(8,128)(2,1)S(1)} %copy.124), kind=kOutput, calls=%fused_computation.139 | convolution fusion | flops 268435456 | bytes 4980736 | tf_op jit(solution)/shard_map/cond/branch_1_fun/qkgd,skd->kgqs/dot_general | solution.py:22
  92.5 3.9 %fusion.97 = bf16[2,2,512,512]{2,3,1,0:T(8,128)(2,1)S(1)} fusion(f32[2,512,512,2]{2,1,3,0:T(8,128)} %fusion.113, f32[2,2,512]{2,1,0:T(2,128)S(1)} %sub.105, f32[2,2,512]{2,1,0:T(2,128)S(1)} %sub.102, pred[512,512]{0,1:T(8,128)(4,1)S(1)} %fusion.109, bf16[512,2,2,128]{3,2,1,0:T(2,128)(2,1)S(1)} %copy-done.15, bf16[2,512,2,128]{3,1,2,0:T(8,128)(2,1)S(1)} %copy.124), kind=kOutput, calls=%fused_computation.120 | convolution fusion | flops 275775488 | bytes 7356416 | tf_op jit(solution)/shard_map/cond/branch_1_fun/qkgd,skd->kgqs/dot_general | solution.py:35
  97.2 1.9 fusion.104
  101.1 4.8 %collective-permute-start.4 = (f32[2,512,2,128]{3,1,2,0:T(8,128)}, f32[2,512,2,128]{3,1,2,0:T(8,128)}, u32[]{:S(2)}, u32[]{:S(2)}) collective-permute-start(f32[2,512,2,128]{3,1,2,0:T(8,128)} %get-tuple-element.113), channel_id=1, source_target_pairs={{4,0},{8,4},{12,8},{16,12},{20,16},{24,20},{28,24},{5,1},{9,5},{13... | collective-permute-start | bytes 3145736 | tf_op jit(solution)/shard_map/ppermute | solution.py:15
  106.6 14.8 %conditional.8 = (f32[512,2,2,128]{3,0,2,1:T(8,128)}, f32[2,512,2,128]{3,1,2,0:T(8,128)S(1)}) conditional(s32[]{:T(128)} %convert_element_type.81, () %tuple.54, (s32[]{:T(128)}, bf16[2,512,2,128]{3,2,1,0:T(2,128)(2,1)}, bf16[512,2,2,128]{3,2,1,0:T(2,128)(2,1)S(1)}, f32[4,512]{1,0:T(4,128)S(1)}, bf16[512,2,2,128]{3,2,1,0:T(2,128)(2,1)}, ...), branch_computations={%region_11.12_spmd, %region_12.13_spmd} | conditional | flops 1355546624 | bytes 51978428 | solution.py:91
  110.8 2.7 %fusion.90 = f32[2,512,512,2]{2,1,3,0:T(8,128)} fusion(bf16[512,2,2,128]{3,2,1,0:T(2,128)(2,1)S(1)} %get-tuple-element.204, bf16[2,512,2,128]{3,1,2,0:T(8,128)(2,1)S(1)} %copy.120), kind=kOutput, calls=%fused_computation.110 | convolution fusion | flops 268435456 | bytes 4980736 | tf_op jit(solution)/shard_map/cond/branch_1_fun/qkgd,skd->kgqs/dot_general | solution.py:22
  113.7 3.9 %fusion.74 = bf16[2,2,512,512]{2,3,1,0:T(8,128)(2,1)S(1)} fusion(f32[2,512,512,2]{2,1,3,0:T(8,128)} %fusion.90, f32[2,2,512]{2,1,0:T(2,128)S(1)} %sub.99, f32[2,2,512]{2,1,0:T(2,128)S(1)} %sub.96, pred[512,512]{0,1:T(8,128)(4,1)} %fusion.86, bf16[512,2,2,128]{3,2,1,0:T(2,128)(2,1)S(1)} %copy-done.16, bf16[2,512,2,128]{3,1,2,0:T(8,128)(2,1)S(1)} %copy.120), kind=kOutput, calls=%fused_computation.91 | convolution fusion | flops 275775488 | bytes 7356416 | tf_op jit(solution)/shard_map/cond/branch_1_fun/qkgd,skd->kgqs/dot_general | solution.py:35
  119.5 1.9 convolution_bitcast_fusion.6
  121.4 6.9 %collective-permute-done.4 = f32[2,512,2,128]{3,1,2,0:T(8,128)} collective-permute-done((f32[2,512,2,128]{3,1,2,0:T(8,128)}, f32[2,512,2,128]{3,1,2,0:T(8,128)}, u32[]{:S(2)}, u32[]{:S(2)}) %collective-permute-start.4) | collective-permute-done | bytes 1048608 | tf_op jit(solution)/shard_map/ppermute | solution.py:15
  128.3 2.3 add.41
  130.6 5.3 %collective-permute-start.5 = (f32[2,512,2,128]{3,1,2,0:T(8,128)}, f32[2,512,2,128]{3,1,2,0:T(8,128)}, u32[]{:S(2)}, u32[]{:S(2)}) collective-permute-start(f32[2,512,2,128]{3,1,2,0:T(8,128)} %add.41), channel_id=1, source_target_pairs={{4,0},{8,4},{12,8},{16,12},{20,16},{24,20},{28,24},{5,1},{9,5},{13... | collective-permute-start | bytes 3145736 | tf_op jit(solution)/shard_map/ppermute | solution.py:15
  137.7 19.8 %collective-permute-done.5 = f32[2,512,2,128]{3,1,2,0:T(8,128)} collective-permute-done((f32[2,512,2,128]{3,1,2,0:T(8,128)}, f32[2,512,2,128]{3,1,2,0:T(8,128)}, u32[]{:S(2)}, u32[]{:S(2)}) %collective-permute-start.5) | collective-permute-done | bytes 1048608 | tf_op jit(solution)/shard_map/ppermute | solution.py:15
  157.5 2.3 add.42
  159.8 5.3 %collective-permute-start.6 = (f32[2,512,2,128]{3,1,2,0:T(8,128)}, f32[2,512,2,128]{3,1,2,0:T(8,128)}, u32[]{:S(2)}, u32[]{:S(2)}) collective-permute-start(f32[2,512,2,128]{3,1,2,0:T(8,128)} %add.42), channel_id=1, source_target_pairs={{4,0},{8,4},{12,8},{16,12},{20,16},{24,20},{28,24},{5,1},{9,5},{13... | collective-permute-start | bytes 3145736 | tf_op jit(solution)/shard_map/ppermute | solution.py:15
  165.7 14.8 %conditional.6 = (f32[512,2,2,128]{3,0,2,1:T(8,128)}, f32[2,512,2,128]{3,1,2,0:T(8,128)S(1)}) conditional(s32[]{:T(128)} %convert_element_type.79, () %tuple.50, (s32[]{:T(128)}, bf16[2,512,2,128]{3,2,1,0:T(2,128)(2,1)}, bf16[512,2,2,128]{3,2,1,0:T(2,128)(2,1)S(1)}, f32[4,512]{1,0:T(4,128)S(1)}, bf16[512,2,2,128]{3,2,1,0:T(2,128)(2,1)}, ...), branch_computations={%region_5.6_spmd, %region_6.7_spmd} | conditional | flops 1355546624 | bytes 51978428 | solution.py:91
  169.9 2.8 %fusion.44 = f32[2,512,512,2]{2,1,3,0:T(8,128)} fusion(bf16[512,2,2,128]{3,2,1,0:T(2,128)(2,1)S(1)} %get-tuple-element.192, bf16[2,512,2,128]{3,1,2,0:T(8,128)(2,1)S(1)} %copy.112), kind=kOutput, calls=%fused_computation.52 | convolution fusion | flops 268435456 | bytes 4980736 | tf_op jit(solution)/shard_map/cond/branch_1_fun/qkgd,skd->kgqs/dot_general | solution.py:22
  172.9 3.9 %fusion.28 = bf16[2,2,512,512]{2,3,1,0:T(8,128)(2,1)S(1)} fusion(f32[2,512,512,2]{2,1,3,0:T(8,128)} %fusion.44, f32[2,2,512]{2,1,0:T(2,128)S(1)} %sub.75, f32[2,2,512]{2,1,0:T(2,128)S(1)} %sub.72, pred[512,512]{0,1:T(8,128)(4,1)} %fusion.40, bf16[512,2,2,128]{3,2,1,0:T(2,128)(2,1)S(1)} %copy-done.18, bf16[2,512,2,128]{3,1,2,0:T(8,128)(2,1)S(1)} %copy.112), kind=kOutput, calls=%fused_computation.33 | convolution fusion | flops 275775488 | bytes 7356416 | tf_op jit(solution)/shard_map/cond/branch_1_fun/qkgd,skd->kgqs/dot_general | solution.py:35
  178.6 1.9 convolution_bitcast_fusion.2
  180.6 5.2 %collective-permute-done.6 = f32[2,512,2,128]{3,1,2,0:T(8,128)} collective-permute-done((f32[2,512,2,128]{3,1,2,0:T(8,128)}, f32[2,512,2,128]{3,1,2,0:T(8,128)}, u32[]{:S(2)}, u32[]{:S(2)}) %collective-permute-start.6) | collective-permute-done | bytes 1048608 | tf_op jit(solution)/shard_map/ppermute | solution.py:15
  185.8 2.3 add.43
  188.1 5.3 %collective-permute-start.7 = (f32[2,512,2,128]{3,1,2,0:T(8,128)}, f32[2,512,2,128]{3,1,2,0:T(8,128)}, u32[]{:S(2)}, u32[]{:S(2)}) collective-permute-start(f32[2,512,2,128]{3,1,2,0:T(8,128)} %add.43), channel_id=1, source_target_pairs={{4,0},{8,4},{12,8},{16,12},{20,16},{24,20},{28,24},{5,1},{9,5},{13... | collective-permute-start | bytes 3145736 | tf_op jit(solution)/shard_map/ppermute | solution.py:15
  194.0 13.2 %conditional.5 = (f32[512,2,2,128]{3,0,2,1:T(8,128)}, f32[2,512,2,128]{3,1,2,0:T(8,128)S(1)}) conditional(s32[]{:T(128)} %convert_element_type.75, () %tuple.48, (s32[]{:T(128)}, bf16[4,128,256]{1,2,0:T(8,128)(2,1)S(1)}, bf16[512,2,2,128]{3,2,1,0:T(2,128)(2,1)S(1)}, f32[4,512]{1,0:T(4,128)S(1)}, bf16[4,128,256]{1,2,0:T(8,128)(2,1)S(1)}, ...), branch_computations={%region_2.3_spmd, %region_3.4_spmd} | conditional | flops 1355546624 | bytes 47784040 | solution.py:91
  196.3 2.8 %fusion.18 = f32[2,512,512,2]{2,1,3,0:T(8,128)} fusion(bf16[512,2,2,128]{3,2,1,0:T(2,128)(2,1)S(1)} %get-tuple-element.185, bf16[512,2,128,1]{2,1,0,3:T(2,128)(2,1)S(1)} %bitcast.288), kind=kOutput, calls=%fused_computation.22 | convolution fusion | flops 268435456 | bytes 4980736 | tf_op jit(solution)/shard_map/cond/branch_1_fun/qkgd,skd->kgqs/dot_general | solution.py:22
  199.5 3.9 %fusion.2 = bf16[2,2,512,512]{2,3,1,0:T(8,128)(2,1)S(1)} fusion(f32[2,512,512,2]{2,1,3,0:T(8,128)} %fusion.18, f32[2,2,512]{2,1,0:T(2,128)S(1)} %sub.69, f32[2,2,512]{2,1,0:T(2,128)S(1)} %sub.56, pred[512,512]{0,1:T(8,128)(4,1)S(1)} %fusion.14, bf16[512,2,2,128]{3,2,1,0:T(2,128)(2,1)S(1)} %copy-done.19, bf16[512,2,128,1]{2,1,0,3:T(2,128)(2,1)S(1)} %bitcast.299), kind=kOutput, calls=%fused_computation.3 | convolution fusion | flops 275775488 | bytes 7356416 | tf_op jit(solution)/shard_map/cond/branch_1_fun/qkgd,skd->kgqs/dot_general | solution.py:35
  205.2 2.0 convolution_bitcast_fusion
  207.2 2.4 add_convert_fusion.1
  211.1 3.5 %all-to-all-start.5 = ((bf16[4,128,512]{2,1,0:T(8,128)(2,1)}), bf16[4,128,512]{2,1,0:T(8,128)(2,1)S(1)}, u32[]{:S(2)}, u32[]{:S(2)}) async-start(bf16[4,128,512]{2,1,0:T(8,128)(2,1)} %convert_element_type.84), calls=%async_computation.5 | async-start | bytes 1048576 | tf_op jit(solution)/shard_map/all_to_all | solution.py:101
  217.2 6.2 %all-to-all-done.5 = bf16[4,128,512]{2,1,0:T(8,128)(2,1)S(1)} async-done(((bf16[4,128,512]{2,1,0:T(8,128)(2,1)}), bf16[4,128,512]{2,1,0:T(8,128)(2,1)S(1)}, u32[]{:S(2)}, u32[]{:S(2)}) %all-to-all-start.5) | async-done | bytes 524320 | tf_op jit(solution)/shard_map/all_to_all | solution.py:101
  223.4 3.4 %all-to-all-start.6 = ((bf16[4,128,256]{2,1,0:T(8,128)(2,1)}), bf16[4,128,256]{2,1,0:T(8,128)(2,1)S(1)}, u32[]{:S(2)}, u32[]{:S(2)}) async-start(bf16[4,128,256]{2,1,0:T(8,128)(2,1)} %convert_element_type.85), calls=%async_computation.6 | async-start | bytes 524288 | tf_op jit(solution)/shard_map/all_to_all | solution.py:102
  227.9 4.8 %all-to-all-done.6 = bf16[4,128,256]{2,1,0:T(8,128)(2,1)S(1)} async-done(((bf16[4,128,256]{2,1,0:T(8,128)(2,1)}), bf16[4,128,256]{2,1,0:T(8,128)(2,1)S(1)}, u32[]{:S(2)}, u32[]{:S(2)}) %all-to-all-start.6) | async-done | bytes 262176 | tf_op jit(solution)/shard_map/all_to_all | solution.py:102
  232.8 3.4 %all-to-all-start.7 = ((bf16[4,128,256]{2,1,0:T(8,128)(2,1)}), bf16[4,128,256]{2,1,0:T(8,128)(2,1)S(1)}, u32[]{:S(2)}, u32[]{:S(2)}) async-start(bf16[4,128,256]{2,1,0:T(8,128)(2,1)} %convert_element_type.86), calls=%async_computation.7 | async-start | bytes 524288 | tf_op jit(solution)/shard_map/all_to_all | solution.py:103
  238.5 3.7 %all-to-all-done.7 = bf16[4,128,256]{2,1,0:T(8,128)(2,1)S(1)} async-done(((bf16[4,128,256]{2,1,0:T(8,128)(2,1)}), bf16[4,128,256]{2,1,0:T(8,128)(2,1)S(1)}, u32[]{:S(2)}, u32[]{:S(2)}) %all-to-all-start.7) | async-done | bytes 262176 | tf_op jit(solution)/shard_map/all_to_all | solution.py:103
  (114 shorter events, 36.5 us)
Async XLA Ops:
  0.6 40.3 %copy-start.11 = (bf16[128,2048]{1,0:T(8,128)(2,1)S(1)}, bf16[128,2048]{1,0:T(8,128)(2,1)}, u32[]{:S(2)}) copy-start(bf16[128,2048]{1,0:T(8,128)(2,1)} %param.18) | copy-start | bytes 1572868
  0.6 55.1 %copy-start.12 = (bf16[128,2048]{1,0:T(8,128)(2,1)S(1)}, bf16[128,2048]{1,0:T(8,128)(2,1)}, u32[]{:S(2)}) copy-start(bf16[128,2048]{1,0:T(8,128)(2,1)} %param.19) | copy-start | bytes 1572868
  2.5 9.4 %all-to-all-start = ((bf16[128,4,256]{0,2,1:T(8,128)(2,1)}), bf16[128,4,256]{0,2,1:T(8,128)(2,1)S(1)}, u32[]{:S(2)}, u32[]{:S(2)}) async-start(bf16[128,4,256]{0,2,1:T(8,128)(2,1)} %bitcast.82), calls=%async_computation | async-start | bytes 524288 | tf_op jit(solution)/shard_map/all_to_all | solution.py:51
  5.9 64.6 %copy-start.13 = (bf16[128,2048]{1,0:T(8,128)(2,1)S(1)}, bf16[128,2048]{1,0:T(8,128)(2,1)}, u32[]{:S(2)}) copy-start(bf16[128,2048]{1,0:T(8,128)(2,1)} %param.17) | copy-start | bytes 1572868
  11.9 9.4 %all-to-all-start.2 = ((bf16[128,4,256]{0,2,1:T(8,128)(2,1)}), bf16[128,4,256]{0,2,1:T(8,128)(2,1)S(1)}, u32[]{:S(2)}, u32[]{:S(2)}) async-start(bf16[128,4,256]{0,2,1:T(8,128)(2,1)} %bitcast.85), calls=%async_computation.2 | async-start | bytes 524288 | tf_op jit(solution)/shard_map/all_to_all | solution.py:52
  21.3 54.3 %copy-start.25 = (s32[20,3]{0,1:T(4,128)S(1)}, s32[20,3]{0,1:T(4,128)}, u32[]{:S(2)}) copy-start(s32[20,3]{0,1:T(4,128)} %param.23) | copy-start | bytes 724
  22.3 16.2 %collective-permute-start = (bf16[2,512,2,128]{3,2,1,0:T(2,128)(2,1)S(1)}, bf16[2,512,2,128]{3,2,1,0:T(2,128)(2,1)S(1)}, u32[]{:S(2)}, u32[]{:S(2)}) collective-permute-start(bf16[2,512,2,128]{3,2,1,0:T(2,128)(2,1)S(1)} %pad_maximum_fusion.5), channel_id=1, source_target_pairs={{0,4},{4,8},{8,12},{12,16},{16,20},{20,24},{24,28},{1,5},{5,9},{9,... | collective-permute-start | bytes 1572872 | tf_op jit(solution)/shard_map/ppermute | solution.py:15
  38.4 38.6 %copy-start.14 = (bf16[2,512,2,128]{3,2,1,0:T(2,128)(2,1)}, bf16[2,512,2,128]{3,2,1,0:T(2,128)(2,1)S(1)}, u32[]{:S(2)}) copy-start(bf16[2,512,2,128]{3,2,1,0:T(2,128)(2,1)S(1)} %collective-permute-done) | copy-start | bytes 1572868
  38.4 15.4 %collective-permute-start.1 = (bf16[2,512,2,128]{3,2,1,0:T(2,128)(2,1)S(1)}, bf16[2,512,2,128]{3,2,1,0:T(2,128)(2,1)}, u32[]{:S(2)}, u32[]{:S(2)}) collective-permute-start(bf16[2,512,2,128]{3,2,1,0:T(2,128)(2,1)S(1)} %collective-permute-done), channel_id=1, source_target_pairs={{0,4},{4,8},{8,12},{12,16},{16,20},{20,24},{24,28},{1,5},{5,9},{9,... | collective-permute-start | bytes 1572872 | tf_op jit(solution)/shard_map/ppermute | solution.py:15
  41.8 14.8 %all-to-all-start.3 = ((bf16[128,4,512]{2,0,1:T(8,128)(2,1)}), bf16[128,4,512]{2,0,1:T(8,128)(2,1)S(1)}, u32[]{:S(2)}, u32[]{:S(2)}) async-start(bf16[128,4,512]{2,0,1:T(8,128)(2,1)} %bitcast.276), calls=%async_computation.3 | async-start | bytes 1048576 | tf_op jit(solution)/shard_map/all_to_all | solution.py:49
  53.8 14.8 %collective-permute-start.2 = (bf16[2,512,2,128]{3,2,1,0:T(2,128)(2,1)}, bf16[2,512,2,128]{3,2,1,0:T(2,128)(2,1)}, u32[]{:S(2)}, u32[]{:S(2)}) collective-permute-start(bf16[2,512,2,128]{3,2,1,0:T(2,128)(2,1)} %collective-permute-done.1), channel_id=1, source_target_pairs={{0,4},{4,8},{8,12},{12,16},{16,20},{20,24},{24,28},{1,5},{5,9},{9,... | collective-permute-start | bytes 1572872 | tf_op jit(solution)/shard_map/ppermute | solution.py:15
  56.6 14.7 %all-to-all-start.4 = ((bf16[128,4,512]{2,0,1:T(8,128)(2,1)}), bf16[128,4,512]{2,0,1:T(8,128)(2,1)S(1)}, u32[]{:S(2)}, u32[]{:S(2)}) async-start(bf16[128,4,512]{2,0,1:T(8,128)(2,1)} %bitcast.275), calls=%async_computation.4 | async-start | bytes 1048576 | tf_op jit(solution)/shard_map/all_to_all | solution.py:50
  68.6 17.7 %collective-permute-start.3 = (bf16[2,512,2,128]{3,2,1,0:T(2,128)(2,1)}, bf16[2,512,2,128]{3,2,1,0:T(2,128)(2,1)}, u32[]{:S(2)}, u32[]{:S(2)}) collective-permute-start(bf16[2,512,2,128]{3,2,1,0:T(2,128)(2,1)} %collective-permute-done.2), channel_id=1, source_target_pairs={{0,4},{4,8},{8,12},{12,16},{16,20},{20,24},{24,28},{1,5},{5,9},{9,... | collective-permute-start | bytes 1572872 | tf_op jit(solution)/shard_map/ppermute | solution.py:15
  71.4 14.9 %copy-start.24 = (f32[4,512]{1,0:T(4,128)S(1)}, f32[4,512]{1,0:T(4,128)}, u32[]{:S(2)}) copy-start(f32[4,512]{1,0:T(4,128)} %param.22) | copy-start | bytes 24580
  71.4 13.1 %all-to-all-start.1 = ((bf16[128,4,512]{2,0,1:T(8,128)(2,1)}), bf16[128,4,512]{2,0,1:T(8,128)(2,1)}, u32[]{:S(2)}, u32[]{:S(2)}) async-start(bf16[128,4,512]{2,0,1:T(8,128)(2,1)} %bitcast.277), calls=%async_computation.1 | async-start | bytes 1048576 | tf_op jit(solution)/shard_map/all_to_all | solution.py:48
  86.3 6.2 %copy-start.15 = (bf16[512,2,2,128]{3,2,1,0:T(2,128)(2,1)S(1)}, bf16[512,2,2,128]{3,2,1,0:T(2,128)(2,1)}, u32[]{:S(2)}) copy-start(bf16[512,2,2,128]{3,2,1,0:T(2,128)(2,1)} %get-tuple-element.212) | copy-start | bytes 1572868 | tf_op jit(solution)/shard_map/cond
  88.5 4.0 %copy-start.20 = (pred[512,512]{0,1:T(8,128)(4,1)}, pred[512,512]{0,1:T(8,128)(4,1)S(1)}, u32[]{:S(2)}) copy-start(pred[512,512]{0,1:T(8,128)(4,1)S(1)} %fusion.109) | copy-start | bytes 786436 | tf_op jit(solution)/shard_map/cond
  92.5 4.7 %copy-start.1 = (f32[2,512,512,2]{2,1,3,0:T(8,128)S(1)}, f32[2,512,512,2]{2,1,3,0:T(8,128)}, u32[]{:S(2)}) copy-start(f32[2,512,512,2]{2,1,3,0:T(8,128)} %fusion.113) | copy-start | bytes 12582916 | tf_op jit(solution)/shard_map/cond
  101.1 27.2 %collective-permute-start.4 = (f32[2,512,2,128]{3,1,2,0:T(8,128)}, f32[2,512,2,128]{3,1,2,0:T(8,128)}, u32[]{:S(2)}, u32[]{:S(2)}) collective-permute-start(f32[2,512,2,128]{3,1,2,0:T(8,128)} %get-tuple-element.113), channel_id=1, source_target_pairs={{4,0},{8,4},{12,8},{16,12},{20,16},{24,20},{28,24},{5,1},{9,5},{13... | collective-permute-start | bytes 3145736 | tf_op jit(solution)/shard_map/ppermute | solution.py:15
  106.8 6.9 %copy-start.16 = (bf16[512,2,2,128]{3,2,1,0:T(2,128)(2,1)S(1)}, bf16[512,2,2,128]{3,2,1,0:T(2,128)(2,1)}, u32[]{:S(2)}) copy-start(bf16[512,2,2,128]{3,2,1,0:T(2,128)(2,1)} %get-tuple-element.206) | copy-start | bytes 1572868 | tf_op jit(solution)/shard_map/cond
  110.8 6.9 %copy-start.5 = (bf16[2,512,2,128]{3,1,2,0:T(8,128)(2,1)}, bf16[2,512,2,128]{3,1,2,0:T(8,128)(2,1)S(1)}, u32[]{:S(2)}) copy-start(bf16[2,512,2,128]{3,1,2,0:T(8,128)(2,1)S(1)} %copy.120) | copy-start | bytes 1572868 | tf_op jit(solution)/shard_map/cond
  113.7 4.7 %copy-start.2 = (f32[2,512,512,2]{2,1,3,0:T(8,128)S(1)}, f32[2,512,512,2]{2,1,3,0:T(8,128)}, u32[]{:S(2)}) copy-start(f32[2,512,512,2]{2,1,3,0:T(8,128)} %fusion.90) | copy-start | bytes 12582916 | tf_op jit(solution)/shard_map/cond
  113.7 4.7 %copy-start.21 = (pred[512,512]{0,1:T(8,128)(4,1)S(1)}, pred[512,512]{0,1:T(8,128)(4,1)}, u32[]{:S(2)}) copy-start(pred[512,512]{0,1:T(8,128)(4,1)} %fusion.86) | copy-start | bytes 786436 | tf_op jit(solution)/shard_map/cond
  118.4 1.0 copy-start.6
  130.6 26.8 %collective-permute-start.5 = (f32[2,512,2,128]{3,1,2,0:T(8,128)}, f32[2,512,2,128]{3,1,2,0:T(8,128)}, u32[]{:S(2)}, u32[]{:S(2)}) collective-permute-start(f32[2,512,2,128]{3,1,2,0:T(8,128)} %add.41), channel_id=1, source_target_pairs={{4,0},{8,4},{12,8},{16,12},{20,16},{24,20},{28,24},{5,1},{9,5},{13... | collective-permute-start | bytes 3145736 | tf_op jit(solution)/shard_map/ppermute | solution.py:15
  159.8 26.0 %collective-permute-start.6 = (f32[2,512,2,128]{3,1,2,0:T(8,128)}, f32[2,512,2,128]{3,1,2,0:T(8,128)}, u32[]{:S(2)}, u32[]{:S(2)}) collective-permute-start(f32[2,512,2,128]{3,1,2,0:T(8,128)} %add.42), channel_id=1, source_target_pairs={{4,0},{8,4},{12,8},{16,12},{20,16},{24,20},{28,24},{5,1},{9,5},{13... | collective-permute-start | bytes 3145736 | tf_op jit(solution)/shard_map/ppermute | solution.py:15
  166.0 6.9 %copy-start.18 = (bf16[512,2,2,128]{3,2,1,0:T(2,128)(2,1)S(1)}, bf16[512,2,2,128]{3,2,1,0:T(2,128)(2,1)}, u32[]{:S(2)}) copy-start(bf16[512,2,2,128]{3,2,1,0:T(2,128)(2,1)} %get-tuple-element.194) | copy-start | bytes 1572868 | tf_op jit(solution)/shard_map/cond
  169.9 6.9 %copy-start.9 = (bf16[2,512,2,128]{3,1,2,0:T(8,128)(2,1)}, bf16[2,512,2,128]{3,1,2,0:T(8,128)(2,1)S(1)}, u32[]{:S(2)}) copy-start(bf16[2,512,2,128]{3,1,2,0:T(8,128)(2,1)S(1)} %copy.112) | copy-start | bytes 1572868 | tf_op jit(solution)/shard_map/cond
  172.9 4.7 %copy-start.4 = (f32[2,512,512,2]{2,1,3,0:T(8,128)S(1)}, f32[2,512,512,2]{2,1,3,0:T(8,128)}, u32[]{:S(2)}) copy-start(f32[2,512,512,2]{2,1,3,0:T(8,128)} %fusion.44) | copy-start | bytes 12582916 | tf_op jit(solution)/shard_map/cond
  172.9 4.7 %copy-start.23 = (pred[512,512]{0,1:T(8,128)(4,1)S(1)}, pred[512,512]{0,1:T(8,128)(4,1)}, u32[]{:S(2)}) copy-start(pred[512,512]{0,1:T(8,128)(4,1)} %fusion.40) | copy-start | bytes 786436 | tf_op jit(solution)/shard_map/cond
  177.6 1.0 copy-start.10
  188.1 26.5 %collective-permute-start.7 = (f32[2,512,2,128]{3,1,2,0:T(8,128)}, f32[2,512,2,128]{3,1,2,0:T(8,128)}, u32[]{:S(2)}, u32[]{:S(2)}) collective-permute-start(f32[2,512,2,128]{3,1,2,0:T(8,128)} %add.43), channel_id=1, source_target_pairs={{4,0},{8,4},{12,8},{16,12},{20,16},{24,20},{28,24},{5,1},{9,5},{13... | collective-permute-start | bytes 3145736 | tf_op jit(solution)/shard_map/ppermute | solution.py:15
  194.0 5.4 %copy-start.19 = (bf16[512,2,2,128]{3,2,1,0:T(2,128)(2,1)S(1)}, bf16[512,2,2,128]{3,2,1,0:T(2,128)(2,1)}, u32[]{:S(2)}) copy-start(bf16[512,2,2,128]{3,2,1,0:T(2,128)(2,1)} %get-tuple-element.188) | copy-start | bytes 1572868 | tf_op jit(solution)/shard_map/cond
  199.5 4.7 %copy-start = (f32[2,512,512,2]{2,1,3,0:T(8,128)S(1)}, f32[2,512,512,2]{2,1,3,0:T(8,128)}, u32[]{:S(2)}) copy-start(f32[2,512,512,2]{2,1,3,0:T(8,128)} %fusion.18) | copy-start | bytes 12582916 | tf_op jit(solution)/shard_map/cond
  211.1 12.3 %all-to-all-start.5 = ((bf16[4,128,512]{2,1,0:T(8,128)(2,1)}), bf16[4,128,512]{2,1,0:T(8,128)(2,1)S(1)}, u32[]{:S(2)}, u32[]{:S(2)}) async-start(bf16[4,128,512]{2,1,0:T(8,128)(2,1)} %convert_element_type.84), calls=%async_computation.5 | async-start | bytes 1048576 | tf_op jit(solution)/shard_map/all_to_all | solution.py:101
  223.4 9.4 %all-to-all-start.6 = ((bf16[4,128,256]{2,1,0:T(8,128)(2,1)}), bf16[4,128,256]{2,1,0:T(8,128)(2,1)S(1)}, u32[]{:S(2)}, u32[]{:S(2)}) async-start(bf16[4,128,256]{2,1,0:T(8,128)(2,1)} %convert_element_type.85), calls=%async_computation.6 | async-start | bytes 524288 | tf_op jit(solution)/shard_map/all_to_all | solution.py:102
  232.8 9.4 %all-to-all-start.7 = ((bf16[4,128,256]{2,1,0:T(8,128)(2,1)}), bf16[4,128,256]{2,1,0:T(8,128)(2,1)S(1)}, u32[]{:S(2)}, u32[]{:S(2)}) async-start(bf16[4,128,256]{2,1,0:T(8,128)(2,1)} %convert_element_type.86), calls=%async_computation.7 | async-start | bytes 524288 | tf_op jit(solution)/shard_map/all_to_all | solution.py:103
where the time goes:
time: 244 us; the launch traced here: 243 us
  waiting for transfers between devices  92.3 us (38%)
  starting transfers between devices  58.7 us (24%)
  matrix products  41 us (17%)
  local copies, waits for them, and re-layouts  21.9 us (9%)
  other arithmetic  16.2 us (7%)
  loops' own time  8.84 us (4%)
  between operations  4.2 us (2%)
    ppermute x8, waiting for transfers between devices, from_behind(): lax.ppermute(value, axis, [(source, source + steps) for source in range(f...  61.7 us
    ppermute x8, starting transfers between devices, from_behind(): lax.ppermute(value, axis, [(source, source + steps) for source in range(f...  30.4 us
    dot_general x4, matrix products, pair_grads(): jnp.einsum('qkgd,skd->kgqs', do_heads, v_block, preferred_element_type=jn...  15.8 us
    dot_general x4, matrix products, pair_grads(): jnp.einsum('qkgd,skd->kgqs', q_heads, k_block, preferred_element_type=jnp...  10.9 us
    another operation x5, loops' own time, shards(): part_q, part_kv = lax.cond(pair_code > 0, compute_pair, skip_pair, travel)  8.84 us
    add x3, other arithmetic, shards(): acc_kv = from_behind(acc_kv, 'seq', -1) + kv_parts[offset]  6.98 us
    dot_general x4, matrix products, pair_grads(): jnp.einsum('kgqs,skd->qkgd', dscores, k_block, preferred_element_type=jnp...  6.77 us
    unnamed x17, local copies, waits for them, and re-layouts  6.47 us
  transfers between devices with their start and end apart: 16, of which 12 were waited for; matrix products, arithmetic and copies ran while one was open for 23% of the time, Pallas kernels for 0%

commit v1 on v0

v1 whole, which is shorter than its diff:
```python
import functools
import math

import jax
import jax.numpy as jnp
from jax import lax
from jax.experimental import pallas as pl
from jax.experimental.pallas import tpu as pltpu
from jax.sharding import Mesh, PartitionSpec as P

HEAD_SIZE = 128
KEY_VALUE_HEADS = 8
QUERY_HEADS = 16
WIN = 5
GROUP = QUERY_HEADS // KEY_VALUE_HEADS
TILE = 256
AUX = 16
LANES = 128
LOG2E = math.log2(math.e)
SCALE = 1.0 / math.sqrt(HEAD_SIZE)
BF16 = jnp.bfloat16
F32 = jnp.float32
CROSS = ("y", "head")
WHOLE = pl.BlockSpec(memory_space=pltpu.VMEM)
SCALARS = pl.BlockSpec(memory_space=pltpu.SMEM)
VMEM_BYTES = 48 * 1024 * 1024


def call(kernel, out_shape, in_specs, name, flops=0, moved=4 << 20, scratch=()):
    return pl.pallas_call(
        kernel,
        out_shape=out_shape,
        in_specs=in_specs,
        out_specs=jax.tree.map(lambda _: WHOLE, out_shape),
        scratch_shapes=scratch,
        name=name,
        cost_estimate=pl.CostEstimate(flops=flops, bytes_accessed=moved, transcendentals=0),
        compiler_params=pltpu.CompilerParams(vmem_limit_bytes=VMEM_BYTES),
    )


def split3(x):
    hi = x.astype(BF16)
    rest = x - hi.astype(F32)
    mid = rest.astype(BF16)
    low = (rest - mid.astype(F32)).astype(BF16)
    return hi, mid, low


def padded_lanes(x):
    rows, width = x.shape
    if width == LANES:
        return x
    return jnp.concatenate([x, jnp.zeros((rows, LANES - width), x.dtype)], axis=1)


def head_of(member, fold, n_head):
    return (member % n_head) * fold + member // n_head


def pack_q_kernel(fold, n_head, me_ref, q_ref, do_ref, o_ref, *refs):
    members = fold * n_head
    pieces, (delta_ref,) = refs[:members], refs[members:]
    tokens = q_ref.shape[0]
    sums = []
    for head in range(QUERY_HEADS):
        cols = slice(head * HEAD_SIZE, (head + 1) * HEAD_SIZE)
        product = do_ref[:, cols].astype(F32) * o_ref[:, cols].astype(F32)
        sums.append(jnp.sum(product, axis=1, keepdims=True))
    sums.append(jnp.zeros((tokens, LANES - QUERY_HEADS), F32))
    delta_ref[...] = padded_lanes(jnp.concatenate(sums, axis=1).T)
    for mask in range(members):
        kv_head = head_of(me_ref[0] ^ mask, fold, n_head)
        out = pieces[mask]
        for g in range(GROUP):
            cols = pl.ds(pl.multiple_of((kv_head * GROUP + g) * HEAD_SIZE, LANES), HEAD_SIZE)
            out[g * tokens : (g + 1) * tokens, :] = q_ref[:, cols]
            out[(GROUP + g) * tokens : (GROUP + g + 1) * tokens, :] = do_ref[:, cols]
        rows = [delta_ref[pl.ds(kv_head * GROUP + g, 1), :] for g in range(GROUP)]
        terms = [term for row in rows for term in split3(row)]
        terms.append(jnp.zeros((AUX - len(terms), LANES), BF16))
        out[2 * GROUP * tokens :, :] = jnp.concatenate(terms, axis=0)


def pack_kv_kernel(fold, n_head, me_ref, k_ref, v_ref, *pieces):
    tokens = k_ref.shape[0]
    for mask, out in enumerate(pieces):
        kv_head = head_of(me_ref[0] ^ mask, fold, n_head)
        cols = pl.ds(pl.multiple_of(kv_head * HEAD_SIZE, LANES), HEAD_SIZE)
        out[:tokens, :] = k_ref[:, cols]
        out[tokens:, :] = v_ref[:, cols]


def assemble_q_kernel(fold, n_head, me_ref, lse_ref, *refs):
    members = fold * n_head
    pieces, (q_out,) = refs[:members], refs[members:]
    tokens = (pieces[0].shape[0] - AUX) // (2 * GROUP)
    body = 2 * GROUP * tokens
    for mask in range(members):
        member = me_ref[0] ^ mask
        q_out[member, :body, :] = pieces[mask][:body, :]
    for mask in range(members):
        member = me_ref[0] ^ mask
        terms = [pieces[mask][body : body + 3 * GROUP, :]]
        for g in range(GROUP):
            terms.extend(split3(lse_ref[member, pl.ds(g, 1), :]))
        terms.append(jnp.zeros((AUX - 6 * GROUP, LANES), BF16))
        q_out[member, body:, :] = jnp.concatenate(terms, axis=0)


def assemble_kv_kernel(me_ref, *refs):
    pieces, kv_out = refs[:-1], refs[-1]
    for mask, piece in enumerate(pieces):
        kv_out[me_ref[0] ^ mask] = piece[...]


def lane_row(parts, tokens):
    if tokens == LANES:
        return jnp.concatenate(parts, axis=1)
    per = LANES // tokens
    lane = lax.broadcasted_iota(jnp.int32, (1, LANES), 1)
    out = []
    for start in range(0, len(parts), per):
        row = parts[start]
        for k in range(1, per):
            moved = pltpu.roll(parts[start + k], k * tokens, 1)
            row = jnp.where(lane >= k * tokens, moved, row)
        out.append(row)
    return jnp.concatenate(out, axis=1)


def role_kernel(fold, n_head, has_dq, has_dkv, code_ref, q_ref, kv_ref, *refs):
    refs = list(refs)
    dq_in = refs.pop(0) if has_dq else None
    dkv_in = refs.pop(0) if has_dkv else None
    dq_out, dkv_out, dq_ref, dkv_ref = refs
    tokens = kv_ref.shape[1] // 2
    block = n_head * tokens
    tiles = block // TILE
    chunks = TILE // tokens
    dq_ref[...] = dq_in[...] if has_dq else jnp.zeros_like(dq_ref)
    dkv_ref[...] = dkv_in[...] if has_dkv else jnp.zeros_like(dkv_ref)

    def one_tile(q_tile, k_tile, code, masked):
        q_chunk = q_tile * chunks
        k_chunk = k_tile * chunks

        def q_rows(which):
            return jnp.concatenate(
                [
                    q_ref[q_chunk + n, (which * GROUP + g) * tokens : (which * GROUP + g + 1) * tokens, :]
                    for g in range(GROUP)
                    for n in range(chunks)
                ],
                axis=0,
            )

        def aux(which):
            base = 2 * GROUP * tokens
            parts = []
            for g in range(GROUP):
                row = base + (which * GROUP + g) * 3
                for n in range(chunks):
                    group = q_ref[q_chunk + n, base : base + AUX, :].astype(F32)
                    at = row - base
                    parts.append(group[at : at + 1] + group[at + 1 : at + 2] + group[at + 2 : at + 3])
            return lane_row(parts, tokens)

        q2, do2 = q_rows(0), q_rows(1)
        delta, lse = aux(0), aux(1)
        k = jnp.concatenate([kv_ref[k_chunk + n, :tokens, :] for n in range(chunks)], axis=0)
        v = jnp.concatenate([kv_ref[k_chunk + n, tokens:, :] for n in range(chunks)], axis=0)
        last = (((1,), (1,)), ((), ()))
        scores = lax.dot_general(k, q2, last, preferred_element_type=F32)
        dprobs = lax.dot_general(v, do2, last, preferred_element_type=F32)
        probs = jnp.exp2(scores * (SCALE * LOG2E) - lse * LOG2E)
        if masked:
            key_id = lax.broadcasted_iota(jnp.int32, probs.shape, 0)
            query_id = lax.broadcasted_iota(jnp.int32, probs.shape, 1) % TILE
            ahead = key_id - query_id
            allowed = jnp.where(code == 2, ahead, 1 - ahead) <= 0
            probs = jnp.where(allowed, probs, 0.0)
        dscores = (probs * (dprobs - delta) * SCALE).astype(BF16)
        low = probs.astype(BF16)
        dv = jnp.dot(low, do2, preferred_element_type=F32)
        dk = jnp.dot(dscores, q2, preferred_element_type=F32)
        dq_ref[q_tile] += jnp.dot(k.T, dscores, preferred_element_type=F32)
        for n in range(chunks):
            rows = slice(n * tokens, (n + 1) * tokens)
            dkv_ref[k_chunk + n, :tokens, :] += dk[rows]
            dkv_ref[k_chunk + n, tokens:, :] += dv[rows]

    def step(index, carry):
        k_in = index % tiles
        q_in = (index // tiles) % tiles
        key_block = (index // (tiles * tiles)) % fold
        query_block = index // (tiles * tiles * fold)
        code = code_ref[query_block, key_block]
        plain = (code == 1) | ((code == 2) & (k_in < q_in)) | ((code == 3) & (k_in > q_in))
        cut = (code >= 2) & (k_in == q_in)
        q_tile = query_block * tiles + q_in
        k_tile = key_block * tiles + k_in

        @pl.when(plain)
        def _():
            one_tile(q_tile, k_tile, code, False)

        @pl.when(cut)
        def _():
            one_tile(q_tile, k_tile, code, True)

        return carry

    lax.fori_loop(0, fold * fold * tiles * tiles, step, 0)
    dq_out[...] = dq_ref[...].astype(dq_out.dtype)
    dkv_out[...] = dkv_ref[...].astype(dkv_out.dtype)


def finish_kernel(has_dq, has_dkv, me_ref, dq_ref, dkv_ref, *refs):
    refs = list(refs)
    dq_far = refs.pop(0) if has_dq else None
    dkv_far = refs.pop(0) if has_dkv else None
    pieces, (rows_ref,) = refs[:-1], refs[-1:]
    tokens = dkv_ref.shape[1] // 2
    chunks = TILE // tokens
    for tile in range(dq_ref.shape[0]):
        total = dq_ref[tile]
        if has_dq:
            total = total + dq_far[tile].astype(F32)
        for g in range(GROUP):
            turned = total[:, g * TILE : (g + 1) * TILE].T
            for n in range(chunks):
                rows_ref[tile * chunks + n, g * tokens : (g + 1) * tokens, :] = turned[
                    n * tokens : (n + 1) * tokens
                ].astype(BF16)
    for mask, out in enumerate(pieces):
        member = me_ref[0] ^ mask
        total = dkv_ref[member]
        if has_dkv:
            total = total + dkv_far[member].astype(F32)
        out[: GROUP * tokens, :] = rows_ref[member]
        out[GROUP * tokens :, :] = total.astype(BF16)


def unpack_kernel(fold, n_head, me_ref, *refs):
    members = fold * n_head
    pieces = refs[:members]
    dq_ref, dk_ref, dv_ref = refs[members:]
    tokens = dk_ref.shape[0]
    for mask, piece in enumerate(pieces):
        kv_head = head_of(me_ref[0] ^ mask, fold, n_head)
        for g in range(GROUP):
            cols = pl.ds(pl.multiple_of((kv_head * GROUP + g) * HEAD_SIZE, LANES), HEAD_SIZE)
            dq_ref[:, cols] = piece[g * tokens : (g + 1) * tokens, :]
        cols = pl.ds(pl.multiple_of(kv_head * HEAD_SIZE, LANES), HEAD_SIZE)
        dk_ref[:, cols] = piece[GROUP * tokens : (GROUP + 1) * tokens, :]
        dv_ref[:, cols] = piece[(GROUP + 1) * tokens :, :]


def exchange(pieces):
    members = len(pieces)
    return [pieces[0]] + [
        lax.ppermute(pieces[mask], CROSS, [(i, i ^ mask) for i in range(members)])
        for mask in range(1, members)
    ]


def along(value, planes, steps):
    pairs = [(i, i + steps) for i in range(planes) if 0 <= i + steps < planes]
    return lax.ppermute(value, "z", pairs)


def shards(queries, output_gradient, outputs, key_vectors, values, logsum, pair_list):
    planes, fold, n_head = (lax.axis_size(a) for a in ("z", "y", "head"))
    members = fold * n_head
    tokens = queries.shape[0]
    block = n_head * tokens
    q_tiles = fold * (block // TILE)
    reach = -(-(WIN - 1) // fold)
    y = lax.axis_index("y")
    z = lax.axis_index("z")
    me = (y * n_head + lax.axis_index("head")).astype(jnp.int32).reshape(1)

    q_piece = jax.ShapeDtypeStruct((2 * GROUP * tokens + AUX, LANES), BF16)
    kv_piece = jax.ShapeDtypeStruct((2 * tokens, LANES), BF16)
    q_pieces = call(
        functools.partial(pack_q_kernel, fold, n_head),
        [q_piece] * members,
        [SCALARS, WHOLE, WHOLE, WHOLE],
        "pack_q",
        scratch=[pltpu.VMEM((LANES, LANES), F32)],
    )(me, queries, output_gradient, outputs)
    kv_pieces = call(
        functools.partial(pack_kv_kernel, fold, n_head),
        [kv_piece] * members,
        [SCALARS, WHOLE, WHOLE],
        "pack_kv",
    )(me, key_vectors, values)

    lse_rows = logsum.reshape(fold, GROUP, block)
    lse_parts = [
        lax.ppermute(
            lax.dynamic_index_in_dim(lse_rows, y ^ mask, 0, keepdims=False),
            "y",
            [(i, i ^ mask) for i in range(fold)],
        )
        if mask
        else lax.dynamic_index_in_dim(lse_rows, y, 0, keepdims=False)
        for mask in range(fold)
    ]
    lse = jnp.stack([lax.select_n(y == 0, lse_parts[fold - 1 - b], lse_parts[b]) for b in range(fold)]) if fold > 1 else lse_parts[0][None]
    lse = lse.reshape(fold, GROUP, n_head, tokens).transpose(0, 2, 1, 3).reshape(members, GROUP, tokens)
    if tokens < LANES:
        lse = jnp.pad(lse, ((0, 0), (0, 0), (0, LANES - tokens)))

    q_own = call(
        functools.partial(assemble_q_kernel, fold, n_head),
        jax.ShapeDtypeStruct((members,) + q_piece.shape, BF16),
        [SCALARS] + [WHOLE] * (members + 1),
        "assemble_q",
    )(me, lse, *exchange(q_pieces))
    kv_own = call(
        assemble_kv_kernel,
        jax.ShapeDtypeStruct((members,) + kv_piece.shape, BF16),
        [SCALARS] + [WHOLE] * members,
        "assemble_kv",
    )(me, *exchange(kv_pieces))

    up = [kv_own]
    down = [q_own]
    for _ in range(reach // 2):
        down.append(along(down[-1], planes, -1))
    for _ in range((reach + 1) // 2):
        up.append(along(up[-1], planes, 1))

    grad_q = [None] * len(down)
    grad_kv = [None] * len(up)
    dq_shape = (q_tiles, HEAD_SIZE, GROUP * TILE)
    dkv_shape = (members, 2 * tokens, HEAD_SIZE)
    inside = jnp.arange(fold, dtype=jnp.int32)
    for distance in range(reach + 1):
        i, j = (distance + 1) // 2, distance // 2
        query_blocks = (z + j) * fold + inside
        key_blocks = (z - i) * fold + inside
        hit = (pair_list[:, 0, None, None] == query_blocks[None, :, None]) & (
            pair_list[:, 1, None, None] == key_blocks[None, None, :]
        )
        codes = jnp.sum(jnp.where(hit, pair_list[:, 2, None, None] + 1, 0), axis=0).astype(jnp.int32)
        last_q = distance == min(2 * j + 1, reach)
        last_kv = distance == min(2 * i, reach)
        has_dq, has_dkv = grad_q[j] is not None, grad_kv[i] is not None
        carried = [g for g in (grad_q[j], grad_kv[i]) if g is not None]
        grad_q[j], grad_kv[i] = call(
            functools.partial(role_kernel, fold, n_head, has_dq, has_dkv),
            [
                jax.ShapeDtypeStruct(dq_shape, BF16 if last_q and j else F32),
                jax.ShapeDtypeStruct(dkv_shape, BF16 if last_kv and i else F32),
            ],
            [SCALARS] + [WHOLE] * (2 + len(carried)),
            f"role_{i}_{j}",
            flops=10 * fold * fold * GROUP * block * block * HEAD_SIZE,
            scratch=[pltpu.VMEM(dq_shape, F32), pltpu.VMEM(dkv_shape, F32)],
        )(codes, down[j], up[i], *carried)

    def gathered(parts, step):
        far = None
        for level in range(len(parts) - 1, 0, -1):
            part = parts[level]
            if far is not None:
                part = (part.astype(F32) + far.astype(F32)).astype(BF16)
            far = along(part, planes, step)
        return far

    far_q = gathered(grad_q, 1)
    far_kv = gathered(grad_kv, -1)
    far = [f for f in (far_q, far_kv) if f is not None]
    out_piece = jax.ShapeDtypeStruct(((GROUP + 2) * tokens, LANES), BF16)
    out_pieces = call(
        functools.partial(finish_kernel, far_q is not None, far_kv is not None),
        [out_piece] * members,
        [SCALARS] + [WHOLE] * (2 + len(far)),
        "finish",
        scratch=[pltpu.VMEM((members, GROUP * tokens, LANES), BF16)],
    )(me, grad_q[0], grad_kv[0], *far)
    return tuple(
        call(
            functools.partial(unpack_kernel, fold, n_head),
            [
                jax.ShapeDtypeStruct((tokens, QUERY_HEADS * HEAD_SIZE), BF16),
                jax.ShapeDtypeStruct((tokens, KEY_VALUE_HEADS * HEAD_SIZE), BF16),
                jax.ShapeDtypeStruct((tokens, KEY_VALUE_HEADS * HEAD_SIZE), BF16),
            ],
            [SCALARS] + [WHOLE] * members,
            "unpack",
        )(me, *exchange(out_pieces))
    )


def solution(mesh):
    n_seq, n_head = mesh.shape["seq"], mesh.shape["head"]
    fold = KEY_VALUE_HEADS // n_head
    assert n_head * fold == KEY_VALUE_HEADS and n_seq % fold == 0
    planes = Mesh(mesh.devices.reshape(n_seq // fold, fold, n_head), ("z", "y", "head"))
    rows = P(("z", "y", "head"), None)
    return jax.shard_map(
        shards,
        mesh=planes,
        in_specs=(rows,) * 5 + (P("head", ("z", "y")), P()),
        out_specs=(rows,) * 3,
        check_vma=False,
    )
```

time: 244 us -> 98.6 us (0.40)
  the two profiles are of different devices: /device:TPU:24 before, /device:TPU:0 now
where the time goes in v1:
time: 98.6 us; the launch traced here: 100 us
  waiting for transfers between devices  46.8 us (47%)
  starting transfers between devices  37.9 us (38%)
  Pallas kernels  10.4 us (11%)
  local copies, waits for them, and re-layouts  3.85 us (4%)
    ppermute x4, waiting for transfers between devices, along(): return lax.ppermute(value, 'z', pairs)  26.3 us
    ppermute x21, waiting for transfers between devices, exchange(): lax.ppermute(pieces[mask], CROSS, [(i, i ^ mask) for i in range(members)])  20.5 us
    ppermute x21, starting transfers between devices, exchange(): lax.ppermute(pieces[mask], CROSS, [(i, i ^ mask) for i in range(members)])  19.9 us
    ppermute x4, starting transfers between devices, along(): return lax.ppermute(value, 'z', pairs)  15 us
    pallas_call x3, Pallas kernels, shards(): call(functools.partial(role_kernel, fold, n_head, has_dq, has_dkv), [jax....  7.31 us
    unnamed x12, local copies, waits for them, and re-layouts  3.13 us
    ppermute x1, starting transfers between devices, shards(): lax.ppermute(lax.dynamic_index_in_dim(lse_rows, y ^ mask, 0, keepdims=Fal...  3.06 us
  transfers between devices with their start and end apart: 26, of which 14 were waited for; matrix products, arithmetic and copies ran while one was open for 0% of the time, Pallas kernels for 7%

profile of v1, /device:TPU:0, one launch (start us, length us, event | category | flops | bytes accessed | tf_op | source)
XLA Modules:
  0.0 100.1 jit_solution(2999824198246867977)
XLA Ops:
  0.6 0.7 reshape.168
  1.4 3.1 %collective-permute-start = (f32[2,512]{1,0:T(2,128)S(1)}, f32[2,512]{1,0:T(2,128)S(1)}, u32[]{:S(2)}, u32[]{:S(2)}) collective-permute-start(f32[2,512]{1,0:T(2,128)S(1)} %dynamic-slice_bitcast_fusion), channel_id=1, source_target_pairs={{0,4},{4,0},{1,5},{5,1},{2,6},{6,2},{3,7},{7,3},{8,12},{12,8},{9,1... | collective-permute-start | bytes 12296 | tf_op jit(solution)/shard_map/ppermute | solution.py:302
  4.4 1.0 %copy-done = bf16[128,2048]{1,0:T(8,128)(2,1)S(1)} copy-done((bf16[128,2048]{1,0:T(8,128)(2,1)S(1)}, bf16[128,2048]{1,0:T(8,128)(2,1)}, u32[]{:S(2)}) %copy-start) | copy-done | bytes 524312
  5.5 1.0 %copy-done.1 = bf16[128,2048]{1,0:T(8,128)(2,1)S(1)} copy-done((bf16[128,2048]{1,0:T(8,128)(2,1)S(1)}, bf16[128,2048]{1,0:T(8,128)(2,1)}, u32[]{:S(2)}) %copy-start.1) | copy-done | bytes 524312
  6.5 1.0 %copy-done.2 = bf16[128,2048]{1,0:T(8,128)(2,1)S(1)} copy-done((bf16[128,2048]{1,0:T(8,128)(2,1)S(1)}, bf16[128,2048]{1,0:T(8,128)(2,1)}, u32[]{:S(2)}) %copy-start.2) | copy-done | bytes 524312
  7.5 0.6 pack_q.1
  8.2 1.6 %collective-permute-start.2 = (bf16[528,128]{1,0:T(8,128)(2,1)S(1)}, bf16[528,128]{1,0:T(8,128)(2,1)S(1)}, u32[]{:S(2)}, u32[]{:S(2)}) collective-permute-start(bf16[528,128]{1,0:T(8,128)(2,1)S(1)} %get-tuple-element.35), channel_id=1, source_target_pairs={{0,2},{1,3},{2,0},{3,1},{4,6},{5,7},{6,4},{7,5},{8,10},{9,11},{10,... | collective-permute-start | bytes 405512 | tf_op jit(solution)/shard_map/ppermute | solution.py:263
  9.8 0.3 collective-permute-start.3
  10.1 0.3 collective-permute-start.4
  10.3 0.8 pack_kv.1
  11.1 1.5 %collective-permute-start.5 = (bf16[528,128]{1,0:T(8,128)(2,1)S(1)}, bf16[528,128]{1,0:T(8,128)(2,1)S(1)}, u32[]{:S(2)}, u32[]{:S(2)}) collective-permute-start(bf16[528,128]{1,0:T(8,128)(2,1)S(1)} %get-tuple-element.38), channel_id=1, source_target_pairs={{0,5},{1,4},{2,7},{3,6},{4,1},{5,0},{6,3},{7,2},{8,13},{9,12},{10,... | collective-permute-start | bytes 405512 | tf_op jit(solution)/shard_map/ppermute | solution.py:263
  12.6 1.5 %collective-permute-start.6 = (bf16[528,128]{1,0:T(8,128)(2,1)S(1)}, bf16[528,128]{1,0:T(8,128)(2,1)S(1)}, u32[]{:S(2)}, u32[]{:S(2)}) collective-permute-start(bf16[528,128]{1,0:T(8,128)(2,1)S(1)} %get-tuple-element.39), channel_id=1, source_target_pairs={{0,6},{1,7},{2,4},{3,5},{4,2},{5,3},{6,0},{7,1},{8,14},{9,15},{10,... | collective-permute-start | bytes 405512 | tf_op jit(solution)/shard_map/ppermute | solution.py:263
  14.1 0.7 collective-permute-done.2.refs_2_
  14.8 0.6 collective-permute-start.7
  15.4 1.3 %collective-permute-done.3.refs_3_ = bf16[528,128]{1,0:T(8,128)(2,1)S(1)} collective-permute-done((bf16[528,128]{1,0:T(8,128)(2,1)S(1)}, bf16[528,128]{1,0:T(8,128)(2,1)S(1)}, u32[]{:S(2)}, u32[]{:S(2)}) %collective-permute-start.3) | collective-permute-done | bytes 135200 | tf_op jit(solution)/shard_map/ppermute | solution.py:263
  16.7 1.1 %collective-permute-start.8 = (bf16[256,128]{1,0:T(8,128)(2,1)}, bf16[256,128]{1,0:T(8,128)(2,1)S(1)}, u32[]{:S(2)}, u32[]{:S(2)}) collective-permute-start(bf16[256,128]{1,0:T(8,128)(2,1)} %get-tuple-element.42), channel_id=1, source_target_pairs={{0,1},{1,0},{2,3},{3,2},{4,5},{5,4},{6,7},{7,6},{8,9},{9,8},{10,11... | collective-permute-start | bytes 196616 | tf_op jit(solution)/shard_map/ppermute | solution.py:263
  17.8 1.5 %collective-permute-start.9 = (bf16[256,128]{1,0:T(8,128)(2,1)}, bf16[256,128]{1,0:T(8,128)(2,1)S(1)}, u32[]{:S(2)}, u32[]{:S(2)}) collective-permute-start(bf16[256,128]{1,0:T(8,128)(2,1)} %get-tuple-element.43), channel_id=1, source_target_pairs={{0,2},{1,3},{2,0},{3,1},{4,6},{5,7},{6,4},{7,5},{8,10},{9,11},{10,... | collective-permute-start | bytes 196616 | tf_op jit(solution)/shard_map/ppermute | solution.py:263
  19.3 4.7 %collective-permute-done.5.refs_5_ = bf16[528,128]{1,0:T(8,128)(2,1)S(1)} collective-permute-done((bf16[528,128]{1,0:T(8,128)(2,1)S(1)}, bf16[528,128]{1,0:T(8,128)(2,1)S(1)}, u32[]{:S(2)}, u32[]{:S(2)}) %collective-permute-start.5) | collective-permute-done | bytes 135200 | tf_op jit(solution)/shard_map/ppermute | solution.py:263
  24.0 1.6 %collective-permute-start.10 = (bf16[256,128]{1,0:T(8,128)(2,1)S(1)}, bf16[256,128]{1,0:T(8,128)(2,1)S(1)}, u32[]{:S(2)}, u32[]{:S(2)}) collective-permute-start(bf16[256,128]{1,0:T(8,128)(2,1)S(1)} %get-tuple-element.44), channel_id=1, source_target_pairs={{0,3},{1,2},{2,1},{3,0},{4,7},{5,6},{6,5},{7,4},{8,11},{9,10},{10,... | collective-permute-start | bytes 196616 | tf_op jit(solution)/shard_map/ppermute | solution.py:263
  25.6 0.5 collective-permute-start.11
  26.2 1.3 %collective-permute-start.16 = (bf16[8,528,128]{2,1,0:T(8,128)(2,1)S(1)}, bf16[8,528,128]{2,1,0:T(8,128)(2,1)S(1)}, u32[]{:S(2)}, u32[]{:S(2)}) collective-permute-start(bf16[8,528,128]{2,1,0:T(8,128)(2,1)S(1)} %assemble_q.1.q_ref), channel_id=1, source_target_pairs={{8,0},{16,8},{24,16},{9,1},{17,9},{25,17},{10,2},{18,10},{26,18},{... | collective-permute-start | bytes 3244040 | tf_op jit(solution)/shard_map/ppermute | solution.py:270
  27.5 1.0 collective-permute-start.12
  28.5 0.7 collective-permute-start.13
  29.2 2.3 %collective-permute-start.14 = (bf16[256,128]{1,0:T(8,128)(2,1)S(1)}, bf16[256,128]{1,0:T(8,128)(2,1)S(1)}, u32[]{:S(2)}, u32[]{:S(2)}) collective-permute-start(bf16[256,128]{1,0:T(8,128)(2,1)S(1)} %get-tuple-element.48), channel_id=1, source_target_pairs={{0,7},{1,6},{2,5},{3,4},{4,3},{5,2},{6,1},{7,0},{8,15},{9,14},{10,... | collective-permute-start | bytes 196616 | tf_op jit(solution)/shard_map/ppermute | solution.py:263
  31.5 0.4 collective-permute-done.12.refs_5_
  31.9 2.4 %collective-permute-done.13.refs_6_ = bf16[256,128]{1,0:T(8,128)(2,1)S(1)} collective-permute-done((bf16[256,128]{1,0:T(8,128)(2,1)S(1)}, bf16[256,128]{1,0:T(8,128)(2,1)S(1)}, u32[]{:S(2)}, u32[]{:S(2)}) %collective-permute-start.13) | collective-permute-done | bytes 65568 | tf_op jit(solution)/shard_map/ppermute | solution.py:263
  34.3 1.0 collective-permute-done.14.refs_7_
  35.3 4.7 %collective-permute-start.15 = (bf16[8,256,128]{2,1,0:T(8,128)(2,1)S(1)}, bf16[8,256,128]{2,1,0:T(8,128)(2,1)S(1)}, u32[]{:S(2)}, u32[]{:S(2)}) collective-permute-start(bf16[8,256,128]{2,1,0:T(8,128)(2,1)S(1)} %assemble_kv.1.kv_ref), channel_id=1, source_target_pairs={{0,8},{8,16},{16,24},{1,9},{9,17},{17,25},{2,10},{10,18},{18,26},{... | collective-permute-start | bytes 1572872 | tf_op jit(solution)/shard_map/ppermute | solution.py:270
  40.4 4.5 %role_0_0.1 = (f32[4,128,512]{2,1,0:T(8,128)S(1)}, f32[8,256,128]{2,1,0:T(8,128)S(1)}) custom-call(s32[2,2]{1,0:T(2,128)S(1)} %get-tuple-element.65.code_ref, bf16[8,528,128]{2,1,0:T(8,128)(2,1)S(1)} %assemble_q.1.q_ref, bf16[8,256,128]{2,1,0:T(8,128)(2,1)S(1)} %assemble_kv.1.kv_ref), custom_call_target="tpu_custom_call" | custom-call | flops 2684354560 | bytes 4194304 | tf_op jit(solution)/shard_map/role_0_0/pallas_call | solution.py:353
  44.9 6.6 %collective-permute-done.15.kv_ref = bf16[8,256,128]{2,1,0:T(8,128)(2,1)S(1)} collective-permute-done((bf16[8,256,128]{2,1,0:T(8,128)(2,1)S(1)}, bf16[8,256,128]{2,1,0:T(8,128)(2,1)S(1)}, u32[]{:S(2)}, u32[]{:S(2)}) %collective-permute-start.15) | collective-permute-done | bytes 524320 | tf_op jit(solution)/shard_map/ppermute | solution.py:270
  51.5 1.4 %role_1_0.1 = (f32[4,128,512]{2,1,0:T(8,128)S(1)}, f32[8,256,128]{2,1,0:T(8,128)S(1)}) custom-call(s32[2,2]{1,0:T(2,128)S(1)} %get-tuple-element.64.code_ref, bf16[8,528,128]{2,1,0:T(8,128)(2,1)S(1)} %assemble_q.1.q_ref, bf16[8,256,128]{2,1,0:T(8,128)(2,1)S(1)} %collective-permute-done.15.kv_ref, f32[4,128,512]{2,1,0:T(8,128)S(1)} %get-tuple-element.49.refs_0_), custom_call_target="tpu_custom_call" | custom-call | flops 2684354560 | bytes 4194304 | tf_op jit(solution)/shard_map/role_1_0/pallas_call | solution.py:353
  52.9 0.5 collective-permute-done.16.q_ref
  53.4 1.4 %role_1_1.1 = (bf16[4,128,512]{2,1,0:T(8,128)(2,1)S(1)}, bf16[8,256,128]{2,1,0:T(8,128)(2,1)S(1)}) custom-call(s32[2,2]{1,0:T(2,128)S(1)} %get-tuple-element.63.code_ref, bf16[8,528,128]{2,1,0:T(8,128)(2,1)S(1)} %collective-permute-done.16.q_ref, bf16[8,256,128]{2,1,0:T(8,128)(2,1)S(1)} %collective-permute-done.15.kv_ref, ...), custom_call_target="tpu_custom_call" | custom-call | flops 2684354560 | bytes 4194304 | tf_op jit(solution)/shard_map/role_1_1/pallas_call | solution.py:353
  54.8 7.7 %collective-permute-start.17 = (bf16[4,128,512]{2,1,0:T(8,128)(2,1)S(1)}, bf16[4,128,512]{2,1,0:T(8,128)(2,1)S(1)}, u32[]{:S(2)}, u32[]{:S(2)}) collective-permute-start(bf16[4,128,512]{2,1,0:T(8,128)(2,1)S(1)} %get-tuple-element.53), channel_id=1, source_target_pairs={{0,8},{8,16},{16,24},{1,9},{9,17},{17,25},{2,10},{10,18},{18,26},{... | collective-permute-start | bytes 1572872 | tf_op jit(solution)/shard_map/ppermute | solution.py:270
  62.5 1.3 %collective-permute-start.18 = (bf16[8,256,128]{2,1,0:T(8,128)(2,1)S(1)}, bf16[8,256,128]{2,1,0:T(8,128)(2,1)S(1)}, u32[]{:S(2)}, u32[]{:S(2)}) collective-permute-start(bf16[8,256,128]{2,1,0:T(8,128)(2,1)S(1)} %get-tuple-element.54), channel_id=1, source_target_pairs={{8,0},{16,8},{24,16},{9,1},{17,9},{25,17},{10,2},{18,10},{26,18},{... | collective-permute-start | bytes 1572872 | tf_op jit(solution)/shard_map/ppermute | solution.py:270
  63.8 9.2 %collective-permute-done.17.refs_0_ = bf16[4,128,512]{2,1,0:T(8,128)(2,1)S(1)} collective-permute-done((bf16[4,128,512]{2,1,0:T(8,128)(2,1)S(1)}, bf16[4,128,512]{2,1,0:T(8,128)(2,1)S(1)}, u32[]{:S(2)}, u32[]{:S(2)}) %collective-permute-start.17) | collective-permute-done | bytes 524320 | tf_op jit(solution)/shard_map/ppermute | solution.py:270
  73.0 10.1 %collective-permute-done.18.refs_1_ = bf16[8,256,128]{2,1,0:T(8,128)(2,1)S(1)} collective-permute-done((bf16[8,256,128]{2,1,0:T(8,128)(2,1)S(1)}, bf16[8,256,128]{2,1,0:T(8,128)(2,1)S(1)}, u32[]{:S(2)}, u32[]{:S(2)}) %collective-permute-start.18) | collective-permute-done | bytes 524320 | tf_op jit(solution)/shard_map/ppermute | solution.py:270
  83.0 0.3 finish.1
  83.4 0.5 collective-permute-start.20
  83.9 1.3 %collective-permute-start.21 = (bf16[512,128]{1,0:T(8,128)(2,1)S(1)}, bf16[512,128]{1,0:T(8,128)(2,1)S(1)}, u32[]{:S(2)}, u32[]{:S(2)}) collective-permute-start(bf16[512,128]{1,0:T(8,128)(2,1)S(1)} %get-tuple-element.58), channel_id=1, source_target_pairs={{0,3},{1,2},{2,1},{3,0},{4,7},{5,6},{6,5},{7,4},{8,11},{9,10},{10,... | collective-permute-start | bytes 393224 | tf_op jit(solution)/shard_map/ppermute | solution.py:263
  85.3 0.5 collective-permute-start.22
  85.8 1.2 %collective-permute-start.23 = (bf16[512,128]{1,0:T(8,128)(2,1)S(1)}, bf16[512,128]{1,0:T(8,128)(2,1)S(1)}, u32[]{:S(2)}, u32[]{:S(2)}) collective-permute-start(bf16[512,128]{1,0:T(8,128)(2,1)S(1)} %get-tuple-element.60), channel_id=1, source_target_pairs={{0,5},{1,4},{2,7},{3,6},{4,1},{5,0},{6,3},{7,2},{8,13},{9,12},{10,... | collective-permute-start | bytes 393224 | tf_op jit(solution)/shard_map/ppermute | solution.py:263
  87.0 1.6 %collective-permute-start.24 = (bf16[512,128]{1,0:T(8,128)(2,1)S(1)}, bf16[512,128]{1,0:T(8,128)(2,1)S(1)}, u32[]{:S(2)}, u32[]{:S(2)}) collective-permute-start(bf16[512,128]{1,0:T(8,128)(2,1)S(1)} %get-tuple-element.61), channel_id=1, source_target_pairs={{0,6},{1,7},{2,4},{3,5},{4,2},{5,3},{6,0},{7,1},{8,14},{9,15},{10,... | collective-permute-start | bytes 393224 | tf_op jit(solution)/shard_map/ppermute | solution.py:263
  88.6 1.2 %collective-permute-done.20.refs_2_ = bf16[512,128]{1,0:T(8,128)(2,1)S(1)} collective-permute-done((bf16[512,128]{1,0:T(8,128)(2,1)S(1)}, bf16[512,128]{1,0:T(8,128)(2,1)S(1)}, u32[]{:S(2)}, u32[]{:S(2)}) %collective-permute-start.20) | collective-permute-done | bytes 131104 | tf_op jit(solution)/shard_map/ppermute | solution.py:263
  89.9 0.3 collective-permute-start.25
  90.1 1.5 %collective-permute-done.21.refs_3_ = bf16[512,128]{1,0:T(8,128)(2,1)S(1)} collective-permute-done((bf16[512,128]{1,0:T(8,128)(2,1)S(1)}, bf16[512,128]{1,0:T(8,128)(2,1)S(1)}, u32[]{:S(2)}, u32[]{:S(2)}) %collective-permute-start.21) | collective-permute-done | bytes 131104 | tf_op jit(solution)/shard_map/ppermute | solution.py:263
  91.7 7.1 %collective-permute-done.23.refs_5_ = bf16[512,128]{1,0:T(8,128)(2,1)S(1)} collective-permute-done((bf16[512,128]{1,0:T(8,128)(2,1)S(1)}, bf16[512,128]{1,0:T(8,128)(2,1)S(1)}, u32[]{:S(2)}, u32[]{:S(2)}) %collective-permute-start.23) | collective-permute-done | bytes 131104 | tf_op jit(solution)/shard_map/ppermute | solution.py:263
  98.9 1.2 %unpack.1 = (bf16[128,2048]{1,0:T(8,128)(2,1)}, bf16[128,1024]{1,0:T(8,128)(2,1)}, bf16[128,1024]{1,0:T(8,128)(2,1)}) custom-call(s32[1]{0:T(128)} %bitcast.me_ref, bf16[512,128]{1,0:T(8,128)(2,1)S(1)} %get-tuple-element.55.refs_0_, bf16[512,128]{1,0:T(8,128)(2,1)S(1)} %collective-permute-done.19.refs_1_, ...), custom_call_target="tpu_custom_call" | custom-call | bytes 4194304 | tf_op jit(solution)/shard_map/unpack/pallas_call | solution.py:386
  (35 shorter events, 0.7 us)
Async XLA Ops:
  1.4 9.8 %collective-permute-start = (f32[2,512]{1,0:T(2,128)S(1)}, f32[2,512]{1,0:T(2,128)S(1)}, u32[]{:S(2)}, u32[]{:S(2)}) collective-permute-start(f32[2,512]{1,0:T(2,128)S(1)} %dynamic-slice_bitcast_fusion), channel_id=1, source_target_pairs={{0,4},{4,0},{1,5},{5,1},{2,6},{6,2},{3,7},{7,3},{8,12},{12,8},{9,1... | collective-permute-start | bytes 12296 | tf_op jit(solution)/shard_map/ppermute | solution.py:302
  4.4 1.0 %copy-start = (bf16[128,2048]{1,0:T(8,128)(2,1)S(1)}, bf16[128,2048]{1,0:T(8,128)(2,1)}, u32[]{:S(2)}) copy-start(bf16[128,2048]{1,0:T(8,128)(2,1)} %q_ref.1) | copy-start | bytes 1572868
  5.5 1.0 %copy-start.1 = (bf16[128,2048]{1,0:T(8,128)(2,1)S(1)}, bf16[128,2048]{1,0:T(8,128)(2,1)}, u32[]{:S(2)}) copy-start(bf16[128,2048]{1,0:T(8,128)(2,1)} %do_ref.1) | copy-start | bytes 1572868
  6.5 1.0 %copy-start.2 = (bf16[128,2048]{1,0:T(8,128)(2,1)S(1)}, bf16[128,2048]{1,0:T(8,128)(2,1)}, u32[]{:S(2)}) copy-start(bf16[128,2048]{1,0:T(8,128)(2,1)} %o_ref.1) | copy-start | bytes 1572868
  7.5 2.8 %copy-start.3 = (bf16[128,1024]{1,0:T(8,128)(2,1)S(1)}, bf16[128,1024]{1,0:T(8,128)(2,1)}, u32[]{:S(2)}) copy-start(bf16[128,1024]{1,0:T(8,128)(2,1)} %k_ref.1) | copy-start | bytes 786436
  7.5 2.8 %copy-start.4 = (bf16[128,1024]{1,0:T(8,128)(2,1)S(1)}, bf16[128,1024]{1,0:T(8,128)(2,1)}, u32[]{:S(2)}) copy-start(bf16[128,1024]{1,0:T(8,128)(2,1)} %v_ref.1) | copy-start | bytes 786436
  8.2 4.4 %collective-permute-start.1 = (bf16[528,128]{1,0:T(8,128)(2,1)S(1)}, bf16[528,128]{1,0:T(8,128)(2,1)S(1)}, u32[]{:S(2)}, u32[]{:S(2)}) collective-permute-start(bf16[528,128]{1,0:T(8,128)(2,1)S(1)} %get-tuple-element.34), channel_id=1, source_target_pairs={{0,1},{1,0},{2,3},{3,2},{4,5},{5,4},{6,7},{7,6},{8,9},{9,8},{10,11... | collective-permute-start | bytes 405512 | tf_op jit(solution)/shard_map/ppermute | solution.py:263
  8.2 6.5 %collective-permute-start.2 = (bf16[528,128]{1,0:T(8,128)(2,1)S(1)}, bf16[528,128]{1,0:T(8,128)(2,1)S(1)}, u32[]{:S(2)}, u32[]{:S(2)}) collective-permute-start(bf16[528,128]{1,0:T(8,128)(2,1)S(1)} %get-tuple-element.35), channel_id=1, source_target_pairs={{0,2},{1,3},{2,0},{3,1},{4,6},{5,7},{6,4},{7,5},{8,10},{9,11},{10,... | collective-permute-start | bytes 405512 | tf_op jit(solution)/shard_map/ppermute | solution.py:263
  9.8 6.9 %collective-permute-start.3 = (bf16[528,128]{1,0:T(8,128)(2,1)S(1)}, bf16[528,128]{1,0:T(8,128)(2,1)S(1)}, u32[]{:S(2)}, u32[]{:S(2)}) collective-permute-start(bf16[528,128]{1,0:T(8,128)(2,1)S(1)} %get-tuple-element.36), channel_id=1, source_target_pairs={{0,3},{1,2},{2,1},{3,0},{4,7},{5,6},{6,5},{7,4},{8,11},{9,10},{10,... | collective-permute-start | bytes 405512 | tf_op jit(solution)/shard_map/ppermute | solution.py:263
  10.1 7.7 %collective-permute-start.4 = (bf16[528,128]{1,0:T(8,128)(2,1)S(1)}, bf16[528,128]{1,0:T(8,128)(2,1)S(1)}, u32[]{:S(2)}, u32[]{:S(2)}) collective-permute-start(bf16[528,128]{1,0:T(8,128)(2,1)S(1)} %get-tuple-element.37), channel_id=1, source_target_pairs={{0,4},{1,5},{2,6},{3,7},{4,0},{5,1},{6,2},{7,3},{8,12},{9,13},{10,... | collective-permute-start | bytes 405512 | tf_op jit(solution)/shard_map/ppermute | solution.py:263
  11.1 12.9 %collective-permute-start.5 = (bf16[528,128]{1,0:T(8,128)(2,1)S(1)}, bf16[528,128]{1,0:T(8,128)(2,1)S(1)}, u32[]{:S(2)}, u32[]{:S(2)}) collective-permute-start(bf16[528,128]{1,0:T(8,128)(2,1)S(1)} %get-tuple-element.38), channel_id=1, source_target_pairs={{0,5},{1,4},{2,7},{3,6},{4,1},{5,0},{6,3},{7,2},{8,13},{9,12},{10,... | collective-permute-start | bytes 405512 | tf_op jit(solution)/shard_map/ppermute | solution.py:263
  12.6 13.0 %collective-permute-start.6 = (bf16[528,128]{1,0:T(8,128)(2,1)S(1)}, bf16[528,128]{1,0:T(8,128)(2,1)S(1)}, u32[]{:S(2)}, u32[]{:S(2)}) collective-permute-start(bf16[528,128]{1,0:T(8,128)(2,1)S(1)} %get-tuple-element.39), channel_id=1, source_target_pairs={{0,6},{1,7},{2,4},{3,5},{4,2},{5,3},{6,0},{7,1},{8,14},{9,15},{10,... | collective-permute-start | bytes 405512 | tf_op jit(solution)/shard_map/ppermute | solution.py:263
  14.8 11.3 %collective-permute-start.7 = (bf16[528,128]{1,0:T(8,128)(2,1)S(1)}, bf16[528,128]{1,0:T(8,128)(2,1)S(1)}, u32[]{:S(2)}, u32[]{:S(2)}) collective-permute-start(bf16[528,128]{1,0:T(8,128)(2,1)S(1)} %get-tuple-element.40), channel_id=1, source_target_pairs={{0,7},{1,6},{2,5},{3,4},{4,3},{5,2},{6,1},{7,0},{8,15},{9,14},{10,... | collective-permute-start | bytes 405512 | tf_op jit(solution)/shard_map/ppermute | solution.py:263
  16.7 10.9 %collective-permute-start.8 = (bf16[256,128]{1,0:T(8,128)(2,1)}, bf16[256,128]{1,0:T(8,128)(2,1)S(1)}, u32[]{:S(2)}, u32[]{:S(2)}) collective-permute-start(bf16[256,128]{1,0:T(8,128)(2,1)} %get-tuple-element.42), channel_id=1, source_target_pairs={{0,1},{1,0},{2,3},{3,2},{4,5},{5,4},{6,7},{7,6},{8,9},{9,8},{10,11... | collective-permute-start | bytes 196616 | tf_op jit(solution)/shard_map/ppermute | solution.py:263
  17.8 10.7 %collective-permute-start.9 = (bf16[256,128]{1,0:T(8,128)(2,1)}, bf16[256,128]{1,0:T(8,128)(2,1)S(1)}, u32[]{:S(2)}, u32[]{:S(2)}) collective-permute-start(bf16[256,128]{1,0:T(8,128)(2,1)} %get-tuple-element.43), channel_id=1, source_target_pairs={{0,2},{1,3},{2,0},{3,1},{4,6},{5,7},{6,4},{7,5},{8,10},{9,11},{10,... | collective-permute-start | bytes 196616 | tf_op jit(solution)/shard_map/ppermute | solution.py:263
  24.0 5.2 %collective-permute-start.10 = (bf16[256,128]{1,0:T(8,128)(2,1)S(1)}, bf16[256,128]{1,0:T(8,128)(2,1)S(1)}, u32[]{:S(2)}, u32[]{:S(2)}) collective-permute-start(bf16[256,128]{1,0:T(8,128)(2,1)S(1)} %get-tuple-element.44), channel_id=1, source_target_pairs={{0,3},{1,2},{2,1},{3,0},{4,7},{5,6},{6,5},{7,4},{8,11},{9,10},{10,... | collective-permute-start | bytes 196616 | tf_op jit(solution)/shard_map/ppermute | solution.py:263
  25.6 5.9 %collective-permute-start.11 = (bf16[256,128]{1,0:T(8,128)(2,1)S(1)}, bf16[256,128]{1,0:T(8,128)(2,1)S(1)}, u32[]{:S(2)}, u32[]{:S(2)}) collective-permute-start(bf16[256,128]{1,0:T(8,128)(2,1)S(1)} %get-tuple-element.45), channel_id=1, source_target_pairs={{0,4},{1,5},{2,6},{3,7},{4,0},{5,1},{6,2},{7,3},{8,12},{9,13},{10,... | collective-permute-start | bytes 196616 | tf_op jit(solution)/shard_map/ppermute | solution.py:263
  26.1 1.4 %copy-start.5 = (s32[20,3]{0,1:T(4,128)S(1)}, s32[20,3]{0,1:T(4,128)}, u32[]{:S(2)}) copy-start(s32[20,3]{0,1:T(4,128)} %param.13) | copy-start | bytes 724
  26.2 27.2 %collective-permute-start.16 = (bf16[8,528,128]{2,1,0:T(8,128)(2,1)S(1)}, bf16[8,528,128]{2,1,0:T(8,128)(2,1)S(1)}, u32[]{:S(2)}, u32[]{:S(2)}) collective-permute-start(bf16[8,528,128]{2,1,0:T(8,128)(2,1)S(1)} %assemble_q.1.q_ref), channel_id=1, source_target_pairs={{8,0},{16,8},{24,16},{9,1},{17,9},{25,17},{10,2},{18,10},{26,18},{... | collective-permute-start | bytes 3244040 | tf_op jit(solution)/shard_map/ppermute | solution.py:270
  27.5 4.4 %collective-permute-start.12 = (bf16[256,128]{1,0:T(8,128)(2,1)S(1)}, bf16[256,128]{1,0:T(8,128)(2,1)S(1)}, u32[]{:S(2)}, u32[]{:S(2)}) collective-permute-start(bf16[256,128]{1,0:T(8,128)(2,1)S(1)} %get-tuple-element.46), channel_id=1, source_target_pairs={{0,5},{1,4},{2,7},{3,6},{4,1},{5,0},{6,3},{7,2},{8,13},{9,12},{10,... | collective-permute-start | bytes 196616 | tf_op jit(solution)/shard_map/ppermute | solution.py:263
  28.5 5.9 %collective-permute-start.13 = (bf16[256,128]{1,0:T(8,128)(2,1)S(1)}, bf16[256,128]{1,0:T(8,128)(2,1)S(1)}, u32[]{:S(2)}, u32[]{:S(2)}) collective-permute-start(bf16[256,128]{1,0:T(8,128)(2,1)S(1)} %get-tuple-element.47), channel_id=1, source_target_pairs={{0,6},{1,7},{2,4},{3,5},{4,2},{5,3},{6,0},{7,1},{8,14},{9,15},{10,... | collective-permute-start | bytes 196616 | tf_op jit(solution)/shard_map/ppermute | solution.py:263
  29.2 6.1 %collective-permute-start.14 = (bf16[256,128]{1,0:T(8,128)(2,1)S(1)}, bf16[256,128]{1,0:T(8,128)(2,1)S(1)}, u32[]{:S(2)}, u32[]{:S(2)}) collective-permute-start(bf16[256,128]{1,0:T(8,128)(2,1)S(1)} %get-tuple-element.48), channel_id=1, source_target_pairs={{0,7},{1,6},{2,5},{3,4},{4,3},{5,2},{6,1},{7,0},{8,15},{9,14},{10,... | collective-permute-start | bytes 196616 | tf_op jit(solution)/shard_map/ppermute | solution.py:263
  35.3 16.1 %collective-permute-start.15 = (bf16[8,256,128]{2,1,0:T(8,128)(2,1)S(1)}, bf16[8,256,128]{2,1,0:T(8,128)(2,1)S(1)}, u32[]{:S(2)}, u32[]{:S(2)}) collective-permute-start(bf16[8,256,128]{2,1,0:T(8,128)(2,1)S(1)} %assemble_kv.1.kv_ref), channel_id=1, source_target_pairs={{0,8},{8,16},{16,24},{1,9},{9,17},{17,25},{2,10},{10,18},{18,26},{... | collective-permute-start | bytes 1572872 | tf_op jit(solution)/shard_map/ppermute | solution.py:270
  54.8 18.2 %collective-permute-start.17 = (bf16[4,128,512]{2,1,0:T(8,128)(2,1)S(1)}, bf16[4,128,512]{2,1,0:T(8,128)(2,1)S(1)}, u32[]{:S(2)}, u32[]{:S(2)}) collective-permute-start(bf16[4,128,512]{2,1,0:T(8,128)(2,1)S(1)} %get-tuple-element.53), channel_id=1, source_target_pairs={{0,8},{8,16},{16,24},{1,9},{9,17},{17,25},{2,10},{10,18},{18,26},{... | collective-permute-start | bytes 1572872 | tf_op jit(solution)/shard_map/ppermute | solution.py:270
  62.5 20.6 %collective-permute-start.18 = (bf16[8,256,128]{2,1,0:T(8,128)(2,1)S(1)}, bf16[8,256,128]{2,1,0:T(8,128)(2,1)S(1)}, u32[]{:S(2)}, u32[]{:S(2)}) collective-permute-start(bf16[8,256,128]{2,1,0:T(8,128)(2,1)S(1)} %get-tuple-element.54), channel_id=1, source_target_pairs={{8,0},{16,8},{24,16},{9,1},{17,9},{25,17},{10,2},{18,10},{26,18},{... | collective-permute-start | bytes 1572872 | tf_op jit(solution)/shard_map/ppermute | solution.py:270
  83.3 3.6 %collective-permute-start.19 = (bf16[512,128]{1,0:T(8,128)(2,1)S(1)}, bf16[512,128]{1,0:T(8,128)(2,1)S(1)}, u32[]{:S(2)}, u32[]{:S(2)}) collective-permute-start(bf16[512,128]{1,0:T(8,128)(2,1)S(1)} %get-tuple-element.56), channel_id=1, source_target_pairs={{0,1},{1,0},{2,3},{3,2},{4,5},{5,4},{6,7},{7,6},{8,9},{9,8},{10,11... | collective-permute-start | bytes 393224 | tf_op jit(solution)/shard_map/ppermute | solution.py:263
  83.4 6.4 %collective-permute-start.20 = (bf16[512,128]{1,0:T(8,128)(2,1)S(1)}, bf16[512,128]{1,0:T(8,128)(2,1)S(1)}, u32[]{:S(2)}, u32[]{:S(2)}) collective-permute-start(bf16[512,128]{1,0:T(8,128)(2,1)S(1)} %get-tuple-element.57), channel_id=1, source_target_pairs={{0,2},{1,3},{2,0},{3,1},{4,6},{5,7},{6,4},{7,5},{8,10},{9,11},{10,... | collective-permute-start | bytes 393224 | tf_op jit(solution)/shard_map/ppermute | solution.py:263
  83.9 7.6 %collective-permute-start.21 = (bf16[512,128]{1,0:T(8,128)(2,1)S(1)}, bf16[512,128]{1,0:T(8,128)(2,1)S(1)}, u32[]{:S(2)}, u32[]{:S(2)}) collective-permute-start(bf16[512,128]{1,0:T(8,128)(2,1)S(1)} %get-tuple-element.58), channel_id=1, source_target_pairs={{0,3},{1,2},{2,1},{3,0},{4,7},{5,6},{6,5},{7,4},{8,11},{9,10},{10,... | collective-permute-start | bytes 393224 | tf_op jit(solution)/shard_map/ppermute | solution.py:263
  85.3 6.4 %collective-permute-start.22 = (bf16[512,128]{1,0:T(8,128)(2,1)S(1)}, bf16[512,128]{1,0:T(8,128)(2,1)S(1)}, u32[]{:S(2)}, u32[]{:S(2)}) collective-permute-start(bf16[512,128]{1,0:T(8,128)(2,1)S(1)} %get-tuple-element.59), channel_id=1, source_target_pairs={{0,4},{1,5},{2,6},{3,7},{4,0},{5,1},{6,2},{7,3},{8,12},{9,13},{10,... | collective-permute-start | bytes 393224 | tf_op jit(solution)/shard_map/ppermute | solution.py:263
  85.8 13.0 %collective-permute-start.23 = (bf16[512,128]{1,0:T(8,128)(2,1)S(1)}, bf16[512,128]{1,0:T(8,128)(2,1)S(1)}, u32[]{:S(2)}, u32[]{:S(2)}) collective-permute-start(bf16[512,128]{1,0:T(8,128)(2,1)S(1)} %get-tuple-element.60), channel_id=1, source_target_pairs={{0,5},{1,4},{2,7},{3,6},{4,1},{5,0},{6,3},{7,2},{8,13},{9,12},{10,... | collective-permute-start | bytes 393224 | tf_op jit(solution)/shard_map/ppermute | solution.py:263
  87.0 11.9 %collective-permute-start.24 = (bf16[512,128]{1,0:T(8,128)(2,1)S(1)}, bf16[512,128]{1,0:T(8,128)(2,1)S(1)}, u32[]{:S(2)}, u32[]{:S(2)}) collective-permute-start(bf16[512,128]{1,0:T(8,128)(2,1)S(1)} %get-tuple-element.61), channel_id=1, source_target_pairs={{0,6},{1,7},{2,4},{3,5},{4,2},{5,3},{6,0},{7,1},{8,14},{9,15},{10,... | collective-permute-start | bytes 393224 | tf_op jit(solution)/shard_map/ppermute | solution.py:263
  89.9 9.0 %collective-permute-start.25 = (bf16[512,128]{1,0:T(8,128)(2,1)S(1)}, bf16[512,128]{1,0:T(8,128)(2,1)S(1)}, u32[]{:S(2)}, u32[]{:S(2)}) collective-permute-start(bf16[512,128]{1,0:T(8,128)(2,1)S(1)} %get-tuple-element.62), channel_id=1, source_target_pairs={{0,7},{1,6},{2,5},{3,4},{4,3},{5,2},{6,1},{7,0},{8,15},{9,14},{10,... | collective-permute-start | bytes 393224 | tf_op jit(solution)/shard_map/ppermute | solution.py:263

commit v2 on v0

v2 whole, which is shorter than its diff:
```python
import functools
import math

import jax
import jax.numpy as jnp
from jax import lax
from jax.experimental import pallas as pl
from jax.experimental.pallas import tpu as pltpu
from jax.sharding import Mesh, PartitionSpec as P


HEAD_SIZE = 128
KEY_VALUE_HEADS = 8
QUERY_HEADS = 16
WIN = 5
GROUP = QUERY_HEADS // KEY_VALUE_HEADS
CORES = 2
KEY_TILE = 256
QUERY_TILE = 128
LANES = 128
PACK = 16
LOG2E = math.log2(math.e)
SCALE = 1.0 / math.sqrt(HEAD_SIZE)
BF16 = jnp.bfloat16
F32 = jnp.float32
CROSS = ("y", "x")
WHOLE = pl.BlockSpec(memory_space=pltpu.VMEM)
SCALARS = pl.BlockSpec(memory_space=pltpu.SMEM)
VMEM_BYTES = 16 * 1024 * 1024


def call(kernel, out_shape, in_specs, flops=0, moved=4 << 20, scratch=()):
    return pl.pallas_call(
        kernel,
        out_shape=out_shape,
        in_specs=in_specs,
        out_specs=jax.tree.map(lambda _: WHOLE, out_shape),
        scratch_shapes=scratch,
        cost_estimate=pl.CostEstimate(flops=flops, bytes_accessed=moved, transcendentals=0),
        compiler_params=pltpu.CompilerParams(vmem_limit_bytes=VMEM_BYTES),
    )


def split3(x):
    hi = x.astype(BF16)
    rest = x - hi.astype(F32)
    mid = rest.astype(BF16)
    low = (rest - mid.astype(F32)).astype(BF16)
    return hi, mid, low


def round_up(n, to):
    return -(-n // to) * to


class Plan:
    def __init__(self, fold, n_x, tokens):
        self.fold, self.n_x, self.tokens = fold, n_x, tokens
        self.chips = fold * n_x
        self.kv_heads = KEY_VALUE_HEADS // self.chips
        self.q_heads = self.kv_heads * GROUP
        self.block = n_x * CORES * tokens
        self.q_rows = self.q_heads * tokens
        self.kv_rows = 2 * self.kv_heads * tokens
        self.aux_sent = round_up(3 * self.q_heads, PACK)
        self.aux = round_up(6 * self.q_heads, PACK)
        self.q_tiles = n_x * tokens // QUERY_TILE
        self.k_tiles = self.block // KEY_TILE
        assert self.k_tiles == 2

    def first_kv_head(self, chip):
        return ((chip % self.n_x) * self.fold + chip // self.n_x) * self.kv_heads


def columns(ref, head):
    return ref.at[:, pl.ds(pl.multiple_of(head * HEAD_SIZE, LANES), HEAD_SIZE)]


def padded_lanes(x):
    rows, width = x.shape
    if width == LANES:
        return x
    return jnp.concatenate([x, jnp.zeros((rows, LANES - width), x.dtype)], axis=1)


def padded_rows(terms, rows):
    have = sum(t.shape[0] for t in terms)
    if have < rows:
        terms = terms + [jnp.zeros((rows - have, LANES), BF16)]
    return jnp.concatenate(terms, axis=0)


def fill_q(plan, me_ref, q_ref, pieces):
    tokens = plan.tokens
    for mask, out in enumerate(pieces):
        kv_head = plan.first_kv_head(me_ref[0] ^ mask)
        for g in range(plan.q_heads):
            out[g * tokens : (g + 1) * tokens, :] = columns(q_ref, kv_head * GROUP + g)[...]


def pack_kernel(plan, me_ref, do_hbm, o_hbm, k_hbm, v_hbm, q_hbm, *refs):
    pieces, q_pieces = refs[: plan.chips], refs[plan.chips : 2 * plan.chips]
    do_ref, o_ref, k_ref, v_ref, q_ref, delta_ref, arrived = refs[2 * plan.chips :]
    tokens = plan.tokens
    half = tokens // 2
    loads = []
    for n, (source, target) in enumerate(
        ((do_hbm, do_ref), (o_hbm, o_ref), (k_hbm, k_ref), (v_hbm, v_ref), (q_hbm, q_ref))
    ):
        pair = []
        for part in range(2):
            rows = pl.ds(part * half, half)
            copy = pltpu.make_async_copy(source.at[rows], target.at[rows], arrived.at[n, part])
            copy.start()
            pair.append(copy)
        loads.append(pair)

    def wait_for(n):
        for copy in loads[n]:
            copy.wait()

    wait_for(0)
    wait_for(1)
    sums = []
    for head in range(QUERY_HEADS):
        cols = slice(head * HEAD_SIZE, (head + 1) * HEAD_SIZE)
        product = do_ref[:, cols].astype(F32) * o_ref[:, cols].astype(F32)
        sums.append(jnp.sum(product, axis=1, keepdims=True))
    sums.append(jnp.zeros((tokens, LANES - QUERY_HEADS), F32))
    delta_ref[...] = padded_lanes(jnp.concatenate(sums, axis=1).T)
    wait_for(2)
    wait_for(3)
    for mask, out in enumerate(pieces):
        kv_head = plan.first_kv_head(me_ref[0] ^ mask)
        terms = []
        for g in range(plan.q_heads):
            head = kv_head * GROUP + g
            out[g * tokens : (g + 1) * tokens, :] = columns(do_ref, head)[...]
            terms.extend(split3(delta_ref[pl.ds(head, 1), :]))
        for h in range(plan.kv_heads):
            at = plan.q_rows + h * tokens
            out[at : at + tokens, :] = columns(k_ref, kv_head + h)[...]
            at += plan.kv_heads * tokens
            out[at : at + tokens, :] = columns(v_ref, kv_head + h)[...]
        out[plan.q_rows + plan.kv_rows :, :] = padded_rows(terms, plan.aux_sent)
    wait_for(4)
    fill_q(plan, me_ref, q_ref, q_pieces)


def pack_q_kernel(plan, me_ref, q_ref, *pieces):
    fill_q(plan, me_ref, q_ref, pieces)


def assemble_kernel(plan, me_ref, lse_ref, *refs):
    pieces, (do_out, kv_out) = refs[:-2], refs[-2:]
    tokens, split = plan.tokens, plan.q_rows + plan.kv_rows
    for mask, piece in enumerate(pieces):
        chip = me_ref[0] ^ mask
        chunk = (chip % plan.n_x) * CORES + me_ref[1]
        do_out[chip, : plan.q_rows, :] = piece[: plan.q_rows, :]
        kv_out[chip] = piece[plan.q_rows : split, :]
        terms = [piece[split : split + 3 * plan.q_heads, :]]
        for g in range(plan.q_heads):
            if tokens == LANES:
                lanes = pl.ds(pl.multiple_of(chunk * LANES, LANES), LANES)
                row = lse_ref[mask // plan.n_x, pl.ds(g, 1), lanes]
            else:
                row = lse_ref[mask // plan.n_x, chunk, pl.ds(g, 1), :]
            terms.extend(split3(row))
        do_out[chip, plan.q_rows :, :] = padded_rows(terms, plan.aux)


def merge_kernel(me_ref, keep_ref, given_ref, *pieces):
    for mask, out in enumerate(pieces):
        chip = me_ref[0] ^ mask
        out[...] = (keep_ref[chip] + given_ref[chip].astype(F32)).astype(BF16)


def lane_row(parts, tokens):
    row = parts[0]
    lane = lax.broadcasted_iota(jnp.int32, row.shape, 1)
    for n, part in enumerate(parts[1:], 1):
        row = jnp.where(lane >= n * tokens, pltpu.roll(part, n * tokens, 1), row)
    return row


def role_kernel(plan, has_dq, me_ref, code_ref, mine_ref, sib_ref, *refs):
    refs = list(refs)
    levels, chips = len(has_dq), plan.chips
    q_pieces = [[refs.pop(0) for _ in range(chips)] for _ in range(levels)]
    do_refs = [refs.pop(0) for _ in range(levels)]
    dq_ins = [refs.pop(0) if has else None for has in has_dq]
    dq_outs = [refs.pop(0) for _ in range(levels)]
    keep, give, kv_ref, q_ref, do_ref, dq_ref, dkv_ref = refs
    core = me_ref[1]
    tokens, n_x, fold = plan.tokens, plan.n_x, plan.fold
    q_per = QUERY_TILE // tokens
    k_per = KEY_TILE // tokens
    kv_ref[core] = mine_ref[...]
    kv_ref[1 - core] = sib_ref[...]
    dkv_ref[...] = jnp.zeros_like(dkv_ref)
    for level in range(levels):
        for mask in range(chips):
            q_ref[level, me_ref[0] ^ mask] = q_pieces[level][mask][...]
        do_ref[level] = do_refs[level][...]
        dq_ref[level] = dq_ins[level][...] if has_dq[level] else jnp.zeros_like(dq_outs[level], F32)

    def q_start(q_in):
        return (q_in * q_per * CORES + core) * tokens

    def q_end(q_in):
        return ((q_in * q_per + q_per - 1) * CORES + core) * tokens + tokens - 1

    last = (((1,), (1,)), ((), ()))

    def row(level, query_block, q_in, key_block, k_tiles, code, masked):
        q_chip = query_block * n_x + q_in * q_per
        tile = query_block * plan.q_tiles + q_in

        def q_part(ref, g):
            return [ref[level, q_chip + n, g * tokens : (g + 1) * tokens, :] for n in range(q_per)]

        def k_place(k_in):
            return [
                (n % CORES, key_block * n_x + k_in * (k_per // CORES) + n // CORES) for n in range(k_per)
            ]

        def k_part(which, h, k_in):
            at = (which * plan.kv_heads + h) * tokens
            return jnp.concatenate([kv_ref[c, chip, at : at + tokens, :] for c, chip in k_place(k_in)], axis=0)

        groups = [do_ref[level, q_chip + n, plan.q_rows :, :].astype(F32) for n in range(q_per)]

        def aux(which, g):
            at = (which * plan.q_heads + g) * 3
            return lane_row([a[at : at + 1] + a[at + 1 : at + 2] + a[at + 2 : at + 3] for a in groups], tokens)

        queries = []
        for h in range(plan.kv_heads):
            heads = range(h * GROUP, (h + 1) * GROUP)
            q2 = jnp.concatenate([r for g in heads for r in q_part(q_ref, g)], axis=0)
            do2 = jnp.concatenate([r for g in heads for r in q_part(do_ref, g)], axis=0)
            delta = jnp.concatenate([aux(0, g) for g in heads], axis=1)
            lse = jnp.concatenate([aux(1, g) for g in heads], axis=1) * LOG2E
            queries.append((q2, do2, delta, lse))
        units = [(h, k_in) for k_in in k_tiles for h in range(plan.kv_heads)]

        def front(unit):
            h, k_in = unit
            q2, do2, _, _ = queries[h]
            k, v = k_part(0, h, k_in), k_part(1, h, k_in)
            scores = lax.dot_general(k, q2, last, preferred_element_type=F32)
            dprobs = lax.dot_general(v, do2, last, preferred_element_type=F32)
            return k, scores, dprobs

        def back(unit, ready):
            h, k_in = unit
            q2, do2, delta, lse = queries[h]
            k, scores, dprobs = ready
            probs = jnp.exp2(scores * (SCALE * LOG2E) - lse)
            if masked:
                key_at = lax.broadcasted_iota(jnp.int32, probs.shape, 0) + k_in * KEY_TILE
                lane = lax.broadcasted_iota(jnp.int32, probs.shape, 1) % QUERY_TILE
                query_at = q_start(q_in) + lane % tokens + (lane // tokens) * (CORES * tokens)
                ahead = key_at - query_at
                allowed = jnp.where(code == 2, ahead, 1 - ahead) <= 0
                probs = jnp.where(allowed, probs, 0.0)
            dscores = (probs * (dprobs - delta) * SCALE).astype(BF16)
            dv = jnp.dot(probs.astype(BF16), do2, preferred_element_type=F32)
            dk = jnp.dot(dscores, q2, preferred_element_type=F32)
            for n, (c, chip) in enumerate(k_place(k_in)):
                rows = slice(n * tokens, (n + 1) * tokens)
                at = h * tokens
                dkv_ref[c, chip, at : at + tokens, :] += dk[rows]
                at += plan.kv_heads * tokens
                dkv_ref[c, chip, at : at + tokens, :] += dv[rows]
            return jnp.dot(k.T, dscores, preferred_element_type=F32)

        ready = front(units[0])
        for n, unit in enumerate(units):
            following = front(units[n + 1]) if n + 1 < len(units) else None
            dq_ref[level, tile, unit[0]] += back(unit, ready)
            ready = following

    def step(index, carry):
        q_in = index % plan.q_tiles
        rest = index // plan.q_tiles
        key_block = rest % fold
        rest = rest // fold
        query_block = rest % fold
        level = rest // fold
        code = code_ref[level, query_block, key_block]
        q_first, q_last = q_start(q_in), q_end(q_in)
        every = tuple(range(plan.k_tiles))
        below = (q_last < (plan.k_tiles - 1) * KEY_TILE) & (code == 2)
        above = (q_first >= KEY_TILE - 1) & (code == 3)

        @pl.when(code == 1)
        def _():
            row(level, query_block, q_in, key_block, every, code, False)

        @pl.when(below | above)
        def _():
            row(level, query_block, q_in, key_block, (jnp.where(below, 0, plan.k_tiles - 1),), code, True)

        @pl.when((code >= 2) & jnp.logical_not(below | above))
        def _():
            row(level, query_block, q_in, key_block, every, code, True)

        return carry

    lax.fori_loop(0, levels * fold * fold * plan.q_tiles, step, 0)
    for level in range(levels):
        dq_outs[level][...] = dq_ref[level].astype(dq_outs[level].dtype)
    keep[...] = dkv_ref[core]
    give[...] = dkv_ref[1 - core].astype(BF16)


def finish_kernel(plan, has_far, me_ref, dq_ref, *refs):
    refs = list(refs)
    far_ref = refs.pop(0) if has_far else None
    pieces, rows_ref = refs[:-1], refs[-1]
    tokens = plan.tokens
    q_per = QUERY_TILE // tokens
    for tile in range(dq_ref.shape[0]):
        for h in range(plan.kv_heads):
            total = dq_ref[tile, h]
            if has_far:
                total = total + far_ref[tile, h].astype(F32)
            turned = total.T.astype(BF16)
            for g in range(GROUP):
                for n in range(q_per):
                    at = (h * GROUP + g) * tokens
                    source = g * QUERY_TILE + n * tokens
                    rows_ref[tile * q_per + n, at : at + tokens, :] = turned[source : source + tokens]
    for mask, out in enumerate(pieces):
        out[...] = rows_ref[me_ref[0] ^ mask]


def unpack_kernel(plan, levels, me_ref, *refs):
    refs = list(refs)
    dq_pieces = [refs.pop(0) for _ in range(plan.chips)]
    kv_pieces = [[refs.pop(0) for _ in range(plan.chips)] for _ in range(levels)]
    dq_ref, dk_ref, dv_ref = refs
    tokens = plan.tokens
    for mask in range(plan.chips):
        kv_head = plan.first_kv_head(me_ref[0] ^ mask)
        for g in range(plan.q_heads):
            columns(dq_ref, kv_head * GROUP + g)[...] = dq_pieces[mask][g * tokens : (g + 1) * tokens, :]
        total = kv_pieces[0][mask][...]
        if levels > 1:
            total = total.astype(F32)
            for level in range(1, levels):
                total = total + kv_pieces[level][mask][...].astype(F32)
            total = total.astype(BF16)
        for h in range(plan.kv_heads):
            columns(dk_ref, kv_head + h)[...] = total[h * tokens : (h + 1) * tokens]
            at = (plan.kv_heads + h) * tokens
            columns(dv_ref, kv_head + h)[...] = total[at : at + tokens]


def exchange(pieces):
    chips = len(pieces)
    return [pieces[0]] + [
        lax.ppermute(pieces[mask], CROSS, [(i, i ^ mask) for i in range(chips)])
        for mask in range(1, chips)
    ]


def deliver(pieces, planes, level):
    chips = len(pieces)
    return [
        lax.ppermute(
            pieces[mask],
            ("z",) + CROSS,
            [(p * chips + i, (p - level) * chips + (i ^ mask)) for p in range(level, planes) for i in range(chips)],
        )
        for mask in range(chips)
    ]


def swap(value):
    return lax.ppermute(value, "core", [(0, 1), (1, 0)])


def along(value, planes, steps):
    pairs = [(i, i + steps) for i in range(planes) if 0 <= i + steps < planes]
    return lax.ppermute(value, "z", pairs)


def query_levels(level, reach):
    return [d - level for d in (2 * level - 1, 2 * level) if 0 <= d <= reach]


def plane_logsum(logsum, plan, y, core):
    other = swap(logsum)
    both = jnp.where(core == 0, jnp.concatenate([logsum, other]), jnp.concatenate([other, logsum]))
    rows = both.reshape(plan.fold, plan.q_heads, plan.block)
    parts = []
    for mask in range(plan.fold):
        part = lax.dynamic_index_in_dim(rows, y ^ mask, 0, keepdims=False)
        if mask:
            part = lax.ppermute(part, "y", [(i, i ^ mask) for i in range(plan.fold)])
        parts.append(part)
    lse = jnp.stack(parts)
    if plan.tokens == LANES:
        return lse
    lse = lse.reshape(plan.fold, plan.q_heads, plan.n_x * CORES, plan.tokens).transpose(0, 2, 1, 3)
    return jnp.pad(lse, ((0, 0), (0, 0), (0, 0), (0, LANES - plan.tokens)))


def body(queries, output_gradient, outputs, key_vectors, values, logsum, pair_list):
    planes, fold, n_x = (lax.axis_size(a) for a in ("z", "y", "x"))
    plan = Plan(fold, n_x, queries.shape[0])
    chips = plan.chips
    reach = -(-(WIN - 1) // fold)
    z, y, x, core = (lax.axis_index(a) for a in ("z", "y", "x", "core"))
    me = jnp.stack([y * n_x + x, core]).astype(jnp.int32)

    def like(rows):
        return jax.ShapeDtypeStruct((rows, LANES), BF16)

    def stacked(rows, dtype=BF16):
        return jax.ShapeDtypeStruct((chips, rows, LANES), dtype)

    raw = [queries]
    for _ in range(1, reach // 2 + 1):
        raw.append(along(raw[-1], planes, -1))

    lse = plane_logsum(logsum, plan, y, core)
    arrays = (output_gradient, outputs, key_vectors, values, queries)
    packed = call(
        functools.partial(pack_kernel, plan),
        [like(plan.q_rows + plan.kv_rows + plan.aux_sent)] * chips + [like(plan.q_rows)] * chips,
        [SCALARS] + [pl.BlockSpec(memory_space=pltpu.HBM)] * len(arrays),
        scratch=[pltpu.VMEM(a.shape, a.dtype) for a in arrays]
        + [pltpu.VMEM((LANES, LANES), F32), pltpu.SemaphoreType.DMA((len(arrays), 2))],
    )(me, *arrays)
    pieces, q_pieces = packed[:chips], packed[chips:]
    do_own, kv_own = call(
        functools.partial(assemble_kernel, plan),
        [stacked(plan.q_rows + plan.aux), stacked(plan.kv_rows)],
        [SCALARS] + [WHOLE] * (chips + 1),
    )(me, lse, *exchange(pieces))

    up = [kv_own]
    for _ in range(1, (reach + 1) // 2 + 1):
        up.append(along(up[-1], planes, 1))
    far_do = [do_own]
    for _ in range(1, reach // 2 + 1):
        far_do.append(along(far_do[-1], planes, -1))
    all_q = [exchange(q_pieces)]
    for n in range(1, len(raw)):
        far_pieces = call(
            functools.partial(pack_q_kernel, plan), [like(plan.q_rows)] * chips, [SCALARS, WHOLE]
        )(me, raw[n])
        all_q.append(exchange(far_pieces))
    up = [(kv, swap(kv)) for kv in up]

    grad_q = [None] * len(all_q)
    grad_kv = []
    dq_shape = (fold * plan.q_tiles, plan.kv_heads, HEAD_SIZE, GROUP * QUERY_TILE)
    inside = jnp.arange(fold, dtype=jnp.int32)
    for i, (mine, sibling) in enumerate(up):
        levels = query_levels(i, reach)
        query_blocks = (z + jnp.array(levels, jnp.int32)[:, None]) * fold + inside
        key_blocks = (z - i) * fold + inside
        row = pair_list[:, :, None, None, None]
        hit = (row[:, 0] == query_blocks[:, :, None]) & (row[:, 1] == key_blocks)
        codes = jnp.sum(jnp.where(hit, row[:, 2] + 1, 0), axis=0).astype(jnp.int32)
        has_dq = tuple(grad_q[j] is not None for j in levels)
        over = [j and j not in query_levels(i + 1, reach) for j in levels]
        *parts, keep, give = call(
            functools.partial(role_kernel, plan, has_dq),
            [jax.ShapeDtypeStruct(dq_shape, BF16 if done else F32) for done in over]
            + [stacked(plan.kv_rows, F32), stacked(plan.kv_rows)],
            [SCALARS] * 2 + [WHOLE] * (2 + len(levels) * (chips + 1) + sum(has_dq)),
            flops=10 * len(levels) * fold * fold * plan.q_heads * plan.block * plan.block * HEAD_SIZE // CORES,
            scratch=[
                pltpu.VMEM((CORES, chips, plan.kv_rows, LANES), BF16),
                pltpu.VMEM((len(levels), chips, plan.q_rows, LANES), BF16),
                pltpu.VMEM((len(levels), chips, plan.q_rows + plan.aux, LANES), BF16),
                pltpu.VMEM((len(levels),) + dq_shape, F32),
                pltpu.VMEM((CORES, chips, plan.kv_rows, LANES), F32),
            ],
        )(
            me,
            codes,
            mine,
            sibling,
            *[piece for j in levels for piece in all_q[j]],
            *[far_do[j] for j in levels],
            *[grad_q[j] for j in levels if grad_q[j] is not None],
        )
        for j, part in zip(levels, parts):
            grad_q[j] = part
        merged = call(merge_kernel, [like(plan.kv_rows)] * chips, [SCALARS] + [WHOLE] * 2)(me, keep, swap(give))
        grad_kv.append(deliver(merged, planes, i) if i else exchange(merged))

    far_q = None
    for level in range(len(grad_q) - 1, 0, -1):
        part = grad_q[level]
        if far_q is not None:
            part = (part.astype(F32) + far_q.astype(F32)).astype(BF16)
        far_q = along(part, planes, 1)
    dq_pieces = call(
        functools.partial(finish_kernel, plan, far_q is not None),
        [like(plan.q_rows)] * chips,
        [SCALARS, WHOLE] + [WHOLE] * (far_q is not None),
        scratch=[pltpu.VMEM((chips, plan.q_rows, LANES), BF16)],
    )(me, grad_q[0], *([] if far_q is None else [far_q]))
    return tuple(
        call(
            functools.partial(unpack_kernel, plan, len(grad_kv)),
            [
                jax.ShapeDtypeStruct((plan.tokens, QUERY_HEADS * HEAD_SIZE), BF16),
                jax.ShapeDtypeStruct((plan.tokens, KEY_VALUE_HEADS * HEAD_SIZE), BF16),
                jax.ShapeDtypeStruct((plan.tokens, KEY_VALUE_HEADS * HEAD_SIZE), BF16),
            ],
            [SCALARS] + [WHOLE] * (chips * (1 + len(grad_kv))),
        )(me, *exchange(dq_pieces), *[piece for level in grad_kv for piece in level])
    )


def solution(mesh):
    n_seq, n_head = mesh.shape["seq"], mesh.shape["head"]
    fold = KEY_VALUE_HEADS // n_head
    assert n_head * fold == KEY_VALUE_HEADS and n_seq % fold == 0 and n_head % CORES == 0
    names = ("z", "y", "x", "core")
    planes = Mesh(mesh.devices.reshape(n_seq // fold, fold, n_head // CORES, CORES), names)
    rows = P(names, None)
    return jax.shard_map(
        body,
        mesh=planes,
        in_specs=(rows,) * 5 + (P(("x", "core"), ("z", "y")), P()),
        out_specs=(rows,) * 3,
        check_vma=False,
    )
```

time: 244 us -> 108 us (0.44)
  the two profiles are of different devices: /device:TPU:24 before, /device:TPU:0 now
where the time goes in v2:
time: 108 us; the launch traced here: 107 us
  waiting for transfers between devices  43.7 us (40%)
  starting transfers between devices  41.4 us (38%)
  Pallas kernels  14.8 us (14%)
  local copies, waits for them, and re-layouts  5.73 us (5%)
    ppermute x15, starting transfers between devices, exchange(): lax.ppermute(pieces[mask], CROSS, [(i, i ^ mask) for i in range(chips)])  17.8 us
    ppermute x4, starting transfers between devices, along(): return lax.ppermute(value, 'z', pairs)  15.7 us
    ppermute x4, waiting for transfers between devices, along(): return lax.ppermute(value, 'z', pairs)  14.4 us
    ppermute x4, waiting for transfers between devices, deliver(): lax.ppermute(pieces[mask], ('z',) + CROSS, [(p * chips + i, (p - level) *...  13.4 us
    ppermute x1, waiting for transfers between devices, plane_logsum(): part = lax.ppermute(part, 'y', [(i, i ^ mask) for i in range(plan.fold)])  10 us
    pallas_call x2, Pallas kernels, body(): call(functools.partial(role_kernel, plan, has_dq), [jax.ShapeDtypeStruct(...  7.46 us
    ppermute x15, waiting for transfers between devices, exchange(): lax.ppermute(pieces[mask], CROSS, [(i, i ^ mask) for i in range(chips)])  5.84 us
    unnamed x14, local copies, waits for them, and re-layouts  5.71 us
  transfers between devices with their start and end apart: 29, of which 11 were waited for; matrix products, arithmetic and copies ran while one was open for 1% of the time, Pallas kernels for 12%

profile of v2, /device:TPU:0, one launch (start us, length us, event | category | flops | bytes accessed | tf_op | source)
XLA Modules:
  0.0 107.2 jit_solution(1875885600297046171)
XLA Ops:
  0.6 0.6 collective-permute-start
  1.2 1.3 %collective-permute-start.10 = (bf16[128,2048]{1,0:T(8,128)(2,1)}, bf16[128,2048]{1,0:T(8,128)(2,1)S(1)}, u32[]{:S(2)}, u32[]{:S(2)}) collective-permute-start(bf16[128,2048]{1,0:T(8,128)(2,1)} %q_hbm.1), channel_id=1, source_target_pairs={{8,0},{16,8},{24,16},{9,1},{17,9},{25,17},{10,2},{18,10},{26,18},{... | collective-permute-start | bytes 1572872 | tf_op jit(solution)/shard_map/ppermute | solution.py:388
  2.6 1.0 copy-done
  3.6 1.0 copy-done.1
  4.6 1.0 copy-done.2
  5.7 0.9 copy-done.3
  6.6 0.9 copy-done.4
  7.6 2.3 %shard_map.112 = (bf16[1040,128]{1,0:T(8,128)(2,1)S(1)}, bf16[1040,128]{1,0:T(8,128)(2,1)S(1)}, bf16[1040,128]{1,0:T(8,128)(2,1)S(1)}, bf16[1040,128]{1,0:T(8,12...) custom-call(s32[2]{0:T(128)S(1)} %pad_add_fusion.me_ref, ...), custom_call_target="tpu_custom_call" | custom-call | bytes 4194304 | tf_op jit(solution)/shard_map/pallas_call | solution.py:432
  9.9 2.6 %collective-permute-start.2 = (bf16[1040,128]{1,0:T(8,128)(2,1)S(1)}, bf16[1040,128]{1,0:T(8,128)(2,1)S(1)}, u32[]{:S(2)}, u32[]{:S(2)}) collective-permute-start(bf16[1040,128]{1,0:T(8,128)(2,1)S(1)} %get-tuple-element.37), channel_id=1, source_target_pairs={{0,2},{2,0},{4,6},{6,4},{1,3},{3,1},{5,7},{7,5},{8,10},{10,8},{12,... | collective-permute-start | bytes 798728 | tf_op jit(solution)/shard_map/ppermute | solution.py:365
  12.5 1.5 %collective-permute-start.3 = (bf16[1040,128]{1,0:T(8,128)(2,1)S(1)}, bf16[1040,128]{1,0:T(8,128)(2,1)S(1)}, u32[]{:S(2)}, u32[]{:S(2)}) collective-permute-start(bf16[1040,128]{1,0:T(8,128)(2,1)S(1)} %get-tuple-element.38), channel_id=1, source_target_pairs={{0,4},{2,6},{4,0},{6,2},{1,5},{3,7},{5,1},{7,3},{8,12},{10,14},{12... | collective-permute-start | bytes 798728 | tf_op jit(solution)/shard_map/ppermute | solution.py:365
  14.1 0.7 copy-done.5
  14.8 2.0 %collective-permute-start.1 = (f32[4,512]{1,0:T(4,128)S(1)}, f32[4,512]{1,0:T(4,128)S(1)}, u32[]{:S(2)}, u32[]{:S(2)}) collective-permute-start(f32[4,512]{1,0:T(4,128)S(1)} %get-tuple-element.70), channel_id=1, source_target_pairs={{0,4},{4,0},{1,5},{5,1},{2,6},{6,2},{3,7},{7,3},{8,12},{12,8},{9,1... | collective-permute-start | bytes 24584 | tf_op jit(solution)/shard_map/ppermute | solution.py:403
  16.8 10.0 %collective-permute-done.1 = f32[4,512]{1,0:T(4,128)S(1)} collective-permute-done((f32[4,512]{1,0:T(4,128)S(1)}, f32[4,512]{1,0:T(4,128)S(1)}, u32[]{:S(2)}, u32[]{:S(2)}) %collective-permute-start.1) | collective-permute-done | bytes 8224 | tf_op jit(solution)/shard_map/ppermute | solution.py:403
  26.9 0.6 shard_map.113
  27.5 4.3 %collective-permute-start.5 = (bf16[4,512,128]{2,1,0:T(8,128)(2,1)S(1)}, bf16[4,512,128]{2,1,0:T(8,128)(2,1)S(1)}, u32[]{:S(2)}, u32[]{:S(2)}) collective-permute-start(bf16[4,512,128]{2,1,0:T(8,128)(2,1)S(1)} %get-tuple-element.40.mine_ref), channel_id=1, source_target_pairs={{0,8},{8,16},{16,24},{1,9},{9,17},{17,25},{2,10},{10,18},{18,26},{... | collective-permute-start | bytes 1572872 | tf_op jit(solution)/shard_map/ppermute | solution.py:388
  32.1 1.3 %collective-permute-start.14 = (bf16[4,544,128]{2,1,0:T(8,128)(2,1)S(1)}, bf16[4,544,128]{2,1,0:T(8,128)(2,1)S(1)}, u32[]{:S(2)}, u32[]{:S(2)}) collective-permute-start(bf16[4,544,128]{2,1,0:T(8,128)(2,1)S(1)} %get-tuple-element.49.refs_4_.refs_8_), channel_id=1, source_target_pairs={{8,0},{16,8},{24,16},{9,1},{17,9},{25,17},{10,2},{18,10},{26,18},{... | collective-permute-start | bytes 1671176 | tf_op jit(solution)/shard_map/ppermute | solution.py:388
  33.4 8.7 %collective-permute-done.5.mine_ref = bf16[4,512,128]{2,1,0:T(8,128)(2,1)S(1)} collective-permute-done((bf16[4,512,128]{2,1,0:T(8,128)(2,1)S(1)}, bf16[4,512,128]{2,1,0:T(8,128)(2,1)S(1)}, u32[]{:S(2)}, u32[]{:S(2)}) %collective-permute-start.5) | collective-permute-done | bytes 524320 | tf_op jit(solution)/shard_map/ppermute | solution.py:388
  42.1 1.7 %collective-permute-start.8 = (bf16[512,128]{1,0:T(8,128)(2,1)S(1)}, bf16[512,128]{1,0:T(8,128)(2,1)S(1)}, u32[]{:S(2)}, u32[]{:S(2)}) collective-permute-start(bf16[512,128]{1,0:T(8,128)(2,1)S(1)} %get-tuple-element.43), channel_id=1, source_target_pairs={{0,4},{2,6},{4,0},{6,2},{1,5},{3,7},{5,1},{7,3},{8,12},{10,14},{12... | collective-permute-start | bytes 393224 | tf_op jit(solution)/shard_map/ppermute | solution.py:365
  43.9 1.3 %collective-permute-start.9 = (bf16[512,128]{1,0:T(8,128)(2,1)S(1)}, bf16[512,128]{1,0:T(8,128)(2,1)S(1)}, u32[]{:S(2)}, u32[]{:S(2)}) collective-permute-start(bf16[512,128]{1,0:T(8,128)(2,1)S(1)} %get-tuple-element.44), channel_id=1, source_target_pairs={{0,6},{2,4},{4,2},{6,0},{1,7},{3,5},{5,3},{7,1},{8,14},{10,12},{12... | collective-permute-start | bytes 393224 | tf_op jit(solution)/shard_map/ppermute | solution.py:365
  45.3 0.2 fusion.code_ref
  45.4 0.7 shard_map.114
  46.1 4.8 %collective-permute-done.8.refs_2_ = bf16[512,128]{1,0:T(8,128)(2,1)S(1)} collective-permute-done((bf16[512,128]{1,0:T(8,128)(2,1)S(1)}, bf16[512,128]{1,0:T(8,128)(2,1)S(1)}, u32[]{:S(2)}, u32[]{:S(2)}) %collective-permute-start.8) | collective-permute-done | bytes 131104 | tf_op jit(solution)/shard_map/ppermute | solution.py:365
  50.9 1.7 %collective-permute-start.11 = (bf16[512,128]{1,0:T(8,128)(2,1)S(1)}, bf16[512,128]{1,0:T(8,128)(2,1)S(1)}, u32[]{:S(2)}, u32[]{:S(2)}) collective-permute-start(bf16[512,128]{1,0:T(8,128)(2,1)S(1)} %get-tuple-element.46), channel_id=1, source_target_pairs={{0,2},{2,0},{4,6},{6,4},{1,3},{3,1},{5,7},{7,5},{8,10},{10,8},{12,... | collective-permute-start | bytes 393224 | tf_op jit(solution)/shard_map/ppermute | solution.py:365
  52.6 1.7 %collective-permute-start.12 = (bf16[512,128]{1,0:T(8,128)(2,1)S(1)}, bf16[512,128]{1,0:T(8,128)(2,1)S(1)}, u32[]{:S(2)}, u32[]{:S(2)}) collective-permute-start(bf16[512,128]{1,0:T(8,128)(2,1)S(1)} %get-tuple-element.47), channel_id=1, source_target_pairs={{0,4},{2,6},{4,0},{6,2},{1,5},{3,7},{5,1},{7,3},{8,12},{10,14},{12... | collective-permute-start | bytes 393224 | tf_op jit(solution)/shard_map/ppermute | solution.py:365
  54.4 5.4 %shard_map.115 = (f32[4,2,128,256]{3,2,1,0:T(8,128)S(1)}, f32[4,512,128]{2,1,0:T(8,128)S(1)}, bf16[4,512,128]{2,1,0:T(8,128)(2,1)S(1)}) custom-call(s32[2]{0:T(128)S(1)} %pad_add_fusion.me_ref, s32[1,2,2]{2,1,0:T(2,128)S(1)} %bitcast.13, bf16[4,512,128]{2,1,0:T(8,128)(2,1)S(1)} %get-tuple-element.40.mine_ref, ...), custom_call_target="tpu_custom_call" | custom-call | flops 2684354560 | bytes 4194304 | tf_op jit(solution)/shard_map/pallas_call | solution.py:473
  59.9 0.5 collective-permute-done.12.refs_6_
  60.4 2.0 %shard_map.116 = (f32[4,2,128,256]{3,2,1,0:T(8,128)S(1)}, bf16[4,2,128,256]{3,2,1,0:T(8,128)(2,1)S(1)}, f32[4,512,128]{2,1,0:T(8,128)S(1)}, bf16[4,512,128]{2,1,0:T(8,128)(2,1)S(1)}) custom-call(s32[2]{0:T(128)S(1)} %pad_add_fusion.me_ref, s32[2,2,2]{2,1,0:T(2,128)S(1)} %fusion.code_ref, bf16[4,512,128]{2,1,0:T(8,128)(2,1)S(1)} %collective-permute-done.5.mine_ref, ...), custom_call_target="tpu_custom_call" | custom-call | flops 5368709120 | bytes 4194304 | tf_op jit(solution)/shard_map/pallas_call | solution.py:473
  62.4 8.9 %collective-permute-start.16 = (bf16[4,2,128,256]{3,2,1,0:T(8,128)(2,1)S(1)}, bf16[4,2,128,256]{3,2,1,0:T(8,128)(2,1)S(1)}, u32[]{:S(2)}, u32[]{:S(2)}) collective-permute-start(bf16[4,2,128,256]{3,2,1,0:T(8,128)(2,1)S(1)} %get-tuple-element.52), channel_id=1, source_target_pairs={{0,8},{8,16},{16,24},{1,9},{9,17},{17,25},{2,10},{10,18},{18,26},{... | collective-permute-start | bytes 1572872 | tf_op jit(solution)/shard_map/ppermute | solution.py:388
  71.4 0.6 shard_map.118
  72.0 1.3 %collective-permute-start.21 = (bf16[512,128]{1,0:T(8,128)(2,1)S(1)}, bf16[512,128]{1,0:T(8,128)(2,1)S(1)}, u32[]{:S(2)}, u32[]{:S(2)}) collective-permute-start(bf16[512,128]{1,0:T(8,128)(2,1)S(1)} %get-tuple-element.60), channel_id=1, source_target_pairs={{0,2},{2,0},{4,6},{6,4},{1,3},{3,1},{5,7},{7,5},{8,10},{10,8},{12,... | collective-permute-start | bytes 393224 | tf_op jit(solution)/shard_map/ppermute | solution.py:365
  73.3 0.8 collective-permute-start.22
  74.1 1.5 %collective-permute-start.23 = (bf16[512,128]{1,0:T(8,128)(2,1)S(1)}, bf16[512,128]{1,0:T(8,128)(2,1)S(1)}, u32[]{:S(2)}, u32[]{:S(2)}) collective-permute-start(bf16[512,128]{1,0:T(8,128)(2,1)S(1)} %get-tuple-element.62), channel_id=1, source_target_pairs={{0,6},{2,4},{4,2},{6,0},{1,7},{3,5},{5,3},{7,1},{8,14},{10,12},{12... | collective-permute-start | bytes 393224 | tf_op jit(solution)/shard_map/ppermute | solution.py:365
  75.6 5.7 %collective-permute-done.16.refs_0_ = bf16[4,2,128,256]{3,2,1,0:T(8,128)(2,1)S(1)} collective-permute-done((bf16[4,2,128,256]{3,2,1,0:T(8,128)(2,1)S(1)}, bf16[4,2,128,256]{3,2,1,0:T(8,128)(2,1)S(1)}, u32[]{:S(2)}, u32[]{:S(2)}) %collective-permute-start.16) | collective-permute-done | bytes 524320 | tf_op jit(solution)/shard_map/ppermute | solution.py:388
  81.3 0.8 shard_map.117
  82.1 1.7 %collective-permute-start.17 = (bf16[512,128]{1,0:T(8,128)(2,1)S(1)}, bf16[512,128]{1,0:T(8,128)(2,1)S(1)}, u32[]{:S(2)}, u32[]{:S(2)}) collective-permute-start(bf16[512,128]{1,0:T(8,128)(2,1)S(1)} %get-tuple-element.54), channel_id=1, source_target_pairs={{0,2},{2,0},{4,6},{6,4},{1,3},{3,1},{5,7},{7,5},{8,10},{10,8},{12,... | collective-permute-start | bytes 393224 | tf_op jit(solution)/shard_map/ppermute | solution.py:365
  83.8 1.7 %collective-permute-start.18 = (bf16[512,128]{1,0:T(8,128)(2,1)S(1)}, bf16[512,128]{1,0:T(8,128)(2,1)S(1)}, u32[]{:S(2)}, u32[]{:S(2)}) collective-permute-start(bf16[512,128]{1,0:T(8,128)(2,1)S(1)} %get-tuple-element.55), channel_id=1, source_target_pairs={{0,4},{2,6},{4,0},{6,2},{1,5},{3,7},{5,1},{7,3},{8,12},{10,14},{12... | collective-permute-start | bytes 393224 | tf_op jit(solution)/shard_map/ppermute | solution.py:365
  85.6 0.6 shard_map.119
  86.4 1.3 %collective-permute-start.25 = (bf16[512,128]{1,0:T(8,128)(2,1)S(1)}, bf16[512,128]{1,0:T(8,128)(2,1)S(1)}, u32[]{:S(2)}, u32[]{:S(2)}) collective-permute-start(bf16[512,128]{1,0:T(8,128)(2,1)S(1)} %get-tuple-element.65), channel_id=1, source_target_pairs={{8,0},{10,2},{12,4},{14,6},{16,8},{18,10},{20,12},{22,14},{24,16},... | collective-permute-start | bytes 393224 | tf_op jit(solution)/shard_map/ppermute | solution.py:373
  87.7 1.3 %collective-permute-start.26 = (bf16[512,128]{1,0:T(8,128)(2,1)S(1)}, bf16[512,128]{1,0:T(8,128)(2,1)S(1)}, u32[]{:S(2)}, u32[]{:S(2)}) collective-permute-start(bf16[512,128]{1,0:T(8,128)(2,1)S(1)} %get-tuple-element.66), channel_id=1, source_target_pairs={{8,2},{10,0},{12,6},{14,4},{16,10},{18,8},{20,14},{22,12},{24,18},... | collective-permute-start | bytes 393224 | tf_op jit(solution)/shard_map/ppermute | solution.py:373
  89.0 1.3 %collective-permute-start.27 = (bf16[512,128]{1,0:T(8,128)(2,1)S(1)}, bf16[512,128]{1,0:T(8,128)(2,1)S(1)}, u32[]{:S(2)}, u32[]{:S(2)}) collective-permute-start(bf16[512,128]{1,0:T(8,128)(2,1)S(1)} %get-tuple-element.67), channel_id=1, source_target_pairs={{8,4},{10,6},{12,0},{14,2},{16,12},{18,14},{20,8},{22,10},{24,20},... | collective-permute-start | bytes 393224 | tf_op jit(solution)/shard_map/ppermute | solution.py:373
  90.3 0.3 collective-permute-done.18.refs_2_
  90.6 1.3 %collective-permute-start.28 = (bf16[512,128]{1,0:T(8,128)(2,1)S(1)}, bf16[512,128]{1,0:T(8,128)(2,1)S(1)}, u32[]{:S(2)}, u32[]{:S(2)}) collective-permute-start(bf16[512,128]{1,0:T(8,128)(2,1)S(1)} %get-tuple-element.68), channel_id=1, source_target_pairs={{8,6},{10,4},{12,2},{14,0},{16,14},{18,12},{20,10},{22,8},{24,22},... | collective-permute-start | bytes 393224 | tf_op jit(solution)/shard_map/ppermute | solution.py:373
  91.9 0.3 collective-permute-done.19.refs_3_
  92.2 4.7 %collective-permute-done.25.refs_8_ = bf16[512,128]{1,0:T(8,128)(2,1)S(1)} collective-permute-done((bf16[512,128]{1,0:T(8,128)(2,1)S(1)}, bf16[512,128]{1,0:T(8,128)(2,1)S(1)}, u32[]{:S(2)}, u32[]{:S(2)}) %collective-permute-start.25) | collective-permute-done | bytes 131104 | tf_op jit(solution)/shard_map/ppermute | solution.py:373
  96.8 3.7 %collective-permute-done.26.refs_9_ = bf16[512,128]{1,0:T(8,128)(2,1)S(1)} collective-permute-done((bf16[512,128]{1,0:T(8,128)(2,1)S(1)}, bf16[512,128]{1,0:T(8,128)(2,1)S(1)}, u32[]{:S(2)}, u32[]{:S(2)}) %collective-permute-start.26) | collective-permute-done | bytes 131104 | tf_op jit(solution)/shard_map/ppermute | solution.py:373
  100.5 2.5 %collective-permute-done.27.refs_10_ = bf16[512,128]{1,0:T(8,128)(2,1)S(1)} collective-permute-done((bf16[512,128]{1,0:T(8,128)(2,1)S(1)}, bf16[512,128]{1,0:T(8,128)(2,1)S(1)}, u32[]{:S(2)}, u32[]{:S(2)}) %collective-permute-start.27) | collective-permute-done | bytes 131104 | tf_op jit(solution)/shard_map/ppermute | solution.py:373
  103.1 2.4 %collective-permute-done.28.refs_11_ = bf16[512,128]{1,0:T(8,128)(2,1)S(1)} collective-permute-done((bf16[512,128]{1,0:T(8,128)(2,1)S(1)}, bf16[512,128]{1,0:T(8,128)(2,1)S(1)}, u32[]{:S(2)}, u32[]{:S(2)}) %collective-permute-start.28) | collective-permute-done | bytes 131104 | tf_op jit(solution)/shard_map/ppermute | solution.py:373
  105.5 1.7 %shard_map.120 = (bf16[128,2048]{1,0:T(8,128)(2,1)}, bf16[128,1024]{1,0:T(8,128)(2,1)}, bf16[128,1024]{1,0:T(8,128)(2,1)}) custom-call(s32[2]{0:T(128)S(1)} %pad_add_fusion.me_ref, bf16[512,128]{1,0:T(8,128)(2,1)S(1)} %get-tuple-element.53.refs_0_, bf16[512,128]{1,0:T(8,128)(2,1)S(1)} %collective-permute-done.17.refs_1_, ...), custom_call_target="tpu_custom_call" | custom-call | bytes 4194304 | tf_op jit(solution)/shard_map/pallas_call | solution.py:513
  (46 shorter events, 1.0 us)
Async XLA Ops:
  0.6 13.4 %collective-permute-start = (f32[4,512]{1,0:T(4,128)}, f32[4,512]{1,0:T(4,128)S(1)}, u32[]{:S(2)}, u32[]{:S(2)}) collective-permute-start(f32[4,512]{1,0:T(4,128)} %param.14), channel_id=1, source_target_pairs={{0,1},{1,0},{2,3},{3,2},{4,5},{5,4},{6,7},{7,6},{8,9},{9,8},{10,11... | collective-permute-start | bytes 24584 | tf_op jit(solution)/shard_map/ppermute | solution.py:383
  1.2 42.7 %collective-permute-start.10 = (bf16[128,2048]{1,0:T(8,128)(2,1)}, bf16[128,2048]{1,0:T(8,128)(2,1)S(1)}, u32[]{:S(2)}, u32[]{:S(2)}) collective-permute-start(bf16[128,2048]{1,0:T(8,128)(2,1)} %q_hbm.1), channel_id=1, source_target_pairs={{8,0},{16,8},{24,16},{9,1},{17,9},{25,17},{10,2},{18,10},{26,18},{... | collective-permute-start | bytes 1572872 | tf_op jit(solution)/shard_map/ppermute | solution.py:388
  2.6 1.0 copy-start
  3.6 1.0 copy-start.1
  4.6 1.0 copy-start.2
  5.7 0.9 copy-start.3
  6.6 0.9 copy-start.4
  9.9 17.0 %collective-permute-start.2 = (bf16[1040,128]{1,0:T(8,128)(2,1)S(1)}, bf16[1040,128]{1,0:T(8,128)(2,1)S(1)}, u32[]{:S(2)}, u32[]{:S(2)}) collective-permute-start(bf16[1040,128]{1,0:T(8,128)(2,1)S(1)} %get-tuple-element.37), channel_id=1, source_target_pairs={{0,2},{2,0},{4,6},{6,4},{1,3},{3,1},{5,7},{7,5},{8,10},{10,8},{12,... | collective-permute-start | bytes 798728 | tf_op jit(solution)/shard_map/ppermute | solution.py:365
  12.5 1.6 %copy-start.6 = (s32[20,3]{0,1:T(4,128)S(1)}, s32[20,3]{0,1:T(4,128)}, u32[]{:S(2)}) copy-start(s32[20,3]{0,1:T(4,128)} %param.15) | copy-start | bytes 724
  12.5 14.4 %collective-permute-start.3 = (bf16[1040,128]{1,0:T(8,128)(2,1)S(1)}, bf16[1040,128]{1,0:T(8,128)(2,1)S(1)}, u32[]{:S(2)}, u32[]{:S(2)}) collective-permute-start(bf16[1040,128]{1,0:T(8,128)(2,1)S(1)} %get-tuple-element.38), channel_id=1, source_target_pairs={{0,4},{2,6},{4,0},{6,2},{1,5},{3,7},{5,1},{7,3},{8,12},{10,14},{12... | collective-permute-start | bytes 798728 | tf_op jit(solution)/shard_map/ppermute | solution.py:365
  14.0 12.9 %collective-permute-start.4 = (bf16[1040,128]{1,0:T(8,128)(2,1)S(1)}, bf16[1040,128]{1,0:T(8,128)(2,1)S(1)}, u32[]{:S(2)}, u32[]{:S(2)}) collective-permute-start(bf16[1040,128]{1,0:T(8,128)(2,1)S(1)} %get-tuple-element.39), channel_id=1, source_target_pairs={{0,6},{2,4},{4,2},{6,0},{1,7},{3,5},{5,3},{7,1},{8,14},{10,12},{12... | collective-permute-start | bytes 798728 | tf_op jit(solution)/shard_map/ppermute | solution.py:365
  14.0 0.7 copy-start.5
  14.8 12.1 %collective-permute-start.1 = (f32[4,512]{1,0:T(4,128)S(1)}, f32[4,512]{1,0:T(4,128)S(1)}, u32[]{:S(2)}, u32[]{:S(2)}) collective-permute-start(f32[4,512]{1,0:T(4,128)S(1)} %get-tuple-element.70), channel_id=1, source_target_pairs={{0,4},{4,0},{1,5},{5,1},{2,6},{6,2},{3,7},{7,3},{8,12},{12,8},{9,1... | collective-permute-start | bytes 24584 | tf_op jit(solution)/shard_map/ppermute | solution.py:403
  26.9 15.3 %collective-permute-start.7 = (bf16[512,128]{1,0:T(8,128)(2,1)S(1)}, bf16[512,128]{1,0:T(8,128)(2,1)S(1)}, u32[]{:S(2)}, u32[]{:S(2)}) collective-permute-start(bf16[512,128]{1,0:T(8,128)(2,1)S(1)} %get-tuple-element.42), channel_id=1, source_target_pairs={{0,2},{2,0},{4,6},{6,4},{1,3},{3,1},{5,7},{7,5},{8,10},{10,8},{12,... | collective-permute-start | bytes 393224 | tf_op jit(solution)/shard_map/ppermute | solution.py:365
  27.5 14.5 %collective-permute-start.5 = (bf16[4,512,128]{2,1,0:T(8,128)(2,1)S(1)}, bf16[4,512,128]{2,1,0:T(8,128)(2,1)S(1)}, u32[]{:S(2)}, u32[]{:S(2)}) collective-permute-start(bf16[4,512,128]{2,1,0:T(8,128)(2,1)S(1)} %get-tuple-element.40.mine_ref), channel_id=1, source_target_pairs={{0,8},{8,16},{16,24},{1,9},{9,17},{17,25},{2,10},{10,18},{18,26},{... | collective-permute-start | bytes 1572872 | tf_op jit(solution)/shard_map/ppermute | solution.py:388
  31.9 22.4 %collective-permute-start.15 = (bf16[4,512,128]{2,1,0:T(8,128)(2,1)S(1)}, bf16[4,512,128]{2,1,0:T(8,128)(2,1)S(1)}, u32[]{:S(2)}, u32[]{:S(2)}) collective-permute-start(bf16[4,512,128]{2,1,0:T(8,128)(2,1)S(1)} %get-tuple-element.40.mine_ref), channel_id=1, source_target_pairs={{0,1},{1,0},{2,3},{3,2},{4,5},{5,4},{6,7},{7,6},{8,9},{9,8},{10,11... | collective-permute-start | bytes 1572872 | tf_op jit(solution)/shard_map/ppermute | solution.py:383
  32.1 28.3 %collective-permute-start.14 = (bf16[4,544,128]{2,1,0:T(8,128)(2,1)S(1)}, bf16[4,544,128]{2,1,0:T(8,128)(2,1)S(1)}, u32[]{:S(2)}, u32[]{:S(2)}) collective-permute-start(bf16[4,544,128]{2,1,0:T(8,128)(2,1)S(1)} %get-tuple-element.49.refs_4_.refs_8_), channel_id=1, source_target_pairs={{8,0},{16,8},{24,16},{9,1},{17,9},{25,17},{10,2},{18,10},{26,18},{... | collective-permute-start | bytes 1671176 | tf_op jit(solution)/shard_map/ppermute | solution.py:388
  42.1 18.3 %collective-permute-start.6 = (bf16[4,512,128]{2,1,0:T(8,128)(2,1)S(1)}, bf16[4,512,128]{2,1,0:T(8,128)(2,1)S(1)}, u32[]{:S(2)}, u32[]{:S(2)}) collective-permute-start(bf16[4,512,128]{2,1,0:T(8,128)(2,1)S(1)} %collective-permute-done.5.mine_ref), channel_id=1, source_target_pairs={{0,1},{1,0},{2,3},{3,2},{4,5},{5,4},{6,7},{7,6},{8,9},{9,8},{10,11... | collective-permute-start | bytes 1572872 | tf_op jit(solution)/shard_map/ppermute | solution.py:383
  42.1 8.8 %collective-permute-start.8 = (bf16[512,128]{1,0:T(8,128)(2,1)S(1)}, bf16[512,128]{1,0:T(8,128)(2,1)S(1)}, u32[]{:S(2)}, u32[]{:S(2)}) collective-permute-start(bf16[512,128]{1,0:T(8,128)(2,1)S(1)} %get-tuple-element.43), channel_id=1, source_target_pairs={{0,4},{2,6},{4,0},{6,2},{1,5},{3,7},{5,1},{7,3},{8,12},{10,14},{12... | collective-permute-start | bytes 393224 | tf_op jit(solution)/shard_map/ppermute | solution.py:365
  43.9 8.7 %collective-permute-start.9 = (bf16[512,128]{1,0:T(8,128)(2,1)S(1)}, bf16[512,128]{1,0:T(8,128)(2,1)S(1)}, u32[]{:S(2)}, u32[]{:S(2)}) collective-permute-start(bf16[512,128]{1,0:T(8,128)(2,1)S(1)} %get-tuple-element.44), channel_id=1, source_target_pairs={{0,6},{2,4},{4,2},{6,0},{1,7},{3,5},{5,3},{7,1},{8,14},{10,12},{12... | collective-permute-start | bytes 393224 | tf_op jit(solution)/shard_map/ppermute | solution.py:365
  50.9 8.9 %collective-permute-start.11 = (bf16[512,128]{1,0:T(8,128)(2,1)S(1)}, bf16[512,128]{1,0:T(8,128)(2,1)S(1)}, u32[]{:S(2)}, u32[]{:S(2)}) collective-permute-start(bf16[512,128]{1,0:T(8,128)(2,1)S(1)} %get-tuple-element.46), channel_id=1, source_target_pairs={{0,2},{2,0},{4,6},{6,4},{1,3},{3,1},{5,7},{7,5},{8,10},{10,8},{12,... | collective-permute-start | bytes 393224 | tf_op jit(solution)/shard_map/ppermute | solution.py:365
  52.6 7.8 %collective-permute-start.12 = (bf16[512,128]{1,0:T(8,128)(2,1)S(1)}, bf16[512,128]{1,0:T(8,128)(2,1)S(1)}, u32[]{:S(2)}, u32[]{:S(2)}) collective-permute-start(bf16[512,128]{1,0:T(8,128)(2,1)S(1)} %get-tuple-element.47), channel_id=1, source_target_pairs={{0,4},{2,6},{4,0},{6,2},{1,5},{3,7},{5,1},{7,3},{8,12},{10,14},{12... | collective-permute-start | bytes 393224 | tf_op jit(solution)/shard_map/ppermute | solution.py:365
  54.3 6.1 %collective-permute-start.13 = (bf16[512,128]{1,0:T(8,128)(2,1)S(1)}, bf16[512,128]{1,0:T(8,128)(2,1)S(1)}, u32[]{:S(2)}, u32[]{:S(2)}) collective-permute-start(bf16[512,128]{1,0:T(8,128)(2,1)S(1)} %get-tuple-element.48), channel_id=1, source_target_pairs={{0,6},{2,4},{4,2},{6,0},{1,7},{3,5},{5,3},{7,1},{8,14},{10,12},{12... | collective-permute-start | bytes 393224 | tf_op jit(solution)/shard_map/ppermute | solution.py:365
  59.8 11.5 %collective-permute-start.20 = (bf16[4,512,128]{2,1,0:T(8,128)(2,1)S(1)}, bf16[4,512,128]{2,1,0:T(8,128)(2,1)S(1)}, u32[]{:S(2)}, u32[]{:S(2)}) collective-permute-start(bf16[4,512,128]{2,1,0:T(8,128)(2,1)S(1)} %get-tuple-element.58), channel_id=1, source_target_pairs={{0,1},{1,0},{2,3},{3,2},{4,5},{5,4},{6,7},{7,6},{8,9},{9,8},{10,11... | collective-permute-start | bytes 1572872 | tf_op jit(solution)/shard_map/ppermute | solution.py:383
  62.4 18.9 %collective-permute-start.16 = (bf16[4,2,128,256]{3,2,1,0:T(8,128)(2,1)S(1)}, bf16[4,2,128,256]{3,2,1,0:T(8,128)(2,1)S(1)}, u32[]{:S(2)}, u32[]{:S(2)}) collective-permute-start(bf16[4,2,128,256]{3,2,1,0:T(8,128)(2,1)S(1)} %get-tuple-element.52), channel_id=1, source_target_pairs={{0,8},{8,16},{16,24},{1,9},{9,17},{17,25},{2,10},{10,18},{18,26},{... | collective-permute-start | bytes 1572872 | tf_op jit(solution)/shard_map/ppermute | solution.py:388
  71.3 12.6 %collective-permute-start.24 = (bf16[4,512,128]{2,1,0:T(8,128)(2,1)S(1)}, bf16[4,512,128]{2,1,0:T(8,128)(2,1)S(1)}, u32[]{:S(2)}, u32[]{:S(2)}) collective-permute-start(bf16[4,512,128]{2,1,0:T(8,128)(2,1)S(1)} %get-tuple-element.64), channel_id=1, source_target_pairs={{0,1},{1,0},{2,3},{3,2},{4,5},{5,4},{6,7},{7,6},{8,9},{9,8},{10,11... | collective-permute-start | bytes 1572872 | tf_op jit(solution)/shard_map/ppermute | solution.py:383
  72.0 14.2 %collective-permute-start.21 = (bf16[512,128]{1,0:T(8,128)(2,1)S(1)}, bf16[512,128]{1,0:T(8,128)(2,1)S(1)}, u32[]{:S(2)}, u32[]{:S(2)}) collective-permute-start(bf16[512,128]{1,0:T(8,128)(2,1)S(1)} %get-tuple-element.60), channel_id=1, source_target_pairs={{0,2},{2,0},{4,6},{6,4},{1,3},{3,1},{5,7},{7,5},{8,10},{10,8},{12,... | collective-permute-start | bytes 393224 | tf_op jit(solution)/shard_map/ppermute | solution.py:365
  73.3 13.1 %collective-permute-start.22 = (bf16[512,128]{1,0:T(8,128)(2,1)S(1)}, bf16[512,128]{1,0:T(8,128)(2,1)S(1)}, u32[]{:S(2)}, u32[]{:S(2)}) collective-permute-start(bf16[512,128]{1,0:T(8,128)(2,1)S(1)} %get-tuple-element.61), channel_id=1, source_target_pairs={{0,4},{2,6},{4,0},{6,2},{1,5},{3,7},{5,1},{7,3},{8,12},{10,14},{12... | collective-permute-start | bytes 393224 | tf_op jit(solution)/shard_map/ppermute | solution.py:365
  74.1 13.6 %collective-permute-start.23 = (bf16[512,128]{1,0:T(8,128)(2,1)S(1)}, bf16[512,128]{1,0:T(8,128)(2,1)S(1)}, u32[]{:S(2)}, u32[]{:S(2)}) collective-permute-start(bf16[512,128]{1,0:T(8,128)(2,1)S(1)} %get-tuple-element.62), channel_id=1, source_target_pairs={{0,6},{2,4},{4,2},{6,0},{1,7},{3,5},{5,3},{7,1},{8,14},{10,12},{12... | collective-permute-start | bytes 393224 | tf_op jit(solution)/shard_map/ppermute | solution.py:365
  82.1 6.9 %collective-permute-start.17 = (bf16[512,128]{1,0:T(8,128)(2,1)S(1)}, bf16[512,128]{1,0:T(8,128)(2,1)S(1)}, u32[]{:S(2)}, u32[]{:S(2)}) collective-permute-start(bf16[512,128]{1,0:T(8,128)(2,1)S(1)} %get-tuple-element.54), channel_id=1, source_target_pairs={{0,2},{2,0},{4,6},{6,4},{1,3},{3,1},{5,7},{7,5},{8,10},{10,8},{12,... | collective-permute-start | bytes 393224 | tf_op jit(solution)/shard_map/ppermute | solution.py:365
  83.8 6.7 %collective-permute-start.18 = (bf16[512,128]{1,0:T(8,128)(2,1)S(1)}, bf16[512,128]{1,0:T(8,128)(2,1)S(1)}, u32[]{:S(2)}, u32[]{:S(2)}) collective-permute-start(bf16[512,128]{1,0:T(8,128)(2,1)S(1)} %get-tuple-element.55), channel_id=1, source_target_pairs={{0,4},{2,6},{4,0},{6,2},{1,5},{3,7},{5,1},{7,3},{8,12},{10,14},{12... | collective-permute-start | bytes 393224 | tf_op jit(solution)/shard_map/ppermute | solution.py:365
  86.2 5.9 %collective-permute-start.19 = (bf16[512,128]{1,0:T(8,128)(2,1)S(1)}, bf16[512,128]{1,0:T(8,128)(2,1)S(1)}, u32[]{:S(2)}, u32[]{:S(2)}) collective-permute-start(bf16[512,128]{1,0:T(8,128)(2,1)S(1)} %get-tuple-element.56), channel_id=1, source_target_pairs={{0,6},{2,4},{4,2},{6,0},{1,7},{3,5},{5,3},{7,1},{8,14},{10,12},{12... | collective-permute-start | bytes 393224 | tf_op jit(solution)/shard_map/ppermute | solution.py:365
  86.4 10.5 %collective-permute-start.25 = (bf16[512,128]{1,0:T(8,128)(2,1)S(1)}, bf16[512,128]{1,0:T(8,128)(2,1)S(1)}, u32[]{:S(2)}, u32[]{:S(2)}) collective-permute-start(bf16[512,128]{1,0:T(8,128)(2,1)S(1)} %get-tuple-element.65), channel_id=1, source_target_pairs={{8,0},{10,2},{12,4},{14,6},{16,8},{18,10},{20,12},{22,14},{24,16},... | collective-permute-start | bytes 393224 | tf_op jit(solution)/shard_map/ppermute | solution.py:373
  87.7 12.9 %collective-permute-start.26 = (bf16[512,128]{1,0:T(8,128)(2,1)S(1)}, bf16[512,128]{1,0:T(8,128)(2,1)S(1)}, u32[]{:S(2)}, u32[]{:S(2)}) collective-permute-start(bf16[512,128]{1,0:T(8,128)(2,1)S(1)} %get-tuple-element.66), channel_id=1, source_target_pairs={{8,2},{10,0},{12,6},{14,4},{16,10},{18,8},{20,14},{22,12},{24,18},... | collective-permute-start | bytes 393224 | tf_op jit(solution)/shard_map/ppermute | solution.py:373
  89.0 14.1 %collective-permute-start.27 = (bf16[512,128]{1,0:T(8,128)(2,1)S(1)}, bf16[512,128]{1,0:T(8,128)(2,1)S(1)}, u32[]{:S(2)}, u32[]{:S(2)}) collective-permute-start(bf16[512,128]{1,0:T(8,128)(2,1)S(1)} %get-tuple-element.67), channel_id=1, source_target_pairs={{8,4},{10,6},{12,0},{14,2},{16,12},{18,14},{20,8},{22,10},{24,20},... | collective-permute-start | bytes 393224 | tf_op jit(solution)/shard_map/ppermute | solution.py:373
  90.6 15.0 %collective-permute-start.28 = (bf16[512,128]{1,0:T(8,128)(2,1)S(1)}, bf16[512,128]{1,0:T(8,128)(2,1)S(1)}, u32[]{:S(2)}, u32[]{:S(2)}) collective-permute-start(bf16[512,128]{1,0:T(8,128)(2,1)S(1)} %get-tuple-element.68), channel_id=1, source_target_pairs={{8,6},{10,4},{12,2},{14,0},{16,14},{18,12},{20,10},{22,8},{24,22},... | collective-permute-start | bytes 393224 | tf_op jit(solution)/shard_map/ppermute | solution.py:373

commit v3 on v2

--- a/solution.py
+++ b/solution.py
@@ -29,15 +29,19 @@
 VMEM_BYTES = 16 * 1024 * 1024
 
 
-def call(kernel, out_shape, in_specs, flops=0, moved=4 << 20, scratch=()):
+def call(kernel, out_shape, in_specs, flops=0, moved=4 << 20, scratch=(), vmem=VMEM_BYTES):
+    def placed(*refs):
+        n_x = lax.axis_size("x")
+        return kernel((lax.axis_index("y") * n_x + lax.axis_index("x"), lax.axis_index("core")), *refs)
+
     return pl.pallas_call(
-        kernel,
+        placed,
         out_shape=out_shape,
         in_specs=in_specs,
         out_specs=jax.tree.map(lambda _: WHOLE, out_shape),
         scratch_shapes=scratch,
         cost_estimate=pl.CostEstimate(flops=flops, bytes_accessed=moved, transcendentals=0),
-        compiler_params=pltpu.CompilerParams(vmem_limit_bytes=VMEM_BYTES),
+        compiler_params=pltpu.CompilerParams(vmem_limit_bytes=vmem),
     )
 
 
@@ -90,22 +94,13 @@
     return jnp.concatenate(terms, axis=0)
 
 
-def fill_q(plan, me_ref, q_ref, pieces):
-    tokens = plan.tokens
-    for mask, out in enumerate(pieces):
-        kv_head = plan.first_kv_head(me_ref[0] ^ mask)
-        for g in range(plan.q_heads):
-            out[g * tokens : (g + 1) * tokens, :] = columns(q_ref, kv_head * GROUP + g)[...]
-
-
-def pack_kernel(plan, me_ref, do_hbm, o_hbm, k_hbm, v_hbm, q_hbm, *refs):
-    pieces, q_pieces = refs[: plan.chips], refs[plan.chips : 2 * plan.chips]
-    do_ref, o_ref, k_ref, v_ref, q_ref, delta_ref, arrived = refs[2 * plan.chips :]
+def pack_kernel(plan, me, do_hbm, o_hbm, k_hbm, v_hbm, *refs):
+    pieces, (do_ref, o_ref, k_ref, v_ref, delta_ref, arrived) = refs[: plan.chips], refs[plan.chips :]
     tokens = plan.tokens
     half = tokens // 2
     loads = []
     for n, (source, target) in enumerate(
-        ((do_hbm, do_ref), (o_hbm, o_ref), (k_hbm, k_ref), (v_hbm, v_ref), (q_hbm, q_ref))
+        ((do_hbm, do_ref), (o_hbm, o_ref), (k_hbm, k_ref), (v_hbm, v_ref))
     ):
         pair = []
         for part in range(2):
@@ -131,7 +126,7 @@
     wait_for(2)
     wait_for(3)
     for mask, out in enumerate(pieces):
-        kv_head = plan.first_kv_head(me_ref[0] ^ mask)
+        kv_head = plan.first_kv_head(me[0] ^ mask)
         terms = []
         for g in range(plan.q_heads):
             head = kv_head * GROUP + g
@@ -143,20 +138,31 @@
             at += plan.kv_heads * tokens
             out[at : at + tokens, :] = columns(v_ref, kv_head + h)[...]
         out[plan.q_rows + plan.kv_rows :, :] = padded_rows(terms, plan.aux_sent)
-    wait_for(4)
-    fill_q(plan, me_ref, q_ref, q_pieces)
-
-
-def pack_q_kernel(plan, me_ref, q_ref, *pieces):
-    fill_q(plan, me_ref, q_ref, pieces)
-
-
-def assemble_kernel(plan, me_ref, lse_ref, *refs):
+
+
+def pack_q_kernel(plan, me, *refs):
+    levels, pieces = refs[: -plan.chips], refs[-plan.chips :]
+    tokens = plan.tokens
+    for mask, out in enumerate(pieces):
+        first = plan.first_kv_head(me[0] ^ mask) * GROUP
+        for level, ref in enumerate(levels):
+            for g in range(plan.q_heads):
+                at = level * plan.q_rows + g * tokens
+                out[at : at + tokens, :] = columns(ref, first + g)[...]
+
+
+def ordered_kernel(me, *refs):
+    pieces, out = refs[:-1], refs[-1]
+    for mask, piece in enumerate(pieces):
+        out[me[0] ^ mask] = piece[...]
+
+
+def assemble_kernel(plan, me, lse_ref, *refs):
     pieces, (do_out, kv_out) = refs[:-2], refs[-2:]
     tokens, split = plan.tokens, plan.q_rows + plan.kv_rows
     for mask, piece in enumerate(pieces):
-        chip = me_ref[0] ^ mask
-        chunk = (chip % plan.n_x) * CORES + me_ref[1]
+        chip = me[0] ^ mask
+        chunk = (chip % plan.n_x) * CORES + me[1]
         do_out[chip, : plan.q_rows, :] = piece[: plan.q_rows, :]
         kv_out[chip] = piece[plan.q_rows : split, :]
         terms = [piece[split : split + 3 * plan.q_heads, :]]
@@ -170,9 +176,9 @@
         do_out[chip, plan.q_rows :, :] = padded_rows(terms, plan.aux)
 
 
-def merge_kernel(me_ref, keep_ref, given_ref, *pieces):
+def merge_kernel(me, keep_ref, given_ref, *pieces):
     for mask, out in enumerate(pieces):
-        chip = me_ref[0] ^ mask
+        chip = me[0] ^ mask
         out[...] = (keep_ref[chip] + given_ref[chip].astype(F32)).astype(BF16)
 
 
@@ -184,15 +190,15 @@
     return row
 
 
-def role_kernel(plan, has_dq, me_ref, code_ref, mine_ref, sib_ref, *refs):
+def role_kernel(plan, at_level, has_dq, me, code_ref, mine_ref, sib_ref, *refs):
     refs = list(refs)
     levels, chips = len(has_dq), plan.chips
-    q_pieces = [[refs.pop(0) for _ in range(chips)] for _ in range(levels)]
+    q_pieces = [refs.pop(0) for _ in range(chips)]
     do_refs = [refs.pop(0) for _ in range(levels)]
     dq_ins = [refs.pop(0) if has else None for has in has_dq]
     dq_outs = [refs.pop(0) for _ in range(levels)]
     keep, give, kv_ref, q_ref, do_ref, dq_ref, dkv_ref = refs
-    core = me_ref[1]
+    core = me[1]
     tokens, n_x, fold = plan.tokens, plan.n_x, plan.fold
     q_per = QUERY_TILE // tokens
     k_per = KEY_TILE // tokens
@@ -201,7 +207,8 @@
     dkv_ref[...] = jnp.zeros_like(dkv_ref)
     for level in range(levels):
         for mask in range(chips):
-            q_ref[level, me_ref[0] ^ mask] = q_pieces[level][mask][...]
+            first = at_level[level] * plan.q_rows
+            q_ref[level, me[0] ^ mask] = q_pieces[mask][first : first + plan.q_rows, :]
         do_ref[level] = do_refs[level][...]
         dq_ref[level] = dq_ins[level][...] if has_dq[level] else jnp.zeros_like(dq_outs[level], F32)
 
@@ -316,7 +323,7 @@
     give[...] = dkv_ref[1 - core].astype(BF16)
 
 
-def finish_kernel(plan, has_far, me_ref, dq_ref, *refs):
+def finish_kernel(plan, has_far, me, dq_ref, *refs):
     refs = list(refs)
     far_ref = refs.pop(0) if has_far else None
     pieces, rows_ref = refs[:-1], refs[-1]
@@ -334,25 +341,24 @@
                     source = g * QUERY_TILE + n * tokens
                     rows_ref[tile * q_per + n, at : at + tokens, :] = turned[source : source + tokens]
     for mask, out in enumerate(pieces):
-        out[...] = rows_ref[me_ref[0] ^ mask]
-
-
-def unpack_kernel(plan, levels, me_ref, *refs):
+        out[...] = rows_ref[me[0] ^ mask]
+
+
+def unpack_kernel(plan, has_far, me, *refs):
     refs = list(refs)
     dq_pieces = [refs.pop(0) for _ in range(plan.chips)]
-    kv_pieces = [[refs.pop(0) for _ in range(plan.chips)] for _ in range(levels)]
+    kv_pieces = [refs.pop(0) for _ in range(plan.chips)]
+    far_ref = refs.pop(0) if has_far else None
     dq_ref, dk_ref, dv_ref = refs
     tokens = plan.tokens
     for mask in range(plan.chips):
-        kv_head = plan.first_kv_head(me_ref[0] ^ mask)
+        chip = me[0] ^ mask
+        kv_head = plan.first_kv_head(chip)
         for g in range(plan.q_heads):
             columns(dq_ref, kv_head * GROUP + g)[...] = dq_pieces[mask][g * tokens : (g + 1) * tokens, :]
-        total = kv_pieces[0][mask][...]
-        if levels > 1:
-            total = total.astype(F32)
-            for level in range(1, levels):
-                total = total + kv_pieces[level][mask][...].astype(F32)
-            total = total.astype(BF16)
+        total = kv_pieces[mask][...]
+        if has_far:
+            total = (total.astype(F32) + far_ref[chip].astype(F32)).astype(BF16)
         for h in range(plan.kv_heads):
             columns(dk_ref, kv_head + h)[...] = total[h * tokens : (h + 1) * tokens]
             at = (plan.kv_heads + h) * tokens
@@ -367,18 +373,6 @@
     ]
 
 
-def deliver(pieces, planes, level):
-    chips = len(pieces)
-    return [
-        lax.ppermute(
-            pieces[mask],
-            ("z",) + CROSS,
-            [(p * chips + i, (p - level) * chips + (i ^ mask)) for p in range(level, planes) for i in range(chips)],
-        )
-        for mask in range(chips)
-    ]
-
-
 def swap(value):
     return lax.ppermute(value, "core", [(0, 1), (1, 0)])
 
@@ -393,16 +387,13 @@
 
 
 def plane_logsum(logsum, plan, y, core):
-    other = swap(logsum)
-    both = jnp.where(core == 0, jnp.concatenate([logsum, other]), jnp.concatenate([other, logsum]))
-    rows = both.reshape(plan.fold, plan.q_heads, plan.block)
-    parts = []
-    for mask in range(plan.fold):
-        part = lax.dynamic_index_in_dim(rows, y ^ mask, 0, keepdims=False)
-        if mask:
-            part = lax.ppermute(part, "y", [(i, i ^ mask) for i in range(plan.fold)])
-        parts.append(part)
-    lse = jnp.stack(parts)
+    blocks = [logsum]
+    for mask in range(1, plan.fold):
+        blocks.append(lax.ppermute(logsum, "y", [(i, i ^ mask) for i in range(plan.fold)]))
+    mine = jnp.stack(blocks)
+    other = swap(mine)
+    both = jnp.where(core == 0, jnp.concatenate([mine, other], axis=1), jnp.concatenate([other, mine], axis=1))
+    lse = lax.dynamic_slice_in_dim(both, y * plan.q_heads, plan.q_heads, axis=1)
     if plan.tokens == LANES:
         return lse
     lse = lse.reshape(plan.fold, plan.q_heads, plan.n_x * CORES, plan.tokens).transpose(0, 2, 1, 3)
@@ -414,8 +405,7 @@
     plan = Plan(fold, n_x, queries.shape[0])
     chips = plan.chips
     reach = -(-(WIN - 1) // fold)
-    z, y, x, core = (lax.axis_index(a) for a in ("z", "y", "x", "core"))
-    me = jnp.stack([y * n_x + x, core]).astype(jnp.int32)
+    z, y, core = (lax.axis_index(a) for a in ("z", "y", "core"))
 
     def like(rows):
         return jax.ShapeDtypeStruct((rows, LANES), BF16)
@@ -428,20 +418,20 @@
         raw.append(along(raw[-1], planes, -1))
 
     lse = plane_logsum(logsum, plan, y, core)
-    arrays = (output_gradient, outputs, key_vectors, values, queries)
-    packed = call(
+    arrays = (output_gradient, outputs, key_vectors, values)
+    pieces = call(
         functools.partial(pack_kernel, plan),
-        [like(plan.q_rows + plan.kv_rows + plan.aux_sent)] * chips + [like(plan.q_rows)] * chips,
-        [SCALARS] + [pl.BlockSpec(memory_space=pltpu.HBM)] * len(arrays),
+        [like(plan.q_rows + plan.kv_rows + plan.aux_sent)] * chips,
+        [pl.BlockSpec(memory_space=pltpu.HBM)] * len(arrays),
         scratch=[pltpu.VMEM(a.shape, a.dtype) for a in arrays]
         + [pltpu.VMEM((LANES, LANES), F32), pltpu.SemaphoreType.DMA((len(arrays), 2))],
-    )(me, *arrays)
-    pieces, q_pieces = packed[:chips], packed[chips:]
+        vmem=60 * 1024 * 1024,
+    )(*arrays)
     do_own, kv_own = call(
         functools.partial(assemble_kernel, plan),
         [stacked(plan.q_rows + plan.aux), stacked(plan.kv_rows)],
-        [SCALARS] + [WHOLE] * (chips + 1),
-    )(me, lse, *exchange(pieces))
+        [WHOLE] * (chips + 1),
+    )(lse, *exchange(pieces))
 
     up = [kv_own]
     for _ in range(1, (reach + 1) // 2 + 1):
@@ -449,15 +439,12 @@
     far_do = [do_own]
     for _ in range(1, reach // 2 + 1):
         far_do.append(along(far_do[-1], planes, -1))
-    all_q = [exchange(q_pieces)]
-    for n in range(1, len(raw)):
-        far_pieces = call(
-            functools.partial(pack_q_kernel, plan), [like(plan.q_rows)] * chips, [SCALARS, WHOLE]
-        )(me, raw[n])
-        all_q.append(exchange(far_pieces))
+    q_pieces = exchange(
+        call(functools.partial(pack_q_kernel, plan), [like(len(raw) * plan.q_rows)] * chips, [WHOLE] * len(raw))(*raw),
+    )
     up = [(kv, swap(kv)) for kv in up]
 
-    grad_q = [None] * len(all_q)
+    grad_q = [None] * len(raw)
     grad_kv = []
     dq_shape = (fold * plan.q_tiles, plan.kv_heads, HEAD_SIZE, GROUP * QUERY_TILE)
     inside = jnp.arange(fold, dtype=jnp.int32)
@@ -471,10 +458,10 @@
         has_dq = tuple(grad_q[j] is not None for j in levels)
         over = [j and j not in query_levels(i + 1, reach) for j in levels]
         *parts, keep, give = call(
-            functools.partial(role_kernel, plan, has_dq),
+            functools.partial(role_kernel, plan, tuple(levels), has_dq),
             [jax.ShapeDtypeStruct(dq_shape, BF16 if done else F32) for done in over]
             + [stacked(plan.kv_rows, F32), stacked(plan.kv_rows)],
-            [SCALARS] * 2 + [WHOLE] * (2 + len(levels) * (chips + 1) + sum(has_dq)),
+            [SCALARS] + [WHOLE] * (2 + chips + len(levels) + sum(has_dq)),
             flops=10 * len(levels) * fold * fold * plan.q_heads * plan.block * plan.block * HEAD_SIZE // CORES,
             scratch=[
                 pltpu.VMEM((CORES, chips, plan.kv_rows, LANES), BF16),
@@ -484,41 +471,44 @@
                 pltpu.VMEM((CORES, chips, plan.kv_rows, LANES), F32),
             ],
         )(
-            me,
             codes,
             mine,
             sibling,
-            *[piece for j in levels for piece in all_q[j]],
+            *q_pieces,
             *[far_do[j] for j in levels],
             *[grad_q[j] for j in levels if grad_q[j] is not None],
         )
         for j, part in zip(levels, parts):
             grad_q[j] = part
-        merged = call(merge_kernel, [like(plan.kv_rows)] * chips, [SCALARS] + [WHOLE] * 2)(me, keep, swap(give))
-        grad_kv.append(deliver(merged, planes, i) if i else exchange(merged))
-
+        merged = call(merge_kernel, [like(plan.kv_rows)] * chips, [WHOLE] * 2)(keep, swap(give))
+        grad_kv.append(exchange(merged))
+
+    def plus(part, far):
+        return part if far is None else (part.astype(F32) + far.astype(F32)).astype(BF16)
+
+    far_kv = None
+    for level in range(len(grad_kv) - 1, 0, -1):
+        part = call(ordered_kernel, stacked(plan.kv_rows), [WHOLE] * chips)(*grad_kv[level])
+        far_kv = along(plus(part, far_kv), planes, -1)
     far_q = None
     for level in range(len(grad_q) - 1, 0, -1):
-        part = grad_q[level]
-        if far_q is not None:
-            part = (part.astype(F32) + far_q.astype(F32)).astype(BF16)
-        far_q = along(part, planes, 1)
+        far_q = along(plus(grad_q[level], far_q), planes, 1)
     dq_pieces = call(
         functools.partial(finish_kernel, plan, far_q is not None),
         [like(plan.q_rows)] * chips,
-        [SCALARS, WHOLE] + [WHOLE] * (far_q is not None),
+        [WHOLE] + [WHOLE] * (far_q is not None),
         scratch=[pltpu.VMEM((chips, plan.q_rows, LANES), BF16)],
-    )(me, grad_q[0], *([] if far_q is None else [far_q]))
+    )(grad_q[0], *([] if far_q is None else [far_q]))
     return tuple(
         call(
-            functools.partial(unpack_kernel, plan, len(grad_kv)),
+            functools.partial(unpack_kernel, plan, far_kv is not None),
             [
                 jax.ShapeDtypeStruct((plan.tokens, QUERY_HEADS * HEAD_SIZE), BF16),
                 jax.ShapeDtypeStruct((plan.tokens, KEY_VALUE_HEADS * HEAD_SIZE), BF16),
                 jax.ShapeDtypeStruct((plan.tokens, KEY_VALUE_HEADS * HEAD_SIZE), BF16),
             ],
-            [SCALARS] + [WHOLE] * (chips * (1 + len(grad_kv))),
-        )(me, *exchange(dq_pieces), *[piece for level in grad_kv for piece in level])
+            [WHOLE] * (2 * chips + (far_kv is not None)),
+        )(*exchange(dq_pieces), *grad_kv[0], *([] if far_kv is None else [far_kv]))
     )
 
 

time: 108 us -> 90.7 us (0.84)
  the two profiles are of different devices: /device:TPU:0 before, /device:TPU:18 now
where the time goes in v3:
time: 90.7 us; the launch traced here: 90.4 us
  waiting for transfers between devices  36.1 us (40%)
  starting transfers between devices  33 us (36%)
  Pallas kernels  18.3 us (20%)
  local copies, waits for them, and re-layouts  1.64 us (2%)
    ppermute x15, waiting for transfers between devices, exchange(): lax.ppermute(pieces[mask], CROSS, [(i, i ^ mask) for i in range(chips)])  32.8 us
    ppermute x15, starting transfers between devices, exchange(): lax.ppermute(pieces[mask], CROSS, [(i, i ^ mask) for i in range(chips)])  16.9 us
    ppermute x5, starting transfers between devices, along(): return lax.ppermute(value, 'z', pairs)  13.9 us
    pallas_call x2, Pallas kernels, body(): call(functools.partial(role_kernel, plan, tuple(levels), has_dq), [jax.Sh...  13.2 us
    pallas_call x1, Pallas kernels, body(): call(functools.partial(pack_kernel, plan), [like(plan.q_rows + plan.kv_ro...  2.93 us
    ppermute x5, waiting for transfers between devices, along(): return lax.ppermute(value, 'z', pairs)  2.09 us
  transfers between devices with their start and end apart: 26, of which 13 were waited for; matrix products, arithmetic and copies ran while one was open for 1% of the time, Pallas kernels for 9%

profile of v3, /device:TPU:18, one launch (start us, length us, event | category | flops | bytes accessed | tf_op | source)
XLA Modules:
  0.0 90.4 jit_solution(13465808725450200937)
XLA Ops:
  0.6 1.6 %collective-permute-start = (f32[4,512]{1,0:T(4,128)}, f32[4,512]{1,0:T(4,128)S(1)}, u32[]{:S(2)}, u32[]{:S(2)}) collective-permute-start(f32[4,512]{1,0:T(4,128)} %param.14), channel_id=1, source_target_pairs={{0,4},{4,0},{1,5},{5,1},{2,6},{6,2},{3,7},{7,3},{8,12},{12,8},{9,1... | collective-permute-start | bytes 24584 | tf_op jit(solution)/shard_map/ppermute | solution.py:392
  2.2 2.3 %collective-permute-start.7 = (bf16[128,2048]{1,0:T(8,128)(2,1)}, bf16[128,2048]{1,0:T(8,128)(2,1)S(1)}, u32[]{:S(2)}, u32[]{:S(2)}) collective-permute-start(bf16[128,2048]{1,0:T(8,128)(2,1)} %refs_0_.3), channel_id=1, source_target_pairs={{8,0},{16,8},{24,16},{9,1},{17,9},{25,17},{10,2},{18,10},{26,18},{... | collective-permute-start | bytes 1572872 | tf_op jit(solution)/shard_map/ppermute | solution.py:382
  4.6 2.9 %shard_map.112 = (bf16[1040,128]{1,0:T(8,128)(2,1)}, bf16[1040,128]{1,0:T(8,128)(2,1)}, bf16[1040,128]{1,0:T(8,128)(2,1)}, bf16[1040,128]{1,0:T(8,128)(2,1)}) custom-call(bf16[128,2048]{1,0:T(8,128)(2,1)} %refs_0_.2, bf16[128,2048]{1,0:T(8,128)(2,1)} %refs_1_.1, bf16[128,1024]{1,0:T(8,128)(2,1)} %refs_2_.1, bf16[128,1024]{1,0:T(8,128)(2,1)} %refs_3_.1), custom_call_target="tpu_custom_call" | custom-call | bytes 4194304 | tf_op jit(solution)/shard_map/pallas_call | solution.py:422
  7.5 0.6 collective-permute-start.2
  8.1 0.5 collective-permute-start.3
  8.6 2.4 %collective-permute-start.4 = (bf16[1040,128]{1,0:T(8,128)(2,1)}, bf16[1040,128]{1,0:T(8,128)(2,1)S(1)}, u32[]{:S(2)}, u32[]{:S(2)}) collective-permute-start(bf16[1040,128]{1,0:T(8,128)(2,1)} %get-tuple-element.35), channel_id=1, source_target_pairs={{0,6},{2,4},{4,2},{6,0},{1,7},{3,5},{5,3},{7,1},{8,14},{10,12},{12... | collective-permute-start | bytes 798728 | tf_op jit(solution)/shard_map/ppermute | solution.py:371
  11.1 0.7 copy-done.2
  11.8 1.2 %collective-permute-done.1 = f32[2,4,512]{2,1,0:T(4,128)S(1)} collective-permute-done((f32[2,4,512]{2,1,0:T(4,128)S(1)}, f32[2,4,512]{2,1,0:T(4,128)S(1)}, u32[]{:S(2)}, u32[]{:S(2)}) %collective-permute-start.1) | collective-permute-done | bytes 16416 | tf_op jit(solution)/shard_map/ppermute | solution.py:377
  13.0 4.1 %collective-permute-done.2.refs_2_ = bf16[1040,128]{1,0:T(8,128)(2,1)S(1)} collective-permute-done((bf16[1040,128]{1,0:T(8,128)(2,1)}, bf16[1040,128]{1,0:T(8,128)(2,1)S(1)}, u32[]{:S(2)}, u32[]{:S(2)}) %collective-permute-start.2) | collective-permute-done | bytes 266272 | tf_op jit(solution)/shard_map/ppermute | solution.py:371
  17.1 4.3 %collective-permute-done.3.refs_3_ = bf16[1040,128]{1,0:T(8,128)(2,1)S(1)} collective-permute-done((bf16[1040,128]{1,0:T(8,128)(2,1)}, bf16[1040,128]{1,0:T(8,128)(2,1)S(1)}, u32[]{:S(2)}, u32[]{:S(2)}) %collective-permute-start.3) | collective-permute-done | bytes 266272 | tf_op jit(solution)/shard_map/ppermute | solution.py:371
  21.3 1.0 %copy-done.1 = bf16[1040,128]{1,0:T(8,128)(2,1)S(1)} copy-done((bf16[1040,128]{1,0:T(8,128)(2,1)S(1)}, bf16[1040,128]{1,0:T(8,128)(2,1)}, u32[]{:S(2)}) %copy-start.1) | copy-done | bytes 266264
  22.3 0.1 shard_map.113
  22.4 3.6 %collective-permute-start.5 = (bf16[4,512,128]{2,1,0:T(8,128)(2,1)S(1)}, bf16[4,512,128]{2,1,0:T(8,128)(2,1)S(1)}, u32[]{:S(2)}, u32[]{:S(2)}) collective-permute-start(bf16[4,512,128]{2,1,0:T(8,128)(2,1)S(1)} %get-tuple-element.36.refs_1_), channel_id=1, source_target_pairs={{0,8},{8,16},{16,24},{1,9},{9,17},{17,25},{2,10},{10,18},{18,26},{... | collective-permute-start | bytes 1572872 | tf_op jit(solution)/shard_map/ppermute | solution.py:382
  26.0 0.1 broadcast_compare_fusion.1
  26.1 0.3 shard_map.114
  26.4 1.6 %collective-permute-start.8 = (bf16[1024,128]{1,0:T(8,128)(2,1)S(1)}, bf16[1024,128]{1,0:T(8,128)(2,1)S(1)}, u32[]{:S(2)}, u32[]{:S(2)}) collective-permute-start(bf16[1024,128]{1,0:T(8,128)(2,1)S(1)} %get-tuple-element.38), channel_id=1, source_target_pairs={{0,2},{2,0},{4,6},{6,4},{1,3},{3,1},{5,7},{7,5},{8,10},{10,8},{12,... | collective-permute-start | bytes 786440 | tf_op jit(solution)/shard_map/ppermute | solution.py:371
  28.1 2.3 %collective-permute-start.11 = (bf16[4,544,128]{2,1,0:T(8,128)(2,1)S(1)}, bf16[4,544,128]{2,1,0:T(8,128)(2,1)S(1)}, u32[]{:S(2)}, u32[]{:S(2)}) collective-permute-start(bf16[4,544,128]{2,1,0:T(8,128)(2,1)S(1)} %get-tuple-element.41.refs_7_), channel_id=1, source_target_pairs={{8,0},{16,8},{24,16},{9,1},{17,9},{25,17},{10,2},{18,10},{26,18},{... | collective-permute-start | bytes 1671176 | tf_op jit(solution)/shard_map/ppermute | solution.py:382
  30.4 0.6 collective-permute-start.9
  31.0 1.9 %collective-permute-done.8.refs_4_ = bf16[1024,128]{1,0:T(8,128)(2,1)S(1)} collective-permute-done((bf16[1024,128]{1,0:T(8,128)(2,1)S(1)}, bf16[1024,128]{1,0:T(8,128)(2,1)S(1)}, u32[]{:S(2)}, u32[]{:S(2)}) %collective-permute-start.8) | collective-permute-done | bytes 262176 | tf_op jit(solution)/shard_map/ppermute | solution.py:371
  32.9 1.4 %collective-permute-start.10 = (bf16[1024,128]{1,0:T(8,128)(2,1)S(1)}, bf16[1024,128]{1,0:T(8,128)(2,1)S(1)}, u32[]{:S(2)}, u32[]{:S(2)}) collective-permute-start(bf16[1024,128]{1,0:T(8,128)(2,1)S(1)} %get-tuple-element.40), channel_id=1, source_target_pairs={{0,6},{2,4},{4,2},{6,0},{1,7},{3,5},{5,3},{7,1},{8,14},{10,12},{12... | collective-permute-start | bytes 786440 | tf_op jit(solution)/shard_map/ppermute | solution.py:371
  34.3 2.1 %collective-permute-done.5.refs_1_ = bf16[4,512,128]{2,1,0:T(8,128)(2,1)S(1)} collective-permute-done((bf16[4,512,128]{2,1,0:T(8,128)(2,1)S(1)}, bf16[4,512,128]{2,1,0:T(8,128)(2,1)S(1)}, u32[]{:S(2)}, u32[]{:S(2)}) %collective-permute-start.5) | collective-permute-done | bytes 524320 | tf_op jit(solution)/shard_map/ppermute | solution.py:382
  36.5 0.1 fusion.6
  36.6 0.2 fusion.5.refs_0_
  36.8 7.7 %collective-permute-done.9.refs_5_ = bf16[1024,128]{1,0:T(8,128)(2,1)S(1)} collective-permute-done((bf16[1024,128]{1,0:T(8,128)(2,1)S(1)}, bf16[1024,128]{1,0:T(8,128)(2,1)S(1)}, u32[]{:S(2)}, u32[]{:S(2)}) %collective-permute-start.9) | collective-permute-done | bytes 262176 | tf_op jit(solution)/shard_map/ppermute | solution.py:371
  44.5 4.1 %shard_map.115 = (f32[4,2,128,256]{3,2,1,0:T(8,128)S(1)}, f32[4,512,128]{2,1,0:T(8,128)S(1)}, bf16[4,512,128]{2,1,0:T(8,128)(2,1)S(1)}) custom-call(s32[1,2,2]{2,1,0:T(2,128)S(1)} %bitcast.10, bf16[4,512,128]{2,1,0:T(8,128)(2,1)S(1)} %get-tuple-element.36.refs_1_, bf16[4,512,128]{2,1,0:T(8,128)(2,1)S(1)} %collective-permute-done.12.refs_2_, ...), custom_call_target="tpu_custom_call" | custom-call | flops 2684354560 | bytes 4194304 | tf_op jit(solution)/shard_map/pallas_call | solution.py:460
  48.7 9.1 %shard_map.116 = (f32[4,2,128,256]{3,2,1,0:T(8,128)S(1)}, bf16[4,2,128,256]{3,2,1,0:T(8,128)(2,1)S(1)}, f32[4,512,128]{2,1,0:T(8,128)S(1)}, bf16[4,512,128]{2,1,0:T(8,128)(2,1)S(1)}) custom-call(s32[2,2,2]{2,1,0:T(2,128)S(1)} %fusion.5.refs_0_, bf16[4,512,128]{2,1,0:T(8,128)(2,1)S(1)} %collective-permute-done.5.refs_1_, ...), custom_call_target="tpu_custom_call" | custom-call | flops 5368709120 | bytes 4194304 | tf_op jit(solution)/shard_map/pallas_call | solution.py:460
  57.9 0.5 collective-permute-start.17
  58.4 1.9 %collective-permute-start.13 = (bf16[4,2,128,256]{3,2,1,0:T(8,128)(2,1)S(1)}, bf16[4,2,128,256]{3,2,1,0:T(8,128)(2,1)S(1)}, u32[]{:S(2)}, u32[]{:S(2)}) collective-permute-start(bf16[4,2,128,256]{3,2,1,0:T(8,128)(2,1)S(1)} %get-tuple-element.44), channel_id=1, source_target_pairs={{0,8},{8,16},{16,24},{1,9},{9,17},{17,25},{2,10},{10,18},{18,26},{... | collective-permute-start | bytes 1572872 | tf_op jit(solution)/shard_map/ppermute | solution.py:382
  60.3 0.1 shard_map.119
  60.4 0.6 collective-permute-start.22
  61.0 1.2 %collective-permute-start.23 = (bf16[512,128]{1,0:T(8,128)(2,1)S(1)}, bf16[512,128]{1,0:T(8,128)(2,1)S(1)}, u32[]{:S(2)}, u32[]{:S(2)}) collective-permute-start(bf16[512,128]{1,0:T(8,128)(2,1)S(1)} %get-tuple-element.59), channel_id=1, source_target_pairs={{0,4},{2,6},{4,0},{6,2},{1,5},{3,7},{5,1},{7,3},{8,12},{10,14},{12... | collective-permute-start | bytes 393224 | tf_op jit(solution)/shard_map/ppermute | solution.py:371
  62.2 1.8 %collective-permute-start.24 = (bf16[512,128]{1,0:T(8,128)(2,1)S(1)}, bf16[512,128]{1,0:T(8,128)(2,1)S(1)}, u32[]{:S(2)}, u32[]{:S(2)}) collective-permute-start(bf16[512,128]{1,0:T(8,128)(2,1)S(1)} %get-tuple-element.60), channel_id=1, source_target_pairs={{0,6},{2,4},{4,2},{6,0},{1,7},{3,5},{5,3},{7,1},{8,14},{10,12},{12... | collective-permute-start | bytes 393224 | tf_op jit(solution)/shard_map/ppermute | solution.py:371
  64.0 2.9 %collective-permute-done.22.refs_1_ = bf16[512,128]{1,0:T(8,128)(2,1)S(1)} collective-permute-done((bf16[512,128]{1,0:T(8,128)(2,1)S(1)}, bf16[512,128]{1,0:T(8,128)(2,1)S(1)}, u32[]{:S(2)}, u32[]{:S(2)}) %collective-permute-start.22) | collective-permute-done | bytes 131104 | tf_op jit(solution)/shard_map/ppermute | solution.py:371
  66.8 2.2 %collective-permute-done.23.refs_2_ = bf16[512,128]{1,0:T(8,128)(2,1)S(1)} collective-permute-done((bf16[512,128]{1,0:T(8,128)(2,1)S(1)}, bf16[512,128]{1,0:T(8,128)(2,1)S(1)}, u32[]{:S(2)}, u32[]{:S(2)}) %collective-permute-start.23) | collective-permute-done | bytes 131104 | tf_op jit(solution)/shard_map/ppermute | solution.py:371
  69.1 3.7 %collective-permute-start.25 = (bf16[4,512,128]{2,1,0:T(8,128)(2,1)S(1)}, bf16[4,512,128]{2,1,0:T(8,128)(2,1)S(1)}, u32[]{:S(2)}, u32[]{:S(2)}) collective-permute-start(bf16[4,512,128]{2,1,0:T(8,128)(2,1)S(1)} %shard_map.120), channel_id=1, source_target_pairs={{8,0},{16,8},{24,16},{9,1},{17,9},{25,17},{10,2},{18,10},{26,18},{... | collective-permute-start | bytes 1572872 | tf_op jit(solution)/shard_map/ppermute | solution.py:382
  72.8 0.1 shard_map.118
  72.9 1.5 %collective-permute-start.18 = (bf16[512,128]{1,0:T(8,128)(2,1)S(1)}, bf16[512,128]{1,0:T(8,128)(2,1)S(1)}, u32[]{:S(2)}, u32[]{:S(2)}) collective-permute-start(bf16[512,128]{1,0:T(8,128)(2,1)S(1)} %get-tuple-element.52), channel_id=1, source_target_pairs={{0,2},{2,0},{4,6},{6,4},{1,3},{3,1},{5,7},{7,5},{8,10},{10,8},{12,... | collective-permute-start | bytes 393224 | tf_op jit(solution)/shard_map/ppermute | solution.py:371
  74.4 0.5 collective-permute-start.19
  75.0 1.5 %collective-permute-start.20 = (bf16[512,128]{1,0:T(8,128)(2,1)S(1)}, bf16[512,128]{1,0:T(8,128)(2,1)S(1)}, u32[]{:S(2)}, u32[]{:S(2)}) collective-permute-start(bf16[512,128]{1,0:T(8,128)(2,1)S(1)} %get-tuple-element.54), channel_id=1, source_target_pairs={{0,6},{2,4},{4,2},{6,0},{1,7},{3,5},{5,3},{7,1},{8,14},{10,12},{12... | collective-permute-start | bytes 393224 | tf_op jit(solution)/shard_map/ppermute | solution.py:371
  76.5 0.2 shard_map.117
  76.7 1.5 %collective-permute-start.14 = (bf16[512,128]{1,0:T(8,128)(2,1)S(1)}, bf16[512,128]{1,0:T(8,128)(2,1)S(1)}, u32[]{:S(2)}, u32[]{:S(2)}) collective-permute-start(bf16[512,128]{1,0:T(8,128)(2,1)S(1)} %get-tuple-element.46), channel_id=1, source_target_pairs={{0,2},{2,0},{4,6},{6,4},{1,3},{3,1},{5,7},{7,5},{8,10},{10,8},{12,... | collective-permute-start | bytes 393224 | tf_op jit(solution)/shard_map/ppermute | solution.py:371
  78.2 1.1 %collective-permute-done.18.refs_5_ = bf16[512,128]{1,0:T(8,128)(2,1)S(1)} collective-permute-done((bf16[512,128]{1,0:T(8,128)(2,1)S(1)}, bf16[512,128]{1,0:T(8,128)(2,1)S(1)}, u32[]{:S(2)}, u32[]{:S(2)}) %collective-permute-start.18) | collective-permute-done | bytes 131104 | tf_op jit(solution)/shard_map/ppermute | solution.py:371
  79.3 1.2 %collective-permute-start.15 = (bf16[512,128]{1,0:T(8,128)(2,1)S(1)}, bf16[512,128]{1,0:T(8,128)(2,1)S(1)}, u32[]{:S(2)}, u32[]{:S(2)}) collective-permute-start(bf16[512,128]{1,0:T(8,128)(2,1)S(1)} %get-tuple-element.47), channel_id=1, source_target_pairs={{0,4},{2,6},{4,0},{6,2},{1,5},{3,7},{5,1},{7,3},{8,12},{10,14},{12... | collective-permute-start | bytes 393224 | tf_op jit(solution)/shard_map/ppermute | solution.py:371
  80.5 2.8 %collective-permute-done.19.refs_6_ = bf16[512,128]{1,0:T(8,128)(2,1)S(1)} collective-permute-done((bf16[512,128]{1,0:T(8,128)(2,1)S(1)}, bf16[512,128]{1,0:T(8,128)(2,1)S(1)}, u32[]{:S(2)}, u32[]{:S(2)}) %collective-permute-start.19) | collective-permute-done | bytes 131104 | tf_op jit(solution)/shard_map/ppermute | solution.py:371
  83.4 1.2 %collective-permute-done.14.refs_1_ = bf16[512,128]{1,0:T(8,128)(2,1)S(1)} collective-permute-done((bf16[512,128]{1,0:T(8,128)(2,1)S(1)}, bf16[512,128]{1,0:T(8,128)(2,1)S(1)}, u32[]{:S(2)}, u32[]{:S(2)}) %collective-permute-start.14) | collective-permute-done | bytes 131104 | tf_op jit(solution)/shard_map/ppermute | solution.py:371
  84.5 0.5 collective-permute-done.15.refs_2_
  85.1 4.2 %collective-permute-done.16.refs_3_ = bf16[512,128]{1,0:T(8,128)(2,1)S(1)} collective-permute-done((bf16[512,128]{1,0:T(8,128)(2,1)S(1)}, bf16[512,128]{1,0:T(8,128)(2,1)S(1)}, u32[]{:S(2)}, u32[]{:S(2)}) %collective-permute-start.16) | collective-permute-done | bytes 131104 | tf_op jit(solution)/shard_map/ppermute | solution.py:371
  89.2 1.2 %shard_map.121 = (bf16[128,2048]{1,0:T(8,128)(2,1)}, bf16[128,1024]{1,0:T(8,128)(2,1)}, bf16[128,1024]{1,0:T(8,128)(2,1)}) custom-call(bf16[512,128]{1,0:T(8,128)(2,1)S(1)} %get-tuple-element.45.refs_0_, bf16[512,128]{1,0:T(8,128)(2,1)S(1)} %collective-permute-done.14.refs_1_, bf16[512,128]{1,0:T(8,128)(2,1)S(1)} %collective-permute-done.15.refs_2_, ...), custom_call_target="tpu_custom_call" | custom-call | bytes 4194304 | tf_op jit(solution)/shard_map/pallas_call | solution.py:503
  (32 shorter events, 0.4 us)
Async XLA Ops:
  0.6 10.5 %collective-permute-start = (f32[4,512]{1,0:T(4,128)}, f32[4,512]{1,0:T(4,128)S(1)}, u32[]{:S(2)}, u32[]{:S(2)}) collective-permute-start(f32[4,512]{1,0:T(4,128)} %param.14), channel_id=1, source_target_pairs={{0,4},{4,0},{1,5},{5,1},{2,6},{6,2},{3,7},{7,3},{8,12},{12,8},{9,1... | collective-permute-start | bytes 24584 | tf_op jit(solution)/shard_map/ppermute | solution.py:392
  2.2 23.9 %collective-permute-start.7 = (bf16[128,2048]{1,0:T(8,128)(2,1)}, bf16[128,2048]{1,0:T(8,128)(2,1)S(1)}, u32[]{:S(2)}, u32[]{:S(2)}) collective-permute-start(bf16[128,2048]{1,0:T(8,128)(2,1)} %refs_0_.3), channel_id=1, source_target_pairs={{8,0},{16,8},{24,16},{9,1},{17,9},{25,17},{10,2},{18,10},{26,18},{... | collective-permute-start | bytes 1572872 | tf_op jit(solution)/shard_map/ppermute | solution.py:382
  7.5 9.5 %collective-permute-start.2 = (bf16[1040,128]{1,0:T(8,128)(2,1)}, bf16[1040,128]{1,0:T(8,128)(2,1)S(1)}, u32[]{:S(2)}, u32[]{:S(2)}) collective-permute-start(bf16[1040,128]{1,0:T(8,128)(2,1)} %get-tuple-element.33), channel_id=1, source_target_pairs={{0,2},{2,0},{4,6},{6,4},{1,3},{3,1},{5,7},{7,5},{8,10},{10,8},{12,... | collective-permute-start | bytes 798728 | tf_op jit(solution)/shard_map/ppermute | solution.py:371
  8.1 3.0 %copy-start.3 = (s32[20,3]{0,1:T(4,128)S(1)}, s32[20,3]{0,1:T(4,128)}, u32[]{:S(2)}) copy-start(s32[20,3]{0,1:T(4,128)} %param.15) | copy-start | bytes 724
  8.1 13.2 %collective-permute-start.3 = (bf16[1040,128]{1,0:T(8,128)(2,1)}, bf16[1040,128]{1,0:T(8,128)(2,1)S(1)}, u32[]{:S(2)}, u32[]{:S(2)}) collective-permute-start(bf16[1040,128]{1,0:T(8,128)(2,1)} %get-tuple-element.34), channel_id=1, source_target_pairs={{0,4},{2,6},{4,0},{6,2},{1,5},{3,7},{5,1},{7,3},{8,12},{10,14},{12... | collective-permute-start | bytes 798728 | tf_op jit(solution)/shard_map/ppermute | solution.py:371
  8.6 12.7 %collective-permute-start.4 = (bf16[1040,128]{1,0:T(8,128)(2,1)}, bf16[1040,128]{1,0:T(8,128)(2,1)S(1)}, u32[]{:S(2)}, u32[]{:S(2)}) collective-permute-start(bf16[1040,128]{1,0:T(8,128)(2,1)} %get-tuple-element.35), channel_id=1, source_target_pairs={{0,6},{2,4},{4,2},{6,0},{1,7},{3,5},{5,3},{7,1},{8,14},{10,12},{12... | collective-permute-start | bytes 798728 | tf_op jit(solution)/shard_map/ppermute | solution.py:371
  11.1 0.7 copy-start.2
  11.8 1.2 %collective-permute-start.1 = (f32[2,4,512]{2,1,0:T(4,128)S(1)}, f32[2,4,512]{2,1,0:T(4,128)S(1)}, u32[]{:S(2)}, u32[]{:S(2)}) collective-permute-start(f32[2,4,512]{2,1,0:T(4,128)S(1)} %pad_maximum_fusion), channel_id=1, source_target_pairs={{0,1},{1,0},{2,3},{3,2},{4,5},{5,4},{6,7},{7,6},{8,9},{9,8},{10,11... | collective-permute-start | bytes 49160 | tf_op jit(solution)/shard_map/ppermute | solution.py:377
  21.3 1.0 %copy-start.1 = (bf16[1040,128]{1,0:T(8,128)(2,1)S(1)}, bf16[1040,128]{1,0:T(8,128)(2,1)}, u32[]{:S(2)}) copy-start(bf16[1040,128]{1,0:T(8,128)(2,1)} %get-tuple-element.32.refs_1_) | copy-start | bytes 798724
  22.3 3.8 %copy-start = (bf16[128,2048]{1,0:T(8,128)(2,1)S(1)}, bf16[128,2048]{1,0:T(8,128)(2,1)}, u32[]{:S(2)}) copy-start(bf16[128,2048]{1,0:T(8,128)(2,1)} %refs_0_.3) | copy-start | bytes 1572868
  22.4 14.0 %collective-permute-start.5 = (bf16[4,512,128]{2,1,0:T(8,128)(2,1)S(1)}, bf16[4,512,128]{2,1,0:T(8,128)(2,1)S(1)}, u32[]{:S(2)}, u32[]{:S(2)}) collective-permute-start(bf16[4,512,128]{2,1,0:T(8,128)(2,1)S(1)} %get-tuple-element.36.refs_1_), channel_id=1, source_target_pairs={{0,8},{8,16},{16,24},{1,9},{9,17},{17,25},{2,10},{10,18},{18,26},{... | collective-permute-start | bytes 1572872 | tf_op jit(solution)/shard_map/ppermute | solution.py:382
  26.4 6.4 %collective-permute-start.8 = (bf16[1024,128]{1,0:T(8,128)(2,1)S(1)}, bf16[1024,128]{1,0:T(8,128)(2,1)S(1)}, u32[]{:S(2)}, u32[]{:S(2)}) collective-permute-start(bf16[1024,128]{1,0:T(8,128)(2,1)S(1)} %get-tuple-element.38), channel_id=1, source_target_pairs={{0,2},{2,0},{4,6},{6,4},{1,3},{3,1},{5,7},{7,5},{8,10},{10,8},{12,... | collective-permute-start | bytes 786440 | tf_op jit(solution)/shard_map/ppermute | solution.py:371
  28.0 16.5 %collective-permute-start.12 = (bf16[4,512,128]{2,1,0:T(8,128)(2,1)S(1)}, bf16[4,512,128]{2,1,0:T(8,128)(2,1)S(1)}, u32[]{:S(2)}, u32[]{:S(2)}) collective-permute-start(bf16[4,512,128]{2,1,0:T(8,128)(2,1)S(1)} %get-tuple-element.36.refs_1_), channel_id=1, source_target_pairs={{0,1},{1,0},{2,3},{3,2},{4,5},{5,4},{6,7},{7,6},{8,9},{9,8},{10,11... | collective-permute-start | bytes 1572872 | tf_op jit(solution)/shard_map/ppermute | solution.py:377
  28.1 20.6 %collective-permute-start.11 = (bf16[4,544,128]{2,1,0:T(8,128)(2,1)S(1)}, bf16[4,544,128]{2,1,0:T(8,128)(2,1)S(1)}, u32[]{:S(2)}, u32[]{:S(2)}) collective-permute-start(bf16[4,544,128]{2,1,0:T(8,128)(2,1)S(1)} %get-tuple-element.41.refs_7_), channel_id=1, source_target_pairs={{8,0},{16,8},{24,16},{9,1},{17,9},{25,17},{10,2},{18,10},{26,18},{... | collective-permute-start | bytes 1671176 | tf_op jit(solution)/shard_map/ppermute | solution.py:382
  30.4 14.1 %collective-permute-start.9 = (bf16[1024,128]{1,0:T(8,128)(2,1)S(1)}, bf16[1024,128]{1,0:T(8,128)(2,1)S(1)}, u32[]{:S(2)}, u32[]{:S(2)}) collective-permute-start(bf16[1024,128]{1,0:T(8,128)(2,1)S(1)} %get-tuple-element.39), channel_id=1, source_target_pairs={{0,4},{2,6},{4,0},{6,2},{1,5},{3,7},{5,1},{7,3},{8,12},{10,14},{12... | collective-permute-start | bytes 786440 | tf_op jit(solution)/shard_map/ppermute | solution.py:371
  32.9 11.6 %collective-permute-start.10 = (bf16[1024,128]{1,0:T(8,128)(2,1)S(1)}, bf16[1024,128]{1,0:T(8,128)(2,1)S(1)}, u32[]{:S(2)}, u32[]{:S(2)}) collective-permute-start(bf16[1024,128]{1,0:T(8,128)(2,1)S(1)} %get-tuple-element.40), channel_id=1, source_target_pairs={{0,6},{2,4},{4,2},{6,0},{1,7},{3,5},{5,3},{7,1},{8,14},{10,12},{12... | collective-permute-start | bytes 786440 | tf_op jit(solution)/shard_map/ppermute | solution.py:371
  36.4 12.3 %collective-permute-start.6 = (bf16[4,512,128]{2,1,0:T(8,128)(2,1)S(1)}, bf16[4,512,128]{2,1,0:T(8,128)(2,1)S(1)}, u32[]{:S(2)}, u32[]{:S(2)}) collective-permute-start(bf16[4,512,128]{2,1,0:T(8,128)(2,1)S(1)} %collective-permute-done.5.refs_1_), channel_id=1, source_target_pairs={{0,1},{1,0},{2,3},{3,2},{4,5},{5,4},{6,7},{7,6},{8,9},{9,8},{10,11... | collective-permute-start | bytes 1572872 | tf_op jit(solution)/shard_map/ppermute | solution.py:377
  57.8 2.5 %collective-permute-start.21 = (bf16[4,512,128]{2,1,0:T(8,128)(2,1)S(1)}, bf16[4,512,128]{2,1,0:T(8,128)(2,1)S(1)}, u32[]{:S(2)}, u32[]{:S(2)}) collective-permute-start(bf16[4,512,128]{2,1,0:T(8,128)(2,1)S(1)} %get-tuple-element.56), channel_id=1, source_target_pairs={{0,1},{1,0},{2,3},{3,2},{4,5},{5,4},{6,7},{7,6},{8,9},{9,8},{10,11... | collective-permute-start | bytes 1572872 | tf_op jit(solution)/shard_map/ppermute | solution.py:377
  57.9 14.9 %collective-permute-start.17 = (bf16[4,512,128]{2,1,0:T(8,128)(2,1)S(1)}, bf16[4,512,128]{2,1,0:T(8,128)(2,1)S(1)}, u32[]{:S(2)}, u32[]{:S(2)}) collective-permute-start(bf16[4,512,128]{2,1,0:T(8,128)(2,1)S(1)} %get-tuple-element.50), channel_id=1, source_target_pairs={{0,1},{1,0},{2,3},{3,2},{4,5},{5,4},{6,7},{7,6},{8,9},{9,8},{10,11... | collective-permute-start | bytes 1572872 | tf_op jit(solution)/shard_map/ppermute | solution.py:377
  58.4 18.1 %collective-permute-start.13 = (bf16[4,2,128,256]{3,2,1,0:T(8,128)(2,1)S(1)}, bf16[4,2,128,256]{3,2,1,0:T(8,128)(2,1)S(1)}, u32[]{:S(2)}, u32[]{:S(2)}) collective-permute-start(bf16[4,2,128,256]{3,2,1,0:T(8,128)(2,1)S(1)} %get-tuple-element.44), channel_id=1, source_target_pairs={{0,8},{8,16},{16,24},{1,9},{9,17},{17,25},{2,10},{10,18},{18,26},{... | collective-permute-start | bytes 1572872 | tf_op jit(solution)/shard_map/ppermute | solution.py:382
  60.4 6.4 %collective-permute-start.22 = (bf16[512,128]{1,0:T(8,128)(2,1)S(1)}, bf16[512,128]{1,0:T(8,128)(2,1)S(1)}, u32[]{:S(2)}, u32[]{:S(2)}) collective-permute-start(bf16[512,128]{1,0:T(8,128)(2,1)S(1)} %get-tuple-element.58), channel_id=1, source_target_pairs={{0,2},{2,0},{4,6},{6,4},{1,3},{3,1},{5,7},{7,5},{8,10},{10,8},{12,... | collective-permute-start | bytes 393224 | tf_op jit(solution)/shard_map/ppermute | solution.py:371
  61.0 8.0 %collective-permute-start.23 = (bf16[512,128]{1,0:T(8,128)(2,1)S(1)}, bf16[512,128]{1,0:T(8,128)(2,1)S(1)}, u32[]{:S(2)}, u32[]{:S(2)}) collective-permute-start(bf16[512,128]{1,0:T(8,128)(2,1)S(1)} %get-tuple-element.59), channel_id=1, source_target_pairs={{0,4},{2,6},{4,0},{6,2},{1,5},{3,7},{5,1},{7,3},{8,12},{10,14},{12... | collective-permute-start | bytes 393224 | tf_op jit(solution)/shard_map/ppermute | solution.py:371
  62.2 6.8 %collective-permute-start.24 = (bf16[512,128]{1,0:T(8,128)(2,1)S(1)}, bf16[512,128]{1,0:T(8,128)(2,1)S(1)}, u32[]{:S(2)}, u32[]{:S(2)}) collective-permute-start(bf16[512,128]{1,0:T(8,128)(2,1)S(1)} %get-tuple-element.60), channel_id=1, source_target_pairs={{0,6},{2,4},{4,2},{6,0},{1,7},{3,5},{5,3},{7,1},{8,14},{10,12},{12... | collective-permute-start | bytes 393224 | tf_op jit(solution)/shard_map/ppermute | solution.py:371
  69.1 20.1 %collective-permute-start.25 = (bf16[4,512,128]{2,1,0:T(8,128)(2,1)S(1)}, bf16[4,512,128]{2,1,0:T(8,128)(2,1)S(1)}, u32[]{:S(2)}, u32[]{:S(2)}) collective-permute-start(bf16[4,512,128]{2,1,0:T(8,128)(2,1)S(1)} %shard_map.120), channel_id=1, source_target_pairs={{8,0},{16,8},{24,16},{9,1},{17,9},{25,17},{10,2},{18,10},{26,18},{... | collective-permute-start | bytes 1572872 | tf_op jit(solution)/shard_map/ppermute | solution.py:382
  72.9 6.4 %collective-permute-start.18 = (bf16[512,128]{1,0:T(8,128)(2,1)S(1)}, bf16[512,128]{1,0:T(8,128)(2,1)S(1)}, u32[]{:S(2)}, u32[]{:S(2)}) collective-permute-start(bf16[512,128]{1,0:T(8,128)(2,1)S(1)} %get-tuple-element.52), channel_id=1, source_target_pairs={{0,2},{2,0},{4,6},{6,4},{1,3},{3,1},{5,7},{7,5},{8,10},{10,8},{12,... | collective-permute-start | bytes 393224 | tf_op jit(solution)/shard_map/ppermute | solution.py:371
  74.4 8.9 %collective-permute-start.19 = (bf16[512,128]{1,0:T(8,128)(2,1)S(1)}, bf16[512,128]{1,0:T(8,128)(2,1)S(1)}, u32[]{:S(2)}, u32[]{:S(2)}) collective-permute-start(bf16[512,128]{1,0:T(8,128)(2,1)S(1)} %get-tuple-element.53), channel_id=1, source_target_pairs={{0,4},{2,6},{4,0},{6,2},{1,5},{3,7},{5,1},{7,3},{8,12},{10,14},{12... | collective-permute-start | bytes 393224 | tf_op jit(solution)/shard_map/ppermute | solution.py:371
  75.0 8.4 %collective-permute-start.20 = (bf16[512,128]{1,0:T(8,128)(2,1)S(1)}, bf16[512,128]{1,0:T(8,128)(2,1)S(1)}, u32[]{:S(2)}, u32[]{:S(2)}) collective-permute-start(bf16[512,128]{1,0:T(8,128)(2,1)S(1)} %get-tuple-element.54), channel_id=1, source_target_pairs={{0,6},{2,4},{4,2},{6,0},{1,7},{3,5},{5,3},{7,1},{8,14},{10,12},{12... | collective-permute-start | bytes 393224 | tf_op jit(solution)/shard_map/ppermute | solution.py:371
  76.7 7.8 %collective-permute-start.14 = (bf16[512,128]{1,0:T(8,128)(2,1)S(1)}, bf16[512,128]{1,0:T(8,128)(2,1)S(1)}, u32[]{:S(2)}, u32[]{:S(2)}) collective-permute-start(bf16[512,128]{1,0:T(8,128)(2,1)S(1)} %get-tuple-element.46), channel_id=1, source_target_pairs={{0,2},{2,0},{4,6},{6,4},{1,3},{3,1},{5,7},{7,5},{8,10},{10,8},{12,... | collective-permute-start | bytes 393224 | tf_op jit(solution)/shard_map/ppermute | solution.py:371
  79.3 5.7 %collective-permute-start.15 = (bf16[512,128]{1,0:T(8,128)(2,1)S(1)}, bf16[512,128]{1,0:T(8,128)(2,1)S(1)}, u32[]{:S(2)}, u32[]{:S(2)}) collective-permute-start(bf16[512,128]{1,0:T(8,128)(2,1)S(1)} %get-tuple-element.47), channel_id=1, source_target_pairs={{0,4},{2,6},{4,0},{6,2},{1,5},{3,7},{5,1},{7,3},{8,12},{10,14},{12... | collective-permute-start | bytes 393224 | tf_op jit(solution)/shard_map/ppermute | solution.py:371
  83.4 5.9 %collective-permute-start.16 = (bf16[512,128]{1,0:T(8,128)(2,1)S(1)}, bf16[512,128]{1,0:T(8,128)(2,1)S(1)}, u32[]{:S(2)}, u32[]{:S(2)}) collective-permute-start(bf16[512,128]{1,0:T(8,128)(2,1)S(1)} %get-tuple-element.48), channel_id=1, source_target_pairs={{0,6},{2,4},{4,2},{6,0},{1,7},{3,5},{5,3},{7,1},{8,14},{10,12},{12... | collective-permute-start | bytes 393224 | tf_op jit(solution)/shard_map/ppermute | solution.py:371

commit v4 on v3

--- a/solution.py
+++ b/solution.py
@@ -151,10 +151,11 @@
                 out[at : at + tokens, :] = columns(ref, first + g)[...]
 
 
-def ordered_kernel(me, *refs):
+def stack_kernel(me, *refs):
     pieces, out = refs[:-1], refs[-1]
-    for mask, piece in enumerate(pieces):
-        out[me[0] ^ mask] = piece[...]
+    rows = pieces[0].shape[0]
+    for n, piece in enumerate(pieces):
+        out[n * rows : (n + 1) * rows, :] = piece[...]
 
 
 def assemble_kernel(plan, me, lse_ref, *refs):
@@ -176,10 +177,12 @@
         do_out[chip, plan.q_rows :, :] = padded_rows(terms, plan.aux)
 
 
-def merge_kernel(me, keep_ref, given_ref, *pieces):
-    for mask, out in enumerate(pieces):
-        chip = me[0] ^ mask
-        out[...] = (keep_ref[chip] + given_ref[chip].astype(F32)).astype(BF16)
+def merge_kernel(groups, me, keep_ref, given_ref, *outs):
+    for group, out in zip(groups, outs):
+        rows = keep_ref.shape[1]
+        for n, mask in enumerate(group):
+            chip = me[0] ^ mask
+            out[n * rows : (n + 1) * rows, :] = (keep_ref[chip] + given_ref[chip].astype(F32)).astype(BF16)
 
 
 def lane_row(parts, tokens):
@@ -190,27 +193,25 @@
     return row
 
 
-def role_kernel(plan, at_level, has_dq, me, code_ref, mine_ref, sib_ref, *refs):
+def role_kernel(plan, level, has_dq, has_dkv, last, me, code_ref, mine_ref, sib_ref, *refs):
     refs = list(refs)
-    levels, chips = len(has_dq), plan.chips
-    q_pieces = [refs.pop(0) for _ in range(chips)]
-    do_refs = [refs.pop(0) for _ in range(levels)]
-    dq_ins = [refs.pop(0) if has else None for has in has_dq]
-    dq_outs = [refs.pop(0) for _ in range(levels)]
-    keep, give, kv_ref, q_ref, do_ref, dq_ref, dkv_ref = refs
+    q_pieces = [refs.pop(0) for _ in range(plan.chips)]
+    do_ref = refs.pop(0)
+    dq_in = refs.pop(0) if has_dq else None
+    dkv_in = refs.pop(0) if has_dkv else None
+    dq_out, dkv_outs, (kv_ref, q_ref, dq_sum, dkv_sum) = refs[0], refs[1:-4], refs[-4:]
+    dq_ref = dq_out if dq_out.dtype == F32 else dq_sum
+    dkv_ref = dkv_sum if last else dkv_outs[0]
     core = me[1]
     tokens, n_x, fold = plan.tokens, plan.n_x, plan.fold
     q_per = QUERY_TILE // tokens
     k_per = KEY_TILE // tokens
     kv_ref[core] = mine_ref[...]
     kv_ref[1 - core] = sib_ref[...]
-    dkv_ref[...] = jnp.zeros_like(dkv_ref)
-    for level in range(levels):
-        for mask in range(chips):
-            first = at_level[level] * plan.q_rows
-            q_ref[level, me[0] ^ mask] = q_pieces[mask][first : first + plan.q_rows, :]
-        do_ref[level] = do_refs[level][...]
-        dq_ref[level] = dq_ins[level][...] if has_dq[level] else jnp.zeros_like(dq_outs[level], F32)
+    dkv_ref[...] = dkv_in[...] if has_dkv else jnp.zeros_like(dkv_ref)
+    dq_ref[...] = dq_in[...] if has_dq else jnp.zeros_like(dq_ref)
+    for mask, piece in enumerate(q_pieces):
+        q_ref[me[0] ^ mask] = piece[level * plan.q_rows : (level + 1) * plan.q_rows, :]
 
     def q_start(q_in):
         return (q_in * q_per * CORES + core) * tokens
@@ -218,14 +219,14 @@
     def q_end(q_in):
         return ((q_in * q_per + q_per - 1) * CORES + core) * tokens + tokens - 1
 
-    last = (((1,), (1,)), ((), ()))
-
-    def row(level, query_block, q_in, key_block, k_tiles, code, masked):
+    rows_by_rows = (((1,), (1,)), ((), ()))
+
+    def row(query_block, q_in, key_block, k_tiles, code, masked):
         q_chip = query_block * n_x + q_in * q_per
         tile = query_block * plan.q_tiles + q_in
 
         def q_part(ref, g):
-            return [ref[level, q_chip + n, g * tokens : (g + 1) * tokens, :] for n in range(q_per)]
+            return [ref[q_chip + n, g * tokens : (g + 1) * tokens, :] for n in range(q_per)]
 
         def k_place(k_in):
             return [
@@ -236,7 +237,7 @@
             at = (which * plan.kv_heads + h) * tokens
             return jnp.concatenate([kv_ref[c, chip, at : at + tokens, :] for c, chip in k_place(k_in)], axis=0)
 
-        groups = [do_ref[level, q_chip + n, plan.q_rows :, :].astype(F32) for n in range(q_per)]
+        groups = [do_ref[q_chip + n, plan.q_rows :, :].astype(F32) for n in range(q_per)]
 
         def aux(which, g):
             at = (which * plan.q_heads + g) * 3
@@ -256,8 +257,8 @@
             h, k_in = unit
             q2, do2, _, _ = queries[h]
             k, v = k_part(0, h, k_in), k_part(1, h, k_in)
-            scores = lax.dot_general(k, q2, last, preferred_element_type=F32)
-            dprobs = lax.dot_general(v, do2, last, preferred_element_type=F32)
+            scores = lax.dot_general(k, q2, rows_by_rows, preferred_element_type=F32)
+            dprobs = lax.dot_general(v, do2, rows_by_rows, preferred_element_type=F32)
             return k, scores, dprobs
 
         def back(unit, ready):
@@ -286,17 +287,15 @@
         ready = front(units[0])
         for n, unit in enumerate(units):
             following = front(units[n + 1]) if n + 1 < len(units) else None
-            dq_ref[level, tile, unit[0]] += back(unit, ready)
+            dq_ref[tile, unit[0]] += back(unit, ready)
             ready = following
 
     def step(index, carry):
         q_in = index % plan.q_tiles
         rest = index // plan.q_tiles
         key_block = rest % fold
-        rest = rest // fold
-        query_block = rest % fold
-        level = rest // fold
-        code = code_ref[level, query_block, key_block]
+        query_block = rest // fold
+        code = code_ref[query_block, key_block]
         q_first, q_last = q_start(q_in), q_end(q_in)
         every = tuple(range(plan.k_tiles))
         below = (q_last < (plan.k_tiles - 1) * KEY_TILE) & (code == 2)
@@ -304,23 +303,25 @@
 
         @pl.when(code == 1)
         def _():
-            row(level, query_block, q_in, key_block, every, code, False)
+            row(query_block, q_in, key_block, every, code, False)
 
         @pl.when(below | above)
         def _():
-            row(level, query_block, q_in, key_block, (jnp.where(below, 0, plan.k_tiles - 1),), code, True)
+            row(query_block, q_in, key_block, (jnp.where(below, 0, plan.k_tiles - 1),), code, True)
 
         @pl.when((code >= 2) & jnp.logical_not(below | above))
         def _():
-            row(level, query_block, q_in, key_block, every, code, True)
+            row(query_block, q_in, key_block, every, code, True)
 
         return carry
 
-    lax.fori_loop(0, levels * fold * fold * plan.q_tiles, step, 0)
-    for level in range(levels):
-        dq_outs[level][...] = dq_ref[level].astype(dq_outs[level].dtype)
-    keep[...] = dkv_ref[core]
-    give[...] = dkv_ref[1 - core].astype(BF16)
+    lax.fori_loop(0, fold * fold * plan.q_tiles, step, 0)
+    if dq_out.dtype != F32:
+        dq_out[...] = dq_ref[...].astype(dq_out.dtype)
+    if last:
+        keep, give = dkv_outs
+        keep[...] = dkv_ref[core]
+        give[...] = dkv_ref[1 - core].astype(BF16)
 
 
 def finish_kernel(plan, has_far, me, dq_ref, *refs):
@@ -344,33 +345,49 @@
         out[...] = rows_ref[me[0] ^ mask]
 
 
-def unpack_kernel(plan, has_far, me, *refs):
+def unpack_kernel(plan, levels, me, *refs):
     refs = list(refs)
+    direct, by_way = routes(plan.chips)
     dq_pieces = [refs.pop(0) for _ in range(plan.chips)]
-    kv_pieces = [refs.pop(0) for _ in range(plan.chips)]
-    far_ref = refs.pop(0) if has_far else None
+    near = [refs.pop(0) for _ in range(plan.chips)]
+    far = {mask: [] for mask in range(plan.chips)}
+    for _ in range(levels - 1):
+        for mask in direct:
+            far[mask].append((refs.pop(0), 0))
+        both = refs.pop(0)
+        for n, mask in enumerate(by_way):
+            far[mask].append((both, n * plan.kv_rows))
     dq_ref, dk_ref, dv_ref = refs
     tokens = plan.tokens
     for mask in range(plan.chips):
-        chip = me[0] ^ mask
-        kv_head = plan.first_kv_head(chip)
+        kv_head = plan.first_kv_head(me[0] ^ mask)
         for g in range(plan.q_heads):
             columns(dq_ref, kv_head * GROUP + g)[...] = dq_pieces[mask][g * tokens : (g + 1) * tokens, :]
-        total = kv_pieces[mask][...]
-        if has_far:
-            total = (total.astype(F32) + far_ref[chip].astype(F32)).astype(BF16)
+        total = near[mask][...]
+        if far[mask]:
+            total = total.astype(F32)
+            for ref, at in far[mask]:
+                total = total + ref[at : at + plan.kv_rows, :].astype(F32)
+            total = total.astype(BF16)
         for h in range(plan.kv_heads):
             columns(dk_ref, kv_head + h)[...] = total[h * tokens : (h + 1) * tokens]
             at = (plan.kv_heads + h) * tokens
             columns(dv_ref, kv_head + h)[...] = total[at : at + tokens]
 
 
+def routes(chips):
+    by_way = [mask for mask in range(chips) if mask.bit_count() == 1]
+    return [mask for mask in range(chips) if mask not in by_way], by_way
+
+
+def send_in_plane(piece, mask, chips):
+    if mask == 0:
+        return piece
+    return lax.ppermute(piece, CROSS, [(i, i ^ mask) for i in range(chips)])
+
+
 def exchange(pieces):
-    chips = len(pieces)
-    return [pieces[0]] + [
-        lax.ppermute(pieces[mask], CROSS, [(i, i ^ mask) for i in range(chips)])
-        for mask in range(1, chips)
-    ]
+    return [send_in_plane(piece, mask, len(pieces)) for mask, piece in enumerate(pieces)]
 
 
 def swap(value):
@@ -383,7 +400,7 @@
 
 
 def query_levels(level, reach):
-    return [d - level for d in (2 * level - 1, 2 * level) if 0 <= d <= reach]
+    return [d - level for d in (2 * level, 2 * level - 1) if 0 <= d <= reach]
 
 
 def plane_logsum(logsum, plan, y, core):
@@ -445,51 +462,61 @@
     up = [(kv, swap(kv)) for kv in up]
 
     grad_q = [None] * len(raw)
-    grad_kv = []
+    near_kv, far_kv = None, []
     dq_shape = (fold * plan.q_tiles, plan.kv_heads, HEAD_SIZE, GROUP * QUERY_TILE)
+    dkv_shape = (CORES, chips, plan.kv_rows, LANES)
     inside = jnp.arange(fold, dtype=jnp.int32)
+    cases = [(i, j) for i in range(len(up)) for j in query_levels(i, reach)]
+    query_blocks = (z + jnp.array([j for _, j in cases], jnp.int32)[:, None]) * fold + inside
+    key_blocks = (z - jnp.array([i for i, _ in cases], jnp.int32)[:, None]) * fold + inside
+    listed = pair_list[:, :, None, None, None]
+    hit = (listed[:, 0] == query_blocks[:, :, None]) & (listed[:, 1] == key_blocks[:, None, :])
+    codes = jnp.sum(jnp.where(hit, listed[:, 2] + 1, 0), axis=0).astype(jnp.int32)
+    direct, by_way = routes(chips)
     for i, (mine, sibling) in enumerate(up):
         levels = query_levels(i, reach)
-        query_blocks = (z + jnp.array(levels, jnp.int32)[:, None]) * fold + inside
-        key_blocks = (z - i) * fold + inside
-        row = pair_list[:, :, None, None, None]
-        hit = (row[:, 0] == query_blocks[:, :, None]) & (row[:, 1] == key_blocks)
-        codes = jnp.sum(jnp.where(hit, row[:, 2] + 1, 0), axis=0).astype(jnp.int32)
-        has_dq = tuple(grad_q[j] is not None for j in levels)
-        over = [j and j not in query_levels(i + 1, reach) for j in levels]
-        *parts, keep, give = call(
-            functools.partial(role_kernel, plan, tuple(levels), has_dq),
-            [jax.ShapeDtypeStruct(dq_shape, BF16 if done else F32) for done in over]
-            + [stacked(plan.kv_rows, F32), stacked(plan.kv_rows)],
-            [SCALARS] + [WHOLE] * (2 + chips + len(levels) + sum(has_dq)),
-            flops=10 * len(levels) * fold * fold * plan.q_heads * plan.block * plan.block * HEAD_SIZE // CORES,
-            scratch=[
-                pltpu.VMEM((CORES, chips, plan.kv_rows, LANES), BF16),
-                pltpu.VMEM((len(levels), chips, plan.q_rows, LANES), BF16),
-                pltpu.VMEM((len(levels), chips, plan.q_rows + plan.aux, LANES), BF16),
-                pltpu.VMEM((len(levels),) + dq_shape, F32),
-                pltpu.VMEM((CORES, chips, plan.kv_rows, LANES), F32),
-            ],
-        )(
-            codes,
-            mine,
-            sibling,
-            *q_pieces,
-            *[far_do[j] for j in levels],
-            *[grad_q[j] for j in levels if grad_q[j] is not None],
-        )
-        for j, part in zip(levels, parts):
-            grad_q[j] = part
-        merged = call(merge_kernel, [like(plan.kv_rows)] * chips, [WHOLE] * 2)(keep, swap(give))
-        grad_kv.append(exchange(merged))
+        carried = None
+        for j in levels:
+            has_dq, last = grad_q[j] is not None, j == levels[-1]
+            done = j and j not in query_levels(i + 1, reach)
+            dkv_outs = (
+                [stacked(plan.kv_rows, F32), stacked(plan.kv_rows)]
+                if last
+                else [jax.ShapeDtypeStruct(dkv_shape, F32)]
+            )
+            given = [g for g in (grad_q[j], carried) if g is not None]
+            grad_q[j], *dkv = call(
+                functools.partial(role_kernel, plan, j, has_dq, carried is not None, last),
+                [jax.ShapeDtypeStruct(dq_shape, BF16 if done else F32)] + dkv_outs,
+                [SCALARS] + [WHOLE] * (3 + chips + len(given)),
+                flops=10 * fold * fold * plan.q_heads * plan.block * plan.block * HEAD_SIZE // CORES,
+                scratch=[
+                    pltpu.VMEM(dkv_shape, BF16),
+                    pltpu.VMEM((chips, plan.q_rows, LANES), BF16),
+                    pltpu.VMEM(dq_shape, F32),
+                    pltpu.VMEM(dkv_shape, F32),
+                ],
+            )(codes[cases.index((i, j))], mine, sibling, *q_pieces, far_do[j], *given)
+            carried = dkv[0]
+        keep, give = dkv
+        groups = [direct] + [[m] for m in by_way] if i else [[m] for m in range(chips)]
+        merged = call(
+            functools.partial(merge_kernel, groups), [like(len(group) * plan.kv_rows) for group in groups], [WHOLE] * 2
+        )(keep, swap(give))
+        if i == 0:
+            near_kv = exchange(merged)
+            continue
+        first = along(merged[0], planes, -i)
+        for n, mask in enumerate(direct):
+            piece = first[n * plan.kv_rows : (n + 1) * plan.kv_rows]
+            far_kv.append(send_in_plane(piece, mask, chips))
+        pair = [send_in_plane(p, m, chips) for p, m in zip(merged[1:], by_way)]
+        both = call(stack_kernel, like(len(by_way) * plan.kv_rows), [WHOLE] * len(by_way))(*pair)
+        far_kv.append(along(both, planes, -i))
 
     def plus(part, far):
         return part if far is None else (part.astype(F32) + far.astype(F32)).astype(BF16)
 
-    far_kv = None
-    for level in range(len(grad_kv) - 1, 0, -1):
-        part = call(ordered_kernel, stacked(plan.kv_rows), [WHOLE] * chips)(*grad_kv[level])
-        far_kv = along(plus(part, far_kv), planes, -1)
     far_q = None
     for level in range(len(grad_q) - 1, 0, -1):
         far_q = along(plus(grad_q[level], far_q), planes, 1)
@@ -501,14 +528,14 @@
     )(grad_q[0], *([] if far_q is None else [far_q]))
     return tuple(
         call(
-            functools.partial(unpack_kernel, plan, far_kv is not None),
+            functools.partial(unpack_kernel, plan, len(up)),
             [
                 jax.ShapeDtypeStruct((plan.tokens, QUERY_HEADS * HEAD_SIZE), BF16),
                 jax.ShapeDtypeStruct((plan.tokens, KEY_VALUE_HEADS * HEAD_SIZE), BF16),
                 jax.ShapeDtypeStruct((plan.tokens, KEY_VALUE_HEADS * HEAD_SIZE), BF16),
             ],
-            [WHOLE] * (2 * chips + (far_kv is not None)),
-        )(*exchange(dq_pieces), *grad_kv[0], *([] if far_kv is None else [far_kv]))
+            [WHOLE] * (2 * chips + len(far_kv)),
+        )(*exchange(dq_pieces), *near_kv, *far_kv)
     )
 
 

time: 90.7 us -> 92.4 us (1.019)
  the two profiles are of different devices: /device:TPU:18 before, /device:TPU:24 now
where the time goes in v4:
time: 92.4 us; the launch traced here: 91.6 us
  starting transfers between devices  39.4 us (43%)
  waiting for transfers between devices  31.2 us (34%)
  Pallas kernels  15.7 us (17%)
  other arithmetic  3.45 us (4%)
  local copies, waits for them, and re-layouts  0.98 us (1%)
    ppermute x15, waiting for transfers between devices, send_in_plane(): return lax.ppermute(piece, CROSS, [(i, i ^ mask) for i in range(chips)])  20.5 us
    ppermute x6, starting transfers between devices, along(): return lax.ppermute(value, 'z', pairs)  19 us
    ppermute x15, starting transfers between devices, send_in_plane(): return lax.ppermute(piece, CROSS, [(i, i ^ mask) for i in range(chips)])  18.3 us
    pallas_call x3, Pallas kernels, body(): call(functools.partial(role_kernel, plan, j, has_dq, carried is not None,...  10.7 us
    ppermute x6, waiting for transfers between devices, along(): return lax.ppermute(value, 'z', pairs)  9.49 us
    pallas_call x1, Pallas kernels, body(): call(functools.partial(pack_kernel, plan), [like(plan.q_rows + plan.kv_ro...  2.93 us
  transfers between devices with their start and end apart: 27, of which 8 were waited for; matrix products, arithmetic and copies ran while one was open for 4% of the time, Pallas kernels for 10%

profile of v4, /device:TPU:24, one launch (start us, length us, event | category | flops | bytes accessed | tf_op | source)
XLA Modules:
  0.0 91.6 jit_solution(10480905589161716478)
XLA Ops:
  0.6 1.6 %collective-permute-start = (f32[4,512]{1,0:T(4,128)}, f32[4,512]{1,0:T(4,128)S(1)}, u32[]{:S(2)}, u32[]{:S(2)}) collective-permute-start(f32[4,512]{1,0:T(4,128)} %param.14), channel_id=1, source_target_pairs={{0,4},{4,0},{1,5},{5,1},{2,6},{6,2},{3,7},{7,3},{8,12},{12,8},{9,1... | collective-permute-start | bytes 24584 | tf_op jit(solution)/shard_map/ppermute | solution.py:409
  2.2 2.4 %collective-permute-start.7 = (bf16[128,2048]{1,0:T(8,128)(2,1)}, bf16[128,2048]{1,0:T(8,128)(2,1)S(1)}, u32[]{:S(2)}, u32[]{:S(2)}) collective-permute-start(bf16[128,2048]{1,0:T(8,128)(2,1)} %refs_0_.3), channel_id=1, source_target_pairs={{8,0},{16,8},{24,16},{9,1},{17,9},{25,17},{10,2},{18,10},{26,18},{... | collective-permute-start | bytes 1572872 | tf_op jit(solution)/shard_map/ppermute | solution.py:399
  4.6 2.9 %shard_map.112 = (bf16[1040,128]{1,0:T(8,128)(2,1)}, bf16[1040,128]{1,0:T(8,128)(2,1)}, bf16[1040,128]{1,0:T(8,128)(2,1)}, bf16[1040,128]{1,0:T(8,128)(2,1)}) custom-call(bf16[128,2048]{1,0:T(8,128)(2,1)} %refs_0_.2, bf16[128,2048]{1,0:T(8,128)(2,1)} %refs_1_.1, bf16[128,1024]{1,0:T(8,128)(2,1)} %refs_2_.1, bf16[128,1024]{1,0:T(8,128)(2,1)} %refs_3_.1), custom_call_target="tpu_custom_call" | custom-call | bytes 4194304 | tf_op jit(solution)/shard_map/pallas_call | solution.py:439
  7.5 1.6 %collective-permute-start.2 = (bf16[1040,128]{1,0:T(8,128)(2,1)}, bf16[1040,128]{1,0:T(8,128)(2,1)S(1)}, u32[]{:S(2)}, u32[]{:S(2)}) collective-permute-start(bf16[1040,128]{1,0:T(8,128)(2,1)} %get-tuple-element.33), channel_id=1, source_target_pairs={{0,2},{2,0},{4,6},{6,4},{1,3},{3,1},{5,7},{7,5},{8,10},{10,8},{12,... | collective-permute-start | bytes 798728 | tf_op jit(solution)/shard_map/ppermute | solution.py:386
  9.1 0.5 collective-permute-start.3
  9.6 1.5 %collective-permute-start.4 = (bf16[1040,128]{1,0:T(8,128)(2,1)}, bf16[1040,128]{1,0:T(8,128)(2,1)S(1)}, u32[]{:S(2)}, u32[]{:S(2)}) collective-permute-start(bf16[1040,128]{1,0:T(8,128)(2,1)} %get-tuple-element.35), channel_id=1, source_target_pairs={{0,6},{2,4},{4,2},{6,0},{1,7},{3,5},{5,3},{7,1},{8,14},{10,12},{12... | collective-permute-start | bytes 798728 | tf_op jit(solution)/shard_map/ppermute | solution.py:386
  11.1 0.8 add_bitcast_fusion
  11.9 0.7 add_multiply_fusion
  12.6 0.7 pad_maximum_fusion
  13.4 1.1 %collective-permute-done.1 = f32[2,4,512]{2,1,0:T(4,128)S(1)} collective-permute-done((f32[2,4,512]{2,1,0:T(4,128)S(1)}, f32[2,4,512]{2,1,0:T(4,128)S(1)}, u32[]{:S(2)}, u32[]{:S(2)}) %collective-permute-start.1) | collective-permute-done | bytes 16416 | tf_op jit(solution)/shard_map/ppermute | solution.py:394
  14.5 0.8 fusion.1.refs_0_
  15.3 1.8 %collective-permute-done.2.refs_2_ = bf16[1040,128]{1,0:T(8,128)(2,1)S(1)} collective-permute-done((bf16[1040,128]{1,0:T(8,128)(2,1)}, bf16[1040,128]{1,0:T(8,128)(2,1)S(1)}, u32[]{:S(2)}, u32[]{:S(2)}) %collective-permute-start.2) | collective-permute-done | bytes 266272 | tf_op jit(solution)/shard_map/ppermute | solution.py:386
  17.1 5.2 %collective-permute-done.3.refs_3_ = bf16[1040,128]{1,0:T(8,128)(2,1)S(1)} collective-permute-done((bf16[1040,128]{1,0:T(8,128)(2,1)}, bf16[1040,128]{1,0:T(8,128)(2,1)S(1)}, u32[]{:S(2)}, u32[]{:S(2)}) %collective-permute-start.3) | collective-permute-done | bytes 266272 | tf_op jit(solution)/shard_map/ppermute | solution.py:386
  22.3 1.0 %copy-done.1 = bf16[1040,128]{1,0:T(8,128)(2,1)S(1)} copy-done((bf16[1040,128]{1,0:T(8,128)(2,1)S(1)}, bf16[1040,128]{1,0:T(8,128)(2,1)}, u32[]{:S(2)}) %copy-start.1) | copy-done | bytes 266264
  23.3 0.1 shard_map.113
  23.4 1.3 %collective-permute-start.5 = (bf16[4,512,128]{2,1,0:T(8,128)(2,1)S(1)}, bf16[4,512,128]{2,1,0:T(8,128)(2,1)S(1)}, u32[]{:S(2)}, u32[]{:S(2)}) collective-permute-start(bf16[4,512,128]{2,1,0:T(8,128)(2,1)S(1)} %get-tuple-element.36.refs_1_), channel_id=1, source_target_pairs={{0,8},{8,16},{16,24},{1,9},{9,17},{17,25},{2,10},{10,18},{18,26},{... | collective-permute-start | bytes 1572872 | tf_op jit(solution)/shard_map/ppermute | solution.py:399
  24.7 0.1 broadcast_compare_fusion
  24.8 0.3 shard_map.114
  25.1 0.6 collective-permute-start.8
  25.8 4.6 %collective-permute-start.12 = (bf16[4,544,128]{2,1,0:T(8,128)(2,1)S(1)}, bf16[4,544,128]{2,1,0:T(8,128)(2,1)S(1)}, u32[]{:S(2)}, u32[]{:S(2)}) collective-permute-start(bf16[4,544,128]{2,1,0:T(8,128)(2,1)S(1)} %get-tuple-element.41.refs_7_), channel_id=1, source_target_pairs={{8,0},{16,8},{24,16},{9,1},{17,9},{25,17},{10,2},{18,10},{26,18},{... | collective-permute-start | bytes 1671176 | tf_op jit(solution)/shard_map/ppermute | solution.py:399
  30.4 1.3 %collective-permute-start.9 = (bf16[1024,128]{1,0:T(8,128)(2,1)S(1)}, bf16[1024,128]{1,0:T(8,128)(2,1)S(1)}, u32[]{:S(2)}, u32[]{:S(2)}) collective-permute-start(bf16[1024,128]{1,0:T(8,128)(2,1)S(1)} %get-tuple-element.39), channel_id=1, source_target_pairs={{0,4},{2,6},{4,0},{6,2},{1,5},{3,7},{5,1},{7,3},{8,12},{10,14},{12... | collective-permute-start | bytes 786440 | tf_op jit(solution)/shard_map/ppermute | solution.py:386
  31.7 1.8 %collective-permute-start.10 = (bf16[1024,128]{1,0:T(8,128)(2,1)S(1)}, bf16[1024,128]{1,0:T(8,128)(2,1)S(1)}, u32[]{:S(2)}, u32[]{:S(2)}) collective-permute-start(bf16[1024,128]{1,0:T(8,128)(2,1)S(1)} %get-tuple-element.40), channel_id=1, source_target_pairs={{0,6},{2,4},{4,2},{6,0},{1,7},{3,5},{5,3},{7,1},{8,14},{10,12},{12... | collective-permute-start | bytes 786440 | tf_op jit(solution)/shard_map/ppermute | solution.py:386
  33.4 2.9 %collective-permute-done.5.refs_1_ = bf16[4,512,128]{2,1,0:T(8,128)(2,1)S(1)} collective-permute-done((bf16[4,512,128]{2,1,0:T(8,128)(2,1)S(1)}, bf16[4,512,128]{2,1,0:T(8,128)(2,1)S(1)}, u32[]{:S(2)}, u32[]{:S(2)}) %collective-permute-start.5) | collective-permute-done | bytes 524320 | tf_op jit(solution)/shard_map/ppermute | solution.py:399
  36.3 0.2 fusion.5
  36.5 8.0 %collective-permute-done.9.refs_5_ = bf16[1024,128]{1,0:T(8,128)(2,1)S(1)} collective-permute-done((bf16[1024,128]{1,0:T(8,128)(2,1)S(1)}, bf16[1024,128]{1,0:T(8,128)(2,1)S(1)}, u32[]{:S(2)}, u32[]{:S(2)}) %collective-permute-start.9) | collective-permute-done | bytes 262176 | tf_op jit(solution)/shard_map/ppermute | solution.py:386
  44.5 5.5 %shard_map.115 = (f32[4,2,128,256]{3,2,1,0:T(8,128)S(1)}, f32[4,512,128]{2,1,0:T(8,128)S(1)}, bf16[4,512,128]{2,1,0:T(8,128)(2,1)S(1)}) custom-call(s32[2,2]{1,0:T(2,128)S(1)} %get-tuple-element.64.refs_0_, bf16[4,512,128]{2,1,0:T(8,128)(2,1)S(1)} %get-tuple-element.36.refs_1_, bf16[4,512,128]{2,1,0:T(8,128)(2,1)S(1)} %collective-permute-done.11.refs_2_, ...), custom_call_target="tpu_custom_call" | custom-call | flops 2684354560 | bytes 4194304 | tf_op jit(solution)/shard_map/pallas_call | solution.py:488
  50.1 1.2 %shard_map.116 = (bf16[4,2,128,256]{3,2,1,0:T(8,128)(2,1)S(1)}, f32[2,4,512,128]{3,2,1,0:T(8,128)S(1)}) custom-call(s32[2,2]{1,0:T(2,128)S(1)} %get-tuple-element.63.refs_0_, bf16[4,512,128]{2,1,0:T(8,128)(2,1)S(1)} %collective-permute-done.5.refs_1_, bf16[4,512,128]{2,1,0:T(8,128)(2,1)S(1)} %collective-permute-done.6.refs_2_, ...), custom_call_target="tpu_custom_call" | custom-call | flops 2684354560 | bytes 4194304 | tf_op jit(solution)/shard_map/pallas_call | solution.py:488
  51.3 4.0 %shard_map.117 = (f32[4,2,128,256]{3,2,1,0:T(8,128)S(1)}, f32[4,512,128]{2,1,0:T(8,128)S(1)}, bf16[4,512,128]{2,1,0:T(8,128)(2,1)S(1)}) custom-call(s32[2,2]{1,0:T(2,128)S(1)} %get-tuple-element.65.refs_0_, bf16[4,512,128]{2,1,0:T(8,128)(2,1)S(1)} %collective-permute-done.5.refs_1_, bf16[4,512,128]{2,1,0:T(8,128)(2,1)S(1)} %collective-permute-done.6.refs_2_, ...), custom_call_target="tpu_custom_call" | custom-call | flops 2684354560 | bytes 4194304 | tf_op jit(solution)/shard_map/pallas_call | solution.py:488
  55.4 0.5 collective-permute-start.17
  55.9 1.3 %collective-permute-start.13 = (bf16[4,2,128,256]{3,2,1,0:T(8,128)(2,1)S(1)}, bf16[4,2,128,256]{3,2,1,0:T(8,128)(2,1)S(1)}, u32[]{:S(2)}, u32[]{:S(2)}) collective-permute-start(bf16[4,2,128,256]{3,2,1,0:T(8,128)(2,1)S(1)} %get-tuple-element.45), channel_id=1, source_target_pairs={{0,8},{8,16},{16,24},{1,9},{9,17},{17,25},{2,10},{10,18},{18,26},{... | collective-permute-start | bytes 1572872 | tf_op jit(solution)/shard_map/ppermute | solution.py:399
  57.2 0.1 collective-permute-done.21.refs_1_
  57.3 0.1 shard_map.120
  57.4 5.8 %collective-permute-start.22 = (bf16[1024,128]{1,0:T(8,128)(2,1)S(1)}, bf16[1024,128]{1,0:T(8,128)(2,1)S(1)}, u32[]{:S(2)}, u32[]{:S(2)}) collective-permute-start(bf16[1024,128]{1,0:T(8,128)(2,1)S(1)} %get-tuple-element.58), channel_id=1, source_target_pairs={{8,0},{16,8},{24,16},{9,1},{17,9},{25,17},{10,2},{18,10},{26,18},{... | collective-permute-start | bytes 786440 | tf_op jit(solution)/shard_map/ppermute | solution.py:399
  63.2 1.6 %collective-permute-start.24 = (bf16[512,128]{1,0:T(8,128)(2,1)S(1)}, bf16[512,128]{1,0:T(8,128)(2,1)S(1)}, u32[]{:S(2)}, u32[]{:S(2)}) collective-permute-start(bf16[512,128]{1,0:T(8,128)(2,1)S(1)} %get-tuple-element.59), channel_id=1, source_target_pairs={{0,2},{2,0},{4,6},{6,4},{1,3},{3,1},{5,7},{7,5},{8,10},{10,8},{12,... | collective-permute-start | bytes 393224 | tf_op jit(solution)/shard_map/ppermute | solution.py:386
  64.7 0.5 collective-permute-start.25
  65.2 0.1 shard_map.119
  65.4 1.3 %collective-permute-start.18 = (bf16[512,128]{1,0:T(8,128)(2,1)S(1)}, bf16[512,128]{1,0:T(8,128)(2,1)S(1)}, u32[]{:S(2)}, u32[]{:S(2)}) collective-permute-start(bf16[512,128]{1,0:T(8,128)(2,1)S(1)} %get-tuple-element.53), channel_id=1, source_target_pairs={{0,2},{2,0},{4,6},{6,4},{1,3},{3,1},{5,7},{7,5},{8,10},{10,8},{12,... | collective-permute-start | bytes 393224 | tf_op jit(solution)/shard_map/ppermute | solution.py:386
  66.7 6.6 %collective-permute-done.13.refs_1_ = bf16[4,2,128,256]{3,2,1,0:T(8,128)(2,1)S(1)} collective-permute-done((bf16[4,2,128,256]{3,2,1,0:T(8,128)(2,1)S(1)}, bf16[4,2,128,256]{3,2,1,0:T(8,128)(2,1)S(1)}, u32[]{:S(2)}, u32[]{:S(2)}) %collective-permute-start.13) | collective-permute-done | bytes 524320 | tf_op jit(solution)/shard_map/ppermute | solution.py:399
  73.3 1.2 %collective-permute-start.19 = (bf16[512,128]{1,0:T(8,128)(2,1)S(1)}, bf16[512,128]{1,0:T(8,128)(2,1)S(1)}, u32[]{:S(2)}, u32[]{:S(2)}) collective-permute-start(bf16[512,128]{1,0:T(8,128)(2,1)S(1)} %get-tuple-element.54), channel_id=1, source_target_pairs={{0,4},{2,6},{4,0},{6,2},{1,5},{3,7},{5,1},{7,3},{8,12},{10,14},{12... | collective-permute-start | bytes 393224 | tf_op jit(solution)/shard_map/ppermute | solution.py:386
  74.5 0.2 shard_map.118
  74.7 1.8 %collective-permute-start.20 = (bf16[512,128]{1,0:T(8,128)(2,1)S(1)}, bf16[512,128]{1,0:T(8,128)(2,1)S(1)}, u32[]{:S(2)}, u32[]{:S(2)}) collective-permute-start(bf16[512,128]{1,0:T(8,128)(2,1)S(1)} %get-tuple-element.55), channel_id=1, source_target_pairs={{0,6},{2,4},{4,2},{6,0},{1,7},{3,5},{5,3},{7,1},{8,14},{10,12},{12... | collective-permute-start | bytes 393224 | tf_op jit(solution)/shard_map/ppermute | solution.py:386
  76.6 0.5 collective-permute-start.14
  77.1 3.7 %collective-permute-start.26 = (bf16[1024,128]{1,0:T(8,128)(2,1)S(1)}, bf16[1024,128]{1,0:T(8,128)(2,1)S(1)}, u32[]{:S(2)}, u32[]{:S(2)}) collective-permute-start(bf16[1024,128]{1,0:T(8,128)(2,1)S(1)} %shard_map.121), channel_id=1, source_target_pairs={{8,0},{16,8},{24,16},{9,1},{17,9},{25,17},{10,2},{18,10},{26,18},{... | collective-permute-start | bytes 786440 | tf_op jit(solution)/shard_map/ppermute | solution.py:399
  80.8 1.3 %collective-permute-start.15 = (bf16[512,128]{1,0:T(8,128)(2,1)S(1)}, bf16[512,128]{1,0:T(8,128)(2,1)S(1)}, u32[]{:S(2)}, u32[]{:S(2)}) collective-permute-start(bf16[512,128]{1,0:T(8,128)(2,1)S(1)} %get-tuple-element.48), channel_id=1, source_target_pairs={{0,4},{2,6},{4,0},{6,2},{1,5},{3,7},{5,1},{7,3},{8,12},{10,14},{12... | collective-permute-start | bytes 393224 | tf_op jit(solution)/shard_map/ppermute | solution.py:386
  82.1 1.8 %collective-permute-start.16 = (bf16[512,128]{1,0:T(8,128)(2,1)S(1)}, bf16[512,128]{1,0:T(8,128)(2,1)S(1)}, u32[]{:S(2)}, u32[]{:S(2)}) collective-permute-start(bf16[512,128]{1,0:T(8,128)(2,1)S(1)} %get-tuple-element.49), channel_id=1, source_target_pairs={{0,6},{2,4},{4,2},{6,0},{1,7},{3,5},{5,3},{7,1},{8,14},{10,12},{12... | collective-permute-start | bytes 393224 | tf_op jit(solution)/shard_map/ppermute | solution.py:386
  83.9 1.1 %collective-permute-start.23 = (bf16[512,128]{1,0:T(8,128)(2,1)S(1)}, bf16[512,128]{1,0:T(8,128)(2,1)S(1)}, u32[]{:S(2)}, u32[]{:S(2)}) collective-permute-start(bf16[512,128]{1,0:T(8,128)(2,1)S(1)} %get-tuple-element.61), channel_id=1, source_target_pairs={{0,6},{2,4},{4,2},{6,0},{1,7},{3,5},{5,3},{7,1},{8,14},{10,12},{12... | collective-permute-start | bytes 393224 | tf_op jit(solution)/shard_map/ppermute | solution.py:386
  85.0 5.4 %collective-permute-done.15.refs_2_ = bf16[512,128]{1,0:T(8,128)(2,1)S(1)} collective-permute-done((bf16[512,128]{1,0:T(8,128)(2,1)S(1)}, bf16[512,128]{1,0:T(8,128)(2,1)S(1)}, u32[]{:S(2)}, u32[]{:S(2)}) %collective-permute-start.15) | collective-permute-done | bytes 131104 | tf_op jit(solution)/shard_map/ppermute | solution.py:386
  90.4 1.2 %shard_map.122 = (bf16[128,2048]{1,0:T(8,128)(2,1)}, bf16[128,1024]{1,0:T(8,128)(2,1)}, bf16[128,1024]{1,0:T(8,128)(2,1)}) custom-call(bf16[512,128]{1,0:T(8,128)(2,1)S(1)} %get-tuple-element.46.refs_0_, bf16[512,128]{1,0:T(8,128)(2,1)S(1)} %collective-permute-done.14.refs_1_, bf16[512,128]{1,0:T(8,128)(2,1)S(1)} %collective-permute-done.15.refs_2_, ...), custom_call_target="tpu_custom_call" | custom-call | bytes 4194304 | tf_op jit(solution)/shard_map/pallas_call | solution.py:530
  (32 shorter events, 0.4 us)
Async XLA Ops:
  0.6 24.1 %copy-start = (bf16[128,2048]{1,0:T(8,128)(2,1)S(1)}, bf16[128,2048]{1,0:T(8,128)(2,1)}, u32[]{:S(2)}) copy-start(bf16[128,2048]{1,0:T(8,128)(2,1)} %refs_0_.3) | copy-start | bytes 1572868
  0.6 11.9 %collective-permute-start = (f32[4,512]{1,0:T(4,128)}, f32[4,512]{1,0:T(4,128)S(1)}, u32[]{:S(2)}, u32[]{:S(2)}) collective-permute-start(f32[4,512]{1,0:T(4,128)} %param.14), channel_id=1, source_target_pairs={{0,4},{4,0},{1,5},{5,1},{2,6},{6,2},{3,7},{7,3},{8,12},{12,8},{9,1... | collective-permute-start | bytes 24584 | tf_op jit(solution)/shard_map/ppermute | solution.py:409
  2.2 22.5 %collective-permute-start.7 = (bf16[128,2048]{1,0:T(8,128)(2,1)}, bf16[128,2048]{1,0:T(8,128)(2,1)S(1)}, u32[]{:S(2)}, u32[]{:S(2)}) collective-permute-start(bf16[128,2048]{1,0:T(8,128)(2,1)} %refs_0_.3), channel_id=1, source_target_pairs={{8,0},{16,8},{24,16},{9,1},{17,9},{25,17},{10,2},{18,10},{26,18},{... | collective-permute-start | bytes 1572872 | tf_op jit(solution)/shard_map/ppermute | solution.py:399
  7.5 9.5 %collective-permute-start.2 = (bf16[1040,128]{1,0:T(8,128)(2,1)}, bf16[1040,128]{1,0:T(8,128)(2,1)S(1)}, u32[]{:S(2)}, u32[]{:S(2)}) collective-permute-start(bf16[1040,128]{1,0:T(8,128)(2,1)} %get-tuple-element.33), channel_id=1, source_target_pairs={{0,2},{2,0},{4,6},{6,4},{1,3},{3,1},{5,7},{7,5},{8,10},{10,8},{12,... | collective-permute-start | bytes 798728 | tf_op jit(solution)/shard_map/ppermute | solution.py:386
  9.1 13.2 %collective-permute-start.3 = (bf16[1040,128]{1,0:T(8,128)(2,1)}, bf16[1040,128]{1,0:T(8,128)(2,1)S(1)}, u32[]{:S(2)}, u32[]{:S(2)}) collective-permute-start(bf16[1040,128]{1,0:T(8,128)(2,1)} %get-tuple-element.34), channel_id=1, source_target_pairs={{0,4},{2,6},{4,0},{6,2},{1,5},{3,7},{5,1},{7,3},{8,12},{10,14},{12... | collective-permute-start | bytes 798728 | tf_op jit(solution)/shard_map/ppermute | solution.py:386
  9.6 12.7 %collective-permute-start.4 = (bf16[1040,128]{1,0:T(8,128)(2,1)}, bf16[1040,128]{1,0:T(8,128)(2,1)S(1)}, u32[]{:S(2)}, u32[]{:S(2)}) collective-permute-start(bf16[1040,128]{1,0:T(8,128)(2,1)} %get-tuple-element.35), channel_id=1, source_target_pairs={{0,6},{2,4},{4,2},{6,0},{1,7},{3,5},{5,3},{7,1},{8,14},{10,12},{12... | collective-permute-start | bytes 798728 | tf_op jit(solution)/shard_map/ppermute | solution.py:386
  13.3 1.2 %collective-permute-start.1 = (f32[2,4,512]{2,1,0:T(4,128)S(1)}, f32[2,4,512]{2,1,0:T(4,128)S(1)}, u32[]{:S(2)}, u32[]{:S(2)}) collective-permute-start(f32[2,4,512]{2,1,0:T(4,128)S(1)} %pad_maximum_fusion), channel_id=1, source_target_pairs={{0,1},{1,0},{2,3},{3,2},{4,5},{5,4},{6,7},{7,6},{8,9},{9,8},{10,11... | collective-permute-start | bytes 49160 | tf_op jit(solution)/shard_map/ppermute | solution.py:394
  22.3 1.0 %copy-start.1 = (bf16[1040,128]{1,0:T(8,128)(2,1)S(1)}, bf16[1040,128]{1,0:T(8,128)(2,1)}, u32[]{:S(2)}) copy-start(bf16[1040,128]{1,0:T(8,128)(2,1)} %get-tuple-element.32.refs_1_) | copy-start | bytes 798724
  23.4 12.9 %collective-permute-start.5 = (bf16[4,512,128]{2,1,0:T(8,128)(2,1)S(1)}, bf16[4,512,128]{2,1,0:T(8,128)(2,1)S(1)}, u32[]{:S(2)}, u32[]{:S(2)}) collective-permute-start(bf16[4,512,128]{2,1,0:T(8,128)(2,1)S(1)} %get-tuple-element.36.refs_1_), channel_id=1, source_target_pairs={{0,8},{8,16},{16,24},{1,9},{9,17},{17,25},{2,10},{10,18},{18,26},{... | collective-permute-start | bytes 1572872 | tf_op jit(solution)/shard_map/ppermute | solution.py:399
  25.1 6.6 %collective-permute-start.8 = (bf16[1024,128]{1,0:T(8,128)(2,1)S(1)}, bf16[1024,128]{1,0:T(8,128)(2,1)S(1)}, u32[]{:S(2)}, u32[]{:S(2)}) collective-permute-start(bf16[1024,128]{1,0:T(8,128)(2,1)S(1)} %get-tuple-element.38), channel_id=1, source_target_pairs={{0,2},{2,0},{4,6},{6,4},{1,3},{3,1},{5,7},{7,5},{8,10},{10,8},{12,... | collective-permute-start | bytes 786440 | tf_op jit(solution)/shard_map/ppermute | solution.py:386
  25.7 18.8 %collective-permute-start.11 = (bf16[4,512,128]{2,1,0:T(8,128)(2,1)S(1)}, bf16[4,512,128]{2,1,0:T(8,128)(2,1)S(1)}, u32[]{:S(2)}, u32[]{:S(2)}) collective-permute-start(bf16[4,512,128]{2,1,0:T(8,128)(2,1)S(1)} %get-tuple-element.36.refs_1_), channel_id=1, source_target_pairs={{0,1},{1,0},{2,3},{3,2},{4,5},{5,4},{6,7},{7,6},{8,9},{9,8},{10,11... | collective-permute-start | bytes 1572872 | tf_op jit(solution)/shard_map/ppermute | solution.py:394
  25.8 24.3 %collective-permute-start.12 = (bf16[4,544,128]{2,1,0:T(8,128)(2,1)S(1)}, bf16[4,544,128]{2,1,0:T(8,128)(2,1)S(1)}, u32[]{:S(2)}, u32[]{:S(2)}) collective-permute-start(bf16[4,544,128]{2,1,0:T(8,128)(2,1)S(1)} %get-tuple-element.41.refs_7_), channel_id=1, source_target_pairs={{8,0},{16,8},{24,16},{9,1},{17,9},{25,17},{10,2},{18,10},{26,18},{... | collective-permute-start | bytes 1671176 | tf_op jit(solution)/shard_map/ppermute | solution.py:399
  30.4 14.1 %collective-permute-start.9 = (bf16[1024,128]{1,0:T(8,128)(2,1)S(1)}, bf16[1024,128]{1,0:T(8,128)(2,1)S(1)}, u32[]{:S(2)}, u32[]{:S(2)}) collective-permute-start(bf16[1024,128]{1,0:T(8,128)(2,1)S(1)} %get-tuple-element.39), channel_id=1, source_target_pairs={{0,4},{2,6},{4,0},{6,2},{1,5},{3,7},{5,1},{7,3},{8,12},{10,14},{12... | collective-permute-start | bytes 786440 | tf_op jit(solution)/shard_map/ppermute | solution.py:386
  31.7 12.9 %collective-permute-start.10 = (bf16[1024,128]{1,0:T(8,128)(2,1)S(1)}, bf16[1024,128]{1,0:T(8,128)(2,1)S(1)}, u32[]{:S(2)}, u32[]{:S(2)}) collective-permute-start(bf16[1024,128]{1,0:T(8,128)(2,1)S(1)} %get-tuple-element.40), channel_id=1, source_target_pairs={{0,6},{2,4},{4,2},{6,0},{1,7},{3,5},{5,3},{7,1},{8,14},{10,12},{12... | collective-permute-start | bytes 786440 | tf_op jit(solution)/shard_map/ppermute | solution.py:386
  36.3 13.8 %collective-permute-start.6 = (bf16[4,512,128]{2,1,0:T(8,128)(2,1)S(1)}, bf16[4,512,128]{2,1,0:T(8,128)(2,1)S(1)}, u32[]{:S(2)}, u32[]{:S(2)}) collective-permute-start(bf16[4,512,128]{2,1,0:T(8,128)(2,1)S(1)} %collective-permute-done.5.refs_1_), channel_id=1, source_target_pairs={{0,1},{1,0},{2,3},{3,2},{4,5},{5,4},{6,7},{7,6},{8,9},{9,8},{10,11... | collective-permute-start | bytes 1572872 | tf_op jit(solution)/shard_map/ppermute | solution.py:394
  55.3 2.0 %collective-permute-start.21 = (bf16[4,512,128]{2,1,0:T(8,128)(2,1)S(1)}, bf16[4,512,128]{2,1,0:T(8,128)(2,1)S(1)}, u32[]{:S(2)}, u32[]{:S(2)}) collective-permute-start(bf16[4,512,128]{2,1,0:T(8,128)(2,1)S(1)} %get-tuple-element.57), channel_id=1, source_target_pairs={{0,1},{1,0},{2,3},{3,2},{4,5},{5,4},{6,7},{7,6},{8,9},{9,8},{10,11... | collective-permute-start | bytes 1572872 | tf_op jit(solution)/shard_map/ppermute | solution.py:394
  55.4 9.9 %collective-permute-start.17 = (bf16[4,512,128]{2,1,0:T(8,128)(2,1)S(1)}, bf16[4,512,128]{2,1,0:T(8,128)(2,1)S(1)}, u32[]{:S(2)}, u32[]{:S(2)}) collective-permute-start(bf16[4,512,128]{2,1,0:T(8,128)(2,1)S(1)} %get-tuple-element.51), channel_id=1, source_target_pairs={{0,1},{1,0},{2,3},{3,2},{4,5},{5,4},{6,7},{7,6},{8,9},{9,8},{10,11... | collective-permute-start | bytes 1572872 | tf_op jit(solution)/shard_map/ppermute | solution.py:394
  55.9 17.4 %collective-permute-start.13 = (bf16[4,2,128,256]{3,2,1,0:T(8,128)(2,1)S(1)}, bf16[4,2,128,256]{3,2,1,0:T(8,128)(2,1)S(1)}, u32[]{:S(2)}, u32[]{:S(2)}) collective-permute-start(bf16[4,2,128,256]{3,2,1,0:T(8,128)(2,1)S(1)} %get-tuple-element.45), channel_id=1, source_target_pairs={{0,8},{8,16},{16,24},{1,9},{9,17},{17,25},{2,10},{10,18},{18,26},{... | collective-permute-start | bytes 1572872 | tf_op jit(solution)/shard_map/ppermute | solution.py:399
  57.4 19.7 %collective-permute-start.22 = (bf16[1024,128]{1,0:T(8,128)(2,1)S(1)}, bf16[1024,128]{1,0:T(8,128)(2,1)S(1)}, u32[]{:S(2)}, u32[]{:S(2)}) collective-permute-start(bf16[1024,128]{1,0:T(8,128)(2,1)S(1)} %get-tuple-element.58), channel_id=1, source_target_pairs={{8,0},{16,8},{24,16},{9,1},{17,9},{25,17},{10,2},{18,10},{26,18},{... | collective-permute-start | bytes 786440 | tf_op jit(solution)/shard_map/ppermute | solution.py:399
  63.2 11.5 %collective-permute-start.24 = (bf16[512,128]{1,0:T(8,128)(2,1)S(1)}, bf16[512,128]{1,0:T(8,128)(2,1)S(1)}, u32[]{:S(2)}, u32[]{:S(2)}) collective-permute-start(bf16[512,128]{1,0:T(8,128)(2,1)S(1)} %get-tuple-element.59), channel_id=1, source_target_pairs={{0,2},{2,0},{4,6},{6,4},{1,3},{3,1},{5,7},{7,5},{8,10},{10,8},{12,... | collective-permute-start | bytes 393224 | tf_op jit(solution)/shard_map/ppermute | solution.py:386
  64.7 11.8 %collective-permute-start.25 = (bf16[512,128]{1,0:T(8,128)(2,1)S(1)}, bf16[512,128]{1,0:T(8,128)(2,1)S(1)}, u32[]{:S(2)}, u32[]{:S(2)}) collective-permute-start(bf16[512,128]{1,0:T(8,128)(2,1)S(1)} %get-tuple-element.60), channel_id=1, source_target_pairs={{0,4},{2,6},{4,0},{6,2},{1,5},{3,7},{5,1},{7,3},{8,12},{10,14},{12... | collective-permute-start | bytes 393224 | tf_op jit(solution)/shard_map/ppermute | solution.py:386
  65.4 15.5 %collective-permute-start.18 = (bf16[512,128]{1,0:T(8,128)(2,1)S(1)}, bf16[512,128]{1,0:T(8,128)(2,1)S(1)}, u32[]{:S(2)}, u32[]{:S(2)}) collective-permute-start(bf16[512,128]{1,0:T(8,128)(2,1)S(1)} %get-tuple-element.53), channel_id=1, source_target_pairs={{0,2},{2,0},{4,6},{6,4},{1,3},{3,1},{5,7},{7,5},{8,10},{10,8},{12,... | collective-permute-start | bytes 393224 | tf_op jit(solution)/shard_map/ppermute | solution.py:386
  73.3 8.8 %collective-permute-start.19 = (bf16[512,128]{1,0:T(8,128)(2,1)S(1)}, bf16[512,128]{1,0:T(8,128)(2,1)S(1)}, u32[]{:S(2)}, u32[]{:S(2)}) collective-permute-start(bf16[512,128]{1,0:T(8,128)(2,1)S(1)} %get-tuple-element.54), channel_id=1, source_target_pairs={{0,4},{2,6},{4,0},{6,2},{1,5},{3,7},{5,1},{7,3},{8,12},{10,14},{12... | collective-permute-start | bytes 393224 | tf_op jit(solution)/shard_map/ppermute | solution.py:386
  74.7 9.1 %collective-permute-start.20 = (bf16[512,128]{1,0:T(8,128)(2,1)S(1)}, bf16[512,128]{1,0:T(8,128)(2,1)S(1)}, u32[]{:S(2)}, u32[]{:S(2)}) collective-permute-start(bf16[512,128]{1,0:T(8,128)(2,1)S(1)} %get-tuple-element.55), channel_id=1, source_target_pairs={{0,6},{2,4},{4,2},{6,0},{1,7},{3,5},{5,3},{7,1},{8,14},{10,12},{12... | collective-permute-start | bytes 393224 | tf_op jit(solution)/shard_map/ppermute | solution.py:386
  76.6 8.4 %collective-permute-start.14 = (bf16[512,128]{1,0:T(8,128)(2,1)S(1)}, bf16[512,128]{1,0:T(8,128)(2,1)S(1)}, u32[]{:S(2)}, u32[]{:S(2)}) collective-permute-start(bf16[512,128]{1,0:T(8,128)(2,1)S(1)} %get-tuple-element.47), channel_id=1, source_target_pairs={{0,2},{2,0},{4,6},{6,4},{1,3},{3,1},{5,7},{7,5},{8,10},{10,8},{12,... | collective-permute-start | bytes 393224 | tf_op jit(solution)/shard_map/ppermute | solution.py:386
  77.1 13.3 %collective-permute-start.26 = (bf16[1024,128]{1,0:T(8,128)(2,1)S(1)}, bf16[1024,128]{1,0:T(8,128)(2,1)S(1)}, u32[]{:S(2)}, u32[]{:S(2)}) collective-permute-start(bf16[1024,128]{1,0:T(8,128)(2,1)S(1)} %shard_map.121), channel_id=1, source_target_pairs={{8,0},{16,8},{24,16},{9,1},{17,9},{25,17},{10,2},{18,10},{26,18},{... | collective-permute-start | bytes 786440 | tf_op jit(solution)/shard_map/ppermute | solution.py:399
  80.8 9.6 %collective-permute-start.15 = (bf16[512,128]{1,0:T(8,128)(2,1)S(1)}, bf16[512,128]{1,0:T(8,128)(2,1)S(1)}, u32[]{:S(2)}, u32[]{:S(2)}) collective-permute-start(bf16[512,128]{1,0:T(8,128)(2,1)S(1)} %get-tuple-element.48), channel_id=1, source_target_pairs={{0,4},{2,6},{4,0},{6,2},{1,5},{3,7},{5,1},{7,3},{8,12},{10,14},{12... | collective-permute-start | bytes 393224 | tf_op jit(solution)/shard_map/ppermute | solution.py:386
  82.1 8.3 %collective-permute-start.16 = (bf16[512,128]{1,0:T(8,128)(2,1)S(1)}, bf16[512,128]{1,0:T(8,128)(2,1)S(1)}, u32[]{:S(2)}, u32[]{:S(2)}) collective-permute-start(bf16[512,128]{1,0:T(8,128)(2,1)S(1)} %get-tuple-element.49), channel_id=1, source_target_pairs={{0,6},{2,4},{4,2},{6,0},{1,7},{3,5},{5,3},{7,1},{8,14},{10,12},{12... | collective-permute-start | bytes 393224 | tf_op jit(solution)/shard_map/ppermute | solution.py:386
  83.9 6.6 %collective-permute-start.23 = (bf16[512,128]{1,0:T(8,128)(2,1)S(1)}, bf16[512,128]{1,0:T(8,128)(2,1)S(1)}, u32[]{:S(2)}, u32[]{:S(2)}) collective-permute-start(bf16[512,128]{1,0:T(8,128)(2,1)S(1)} %get-tuple-element.61), channel_id=1, source_target_pairs={{0,6},{2,4},{4,2},{6,0},{1,7},{3,5},{5,3},{7,1},{8,14},{10,12},{12... | collective-permute-start | bytes 393224 | tf_op jit(solution)/shard_map/ppermute | solution.py:386

commit v5 on v4

--- a/solution.py
+++ b/solution.py
@@ -25,11 +25,12 @@
 F32 = jnp.float32
 CROSS = ("y", "x")
 WHOLE = pl.BlockSpec(memory_space=pltpu.VMEM)
+IN_HBM = pl.BlockSpec(memory_space=pltpu.HBM)
 SCALARS = pl.BlockSpec(memory_space=pltpu.SMEM)
 VMEM_BYTES = 16 * 1024 * 1024
 
 
-def call(kernel, out_shape, in_specs, flops=0, moved=4 << 20, scratch=(), vmem=VMEM_BYTES):
+def call(kernel, out_shape, in_specs, flops=0, moved=4 << 20, scratch=()):
     def placed(*refs):
         n_x = lax.axis_size("x")
         return kernel((lax.axis_index("y") * n_x + lax.axis_index("x"), lax.axis_index("core")), *refs)
@@ -41,7 +42,7 @@
         out_specs=jax.tree.map(lambda _: WHOLE, out_shape),
         scratch_shapes=scratch,
         cost_estimate=pl.CostEstimate(flops=flops, bytes_accessed=moved, transcendentals=0),
-        compiler_params=pltpu.CompilerParams(vmem_limit_bytes=vmem),
+        compiler_params=pltpu.CompilerParams(vmem_limit_bytes=VMEM_BYTES),
     )
 
 
@@ -94,26 +95,29 @@
     return jnp.concatenate(terms, axis=0)
 
 
-def pack_kernel(plan, me, do_hbm, o_hbm, k_hbm, v_hbm, *refs):
-    pieces, (do_ref, o_ref, k_ref, v_ref, delta_ref, arrived) = refs[: plan.chips], refs[plan.chips :]
-    tokens = plan.tokens
-    half = tokens // 2
-    loads = []
-    for n, (source, target) in enumerate(
-        ((do_hbm, do_ref), (o_hbm, o_ref), (k_hbm, k_ref), (v_hbm, v_ref))
-    ):
-        pair = []
+def load(arrived, pairs):
+    started = []
+    for n, (source, target) in enumerate(pairs):
+        half = target.shape[0] // 2
+        halves = []
         for part in range(2):
             rows = pl.ds(part * half, half)
             copy = pltpu.make_async_copy(source.at[rows], target.at[rows], arrived.at[n, part])
             copy.start()
-            pair.append(copy)
-        loads.append(pair)
+            halves.append(copy)
+        started.append(halves)
 
     def wait_for(n):
-        for copy in loads[n]:
+        for copy in started[n]:
             copy.wait()
 
+    return wait_for
+
+
+def pack_kernel(plan, me, do_hbm, o_hbm, k_hbm, v_hbm, *refs):
+    pieces, (do_ref, o_ref, k_ref, v_ref, delta_ref, arrived) = refs[: plan.chips], refs[plan.chips :]
+    tokens = plan.tokens
+    wait_for = load(arrived, ((do_hbm, do_ref), (o_hbm, o_ref), (k_hbm, k_ref), (v_hbm, v_ref)))
     wait_for(0)
     wait_for(1)
     sums = []
@@ -140,12 +144,16 @@
         out[plan.q_rows + plan.kv_rows :, :] = padded_rows(terms, plan.aux_sent)
 
 
-def pack_q_kernel(plan, me, *refs):
-    levels, pieces = refs[: -plan.chips], refs[-plan.chips :]
+def pack_q_kernel(plan, me, own_hbm, *refs):
+    own_ref, arrived = refs[-2:]
+    above, pieces = refs[: -plan.chips - 2], refs[-plan.chips - 2 : -2]
     tokens = plan.tokens
-    for mask, out in enumerate(pieces):
-        first = plan.first_kv_head(me[0] ^ mask) * GROUP
-        for level, ref in enumerate(levels):
+    wait_for = load(arrived, ((own_hbm, own_ref),))
+    for level, ref in reversed(list(enumerate((own_ref,) + above))):
+        if level == 0:
+            wait_for(0)
+        for mask, out in enumerate(pieces):
+            first = plan.first_kv_head(me[0] ^ mask) * GROUP
             for g in range(plan.q_heads):
                 at = level * plan.q_rows + g * tokens
                 out[at : at + tokens, :] = columns(ref, first + g)[...]
@@ -430,6 +438,7 @@
     def stacked(rows, dtype=BF16):
         return jax.ShapeDtypeStruct((chips, rows, LANES), dtype)
 
+    kept = functools.partial(pltpu.with_memory_space_constraint, memory_space=pltpu.HBM)
     raw = [queries]
     for _ in range(1, reach // 2 + 1):
         raw.append(along(raw[-1], planes, -1))
@@ -439,11 +448,10 @@
     pieces = call(
         functools.partial(pack_kernel, plan),
         [like(plan.q_rows + plan.kv_rows + plan.aux_sent)] * chips,
-        [pl.BlockSpec(memory_space=pltpu.HBM)] * len(arrays),
+        [IN_HBM] * len(arrays),
         scratch=[pltpu.VMEM(a.shape, a.dtype) for a in arrays]
         + [pltpu.VMEM((LANES, LANES), F32), pltpu.SemaphoreType.DMA((len(arrays), 2))],
-        vmem=60 * 1024 * 1024,
-    )(*arrays)
+    )(*map(kept, arrays))
     do_own, kv_own = call(
         functools.partial(assemble_kernel, plan),
         [stacked(plan.q_rows + plan.aux), stacked(plan.kv_rows)],
@@ -457,7 +465,12 @@
     for _ in range(1, reach // 2 + 1):
         far_do.append(along(far_do[-1], planes, -1))
     q_pieces = exchange(
-        call(functools.partial(pack_q_kernel, plan), [like(len(raw) * plan.q_rows)] * chips, [WHOLE] * len(raw))(*raw),
+        call(
+            functools.partial(pack_q_kernel, plan),
+            [like(len(raw) * plan.q_rows)] * chips,
+            [IN_HBM] + [WHOLE] * (len(raw) - 1),
+            scratch=[pltpu.VMEM(queries.shape, BF16), pltpu.SemaphoreType.DMA((1, 2))],
+        )(kept(queries), *raw[1:]),
     )
     up = [(kv, swap(kv)) for kv in up]
 

time: 92.4 us -> 91.2 us (0.987)
  local copies, waits for them, and re-layouts: 0.98 us -> 0.02 us
    unnamed x4 -> x0, local copies, waits for them, and re-layouts: 0.96 us -> none
    pallas_call x1, Pallas kernels: 2.93 us -> 1.99 us  [body(): call(functools.partial(pack_kernel, plan), [like(plan.q_rows + plan.kv_ro...]
where the time goes in v5:
time: 91.2 us; the launch traced here: 90.4 us
  starting transfers between devices  39.4 us (43%)
  waiting for transfers between devices  31 us (34%)
  Pallas kernels  15.7 us (17%)
  other arithmetic  3.45 us (4%)
    ppermute x15, waiting for transfers between devices, send_in_plane(): return lax.ppermute(piece, CROSS, [(i, i ^ mask) for i in range(chips)])  21.2 us
    ppermute x6, starting transfers between devices, along(): return lax.ppermute(value, 'z', pairs)  19 us
    ppermute x15, starting transfers between devices, send_in_plane(): return lax.ppermute(piece, CROSS, [(i, i ^ mask) for i in range(chips)])  18.3 us
    pallas_call x3, Pallas kernels, body(): call(functools.partial(role_kernel, plan, j, has_dq, carried is not None,...  10.7 us
    ppermute x6, waiting for transfers between devices, along(): return lax.ppermute(value, 'z', pairs)  8.6 us
    pallas_call x1, Pallas kernels, body(): call(functools.partial(pack_kernel, plan), [like(plan.q_rows + plan.kv_ro...  1.99 us
  transfers between devices with their start and end apart: 27, of which 8 were waited for; matrix products, arithmetic and copies ran while one was open for 4% of the time, Pallas kernels for 10%

profile of v5, /device:TPU:24, one launch (start us, length us, event | category | flops | bytes accessed | tf_op | source)
XLA Modules:
  0.0 90.4 jit_solution(6680536887472452670)
XLA Ops:
  0.6 1.6 %collective-permute-start = (f32[4,512]{1,0:T(4,128)}, f32[4,512]{1,0:T(4,128)S(1)}, u32[]{:S(2)}, u32[]{:S(2)}) collective-permute-start(f32[4,512]{1,0:T(4,128)} %param.14), channel_id=1, source_target_pairs={{0,4},{4,0},{1,5},{5,1},{2,6},{6,2},{3,7},{7,3},{8,12},{12,8},{9,1... | collective-permute-start | bytes 24584 | tf_op jit(solution)/shard_map/ppermute | solution.py:417
  2.2 2.4 %collective-permute-start.7 = (bf16[128,2048]{1,0:T(8,128)(2,1)}, bf16[128,2048]{1,0:T(8,128)(2,1)S(1)}, u32[]{:S(2)}, u32[]{:S(2)}) collective-permute-start(bf16[128,2048]{1,0:T(8,128)(2,1)} %refs_0_.3), channel_id=1, source_target_pairs={{8,0},{16,8},{24,16},{9,1},{17,9},{25,17},{10,2},{18,10},{26,18},{... | collective-permute-start | bytes 1572872 | tf_op jit(solution)/shard_map/ppermute | solution.py:407
  4.6 2.0 %shard_map.112 = (bf16[1040,128]{1,0:T(8,128)(2,1)S(1)}, bf16[1040,128]{1,0:T(8,128)(2,1)S(1)}, bf16[1040,128]{1,0:T(8,128)(2,1)S(1)}, bf16[1040,128]{1,0:T(8,128)(2,1)S(1)}) custom-call(bf16[128,2048]{1,0:T(8,128)(2,1)} %refs_0_.2, bf16[128,2048]{1,0:T(8,128)(2,1)} %refs_1_.1, bf16[128,1024]{1,0:T(8,128)(2,1)} %refs_2_.1, bf16[128,1024]{1,0:T(8,128)(2,1)} %refs_3_.1), custom_call_target="tpu_custom_call" | custom-call | bytes 4194304 | tf_op jit(solution)/shard_map/pallas_call | solution.py:448
  6.6 1.6 %collective-permute-start.2 = (bf16[1040,128]{1,0:T(8,128)(2,1)S(1)}, bf16[1040,128]{1,0:T(8,128)(2,1)S(1)}, u32[]{:S(2)}, u32[]{:S(2)}) collective-permute-start(bf16[1040,128]{1,0:T(8,128)(2,1)S(1)} %get-tuple-element.33), channel_id=1, source_target_pairs={{0,2},{2,0},{4,6},{6,4},{1,3},{3,1},{5,7},{7,5},{8,10},{10,8},{12,... | collective-permute-start | bytes 798728 | tf_op jit(solution)/shard_map/ppermute | solution.py:394
  8.2 0.5 collective-permute-start.3
  8.7 1.5 %collective-permute-start.4 = (bf16[1040,128]{1,0:T(8,128)(2,1)S(1)}, bf16[1040,128]{1,0:T(8,128)(2,1)S(1)}, u32[]{:S(2)}, u32[]{:S(2)}) collective-permute-start(bf16[1040,128]{1,0:T(8,128)(2,1)S(1)} %get-tuple-element.35), channel_id=1, source_target_pairs={{0,6},{2,4},{4,2},{6,0},{1,7},{3,5},{5,3},{7,1},{8,14},{10,12},{12... | collective-permute-start | bytes 798728 | tf_op jit(solution)/shard_map/ppermute | solution.py:394
  10.2 0.8 add_bitcast_fusion
  11.0 0.7 add_multiply_fusion
  11.6 0.7 pad_maximum_fusion
  12.4 1.1 %collective-permute-done.1 = f32[2,4,512]{2,1,0:T(4,128)S(1)} collective-permute-done((f32[2,4,512]{2,1,0:T(4,128)S(1)}, f32[2,4,512]{2,1,0:T(4,128)S(1)}, u32[]{:S(2)}, u32[]{:S(2)}) %collective-permute-start.1) | collective-permute-done | bytes 16416 | tf_op jit(solution)/shard_map/ppermute | solution.py:402
  13.5 0.8 fusion.1.refs_0_
  14.3 1.6 %collective-permute-done.2.refs_2_ = bf16[1040,128]{1,0:T(8,128)(2,1)S(1)} collective-permute-done((bf16[1040,128]{1,0:T(8,128)(2,1)S(1)}, bf16[1040,128]{1,0:T(8,128)(2,1)S(1)}, u32[]{:S(2)}, u32[]{:S(2)}) %collective-permute-start.2) | collective-permute-done | bytes 266272 | tf_op jit(solution)/shard_map/ppermute | solution.py:394
  15.9 5.2 %collective-permute-done.3.refs_3_ = bf16[1040,128]{1,0:T(8,128)(2,1)S(1)} collective-permute-done((bf16[1040,128]{1,0:T(8,128)(2,1)S(1)}, bf16[1040,128]{1,0:T(8,128)(2,1)S(1)}, u32[]{:S(2)}, u32[]{:S(2)}) %collective-permute-start.3) | collective-permute-done | bytes 266272 | tf_op jit(solution)/shard_map/ppermute | solution.py:394
  21.2 0.1 shard_map.113
  21.3 1.3 %collective-permute-start.5 = (bf16[4,512,128]{2,1,0:T(8,128)(2,1)S(1)}, bf16[4,512,128]{2,1,0:T(8,128)(2,1)S(1)}, u32[]{:S(2)}, u32[]{:S(2)}) collective-permute-start(bf16[4,512,128]{2,1,0:T(8,128)(2,1)S(1)} %get-tuple-element.36.refs_1_), channel_id=1, source_target_pairs={{0,8},{8,16},{16,24},{1,9},{9,17},{17,25},{2,10},{10,18},{18,26},{... | collective-permute-start | bytes 1572872 | tf_op jit(solution)/shard_map/ppermute | solution.py:407
  22.6 0.1 broadcast_compare_fusion
  22.6 1.2 %shard_map.114 = (bf16[1024,128]{1,0:T(8,128)(2,1)S(1)}, bf16[1024,128]{1,0:T(8,128)(2,1)S(1)}, bf16[1024,128]{1,0:T(8,128)(2,1)S(1)}, bf16[1024,128]{1,0:T(8,128)(2,1)S(1)}) custom-call(bf16[128,2048]{1,0:T(8,128)(2,1)} %refs_0_.3, bf16[128,2048]{1,0:T(8,128)(2,1)S(1)} %collective-permute-done.7.refs_1_), custom_call_target="tpu_custom_call" | custom-call | bytes 4194304 | tf_op jit(solution)/shard_map/pallas_call | solution.py:468
  23.8 0.6 collective-permute-start.8
  24.5 0.1 broadcast_compare_fusion.1
  24.6 4.6 %collective-permute-start.12 = (bf16[4,544,128]{2,1,0:T(8,128)(2,1)S(1)}, bf16[4,544,128]{2,1,0:T(8,128)(2,1)S(1)}, u32[]{:S(2)}, u32[]{:S(2)}) collective-permute-start(bf16[4,544,128]{2,1,0:T(8,128)(2,1)S(1)} %get-tuple-element.41.refs_7_), channel_id=1, source_target_pairs={{8,0},{16,8},{24,16},{9,1},{17,9},{25,17},{10,2},{18,10},{26,18},{... | collective-permute-start | bytes 1671176 | tf_op jit(solution)/shard_map/ppermute | solution.py:407
  29.2 1.3 %collective-permute-start.9 = (bf16[1024,128]{1,0:T(8,128)(2,1)S(1)}, bf16[1024,128]{1,0:T(8,128)(2,1)S(1)}, u32[]{:S(2)}, u32[]{:S(2)}) collective-permute-start(bf16[1024,128]{1,0:T(8,128)(2,1)S(1)} %get-tuple-element.39), channel_id=1, source_target_pairs={{0,4},{2,6},{4,0},{6,2},{1,5},{3,7},{5,1},{7,3},{8,12},{10,14},{12... | collective-permute-start | bytes 786440 | tf_op jit(solution)/shard_map/ppermute | solution.py:394
  30.4 1.7 %collective-permute-start.10 = (bf16[1024,128]{1,0:T(8,128)(2,1)S(1)}, bf16[1024,128]{1,0:T(8,128)(2,1)S(1)}, u32[]{:S(2)}, u32[]{:S(2)}) collective-permute-start(bf16[1024,128]{1,0:T(8,128)(2,1)S(1)} %get-tuple-element.40), channel_id=1, source_target_pairs={{0,6},{2,4},{4,2},{6,0},{1,7},{3,5},{5,3},{7,1},{8,14},{10,12},{12... | collective-permute-start | bytes 786440 | tf_op jit(solution)/shard_map/ppermute | solution.py:394
  32.2 2.0 %collective-permute-done.5.refs_1_ = bf16[4,512,128]{2,1,0:T(8,128)(2,1)S(1)} collective-permute-done((bf16[4,512,128]{2,1,0:T(8,128)(2,1)S(1)}, bf16[4,512,128]{2,1,0:T(8,128)(2,1)S(1)}, u32[]{:S(2)}, u32[]{:S(2)}) %collective-permute-start.5) | collective-permute-done | bytes 524320 | tf_op jit(solution)/shard_map/ppermute | solution.py:407
  34.2 0.2 fusion.5
  34.4 8.9 %collective-permute-done.9.refs_5_ = bf16[1024,128]{1,0:T(8,128)(2,1)S(1)} collective-permute-done((bf16[1024,128]{1,0:T(8,128)(2,1)S(1)}, bf16[1024,128]{1,0:T(8,128)(2,1)S(1)}, u32[]{:S(2)}, u32[]{:S(2)}) %collective-permute-start.9) | collective-permute-done | bytes 262176 | tf_op jit(solution)/shard_map/ppermute | solution.py:394
  43.3 5.5 %shard_map.115 = (f32[4,2,128,256]{3,2,1,0:T(8,128)S(1)}, f32[4,512,128]{2,1,0:T(8,128)S(1)}, bf16[4,512,128]{2,1,0:T(8,128)(2,1)S(1)}) custom-call(s32[2,2]{1,0:T(2,128)S(1)} %get-tuple-element.64.refs_0_, bf16[4,512,128]{2,1,0:T(8,128)(2,1)S(1)} %get-tuple-element.36.refs_1_, bf16[4,512,128]{2,1,0:T(8,128)(2,1)S(1)} %collective-permute-done.11.refs_2_, ...), custom_call_target="tpu_custom_call" | custom-call | flops 2684354560 | bytes 4194304 | tf_op jit(solution)/shard_map/pallas_call | solution.py:501
  48.9 1.2 %shard_map.116 = (bf16[4,2,128,256]{3,2,1,0:T(8,128)(2,1)S(1)}, f32[2,4,512,128]{3,2,1,0:T(8,128)S(1)}) custom-call(s32[2,2]{1,0:T(2,128)S(1)} %get-tuple-element.63.refs_0_, bf16[4,512,128]{2,1,0:T(8,128)(2,1)S(1)} %collective-permute-done.5.refs_1_, bf16[4,512,128]{2,1,0:T(8,128)(2,1)S(1)} %collective-permute-done.6.refs_2_, ...), custom_call_target="tpu_custom_call" | custom-call | flops 2684354560 | bytes 4194304 | tf_op jit(solution)/shard_map/pallas_call | solution.py:501
  50.1 4.0 %shard_map.117 = (f32[4,2,128,256]{3,2,1,0:T(8,128)S(1)}, f32[4,512,128]{2,1,0:T(8,128)S(1)}, bf16[4,512,128]{2,1,0:T(8,128)(2,1)S(1)}) custom-call(s32[2,2]{1,0:T(2,128)S(1)} %get-tuple-element.65.refs_0_, bf16[4,512,128]{2,1,0:T(8,128)(2,1)S(1)} %collective-permute-done.5.refs_1_, bf16[4,512,128]{2,1,0:T(8,128)(2,1)S(1)} %collective-permute-done.6.refs_2_, ...), custom_call_target="tpu_custom_call" | custom-call | flops 2684354560 | bytes 4194304 | tf_op jit(solution)/shard_map/pallas_call | solution.py:501
  54.1 0.5 collective-permute-start.17
  54.6 1.3 %collective-permute-start.13 = (bf16[4,2,128,256]{3,2,1,0:T(8,128)(2,1)S(1)}, bf16[4,2,128,256]{3,2,1,0:T(8,128)(2,1)S(1)}, u32[]{:S(2)}, u32[]{:S(2)}) collective-permute-start(bf16[4,2,128,256]{3,2,1,0:T(8,128)(2,1)S(1)} %get-tuple-element.45), channel_id=1, source_target_pairs={{0,8},{8,16},{16,24},{1,9},{9,17},{17,25},{2,10},{10,18},{18,26},{... | collective-permute-start | bytes 1572872 | tf_op jit(solution)/shard_map/ppermute | solution.py:407
  55.9 0.1 collective-permute-done.21.refs_1_
  56.0 0.1 shard_map.120
  56.2 5.8 %collective-permute-start.22 = (bf16[1024,128]{1,0:T(8,128)(2,1)S(1)}, bf16[1024,128]{1,0:T(8,128)(2,1)S(1)}, u32[]{:S(2)}, u32[]{:S(2)}) collective-permute-start(bf16[1024,128]{1,0:T(8,128)(2,1)S(1)} %get-tuple-element.58), channel_id=1, source_target_pairs={{8,0},{16,8},{24,16},{9,1},{17,9},{25,17},{10,2},{18,10},{26,18},{... | collective-permute-start | bytes 786440 | tf_op jit(solution)/shard_map/ppermute | solution.py:407
  62.0 1.6 %collective-permute-start.24 = (bf16[512,128]{1,0:T(8,128)(2,1)S(1)}, bf16[512,128]{1,0:T(8,128)(2,1)S(1)}, u32[]{:S(2)}, u32[]{:S(2)}) collective-permute-start(bf16[512,128]{1,0:T(8,128)(2,1)S(1)} %get-tuple-element.59), channel_id=1, source_target_pairs={{0,2},{2,0},{4,6},{6,4},{1,3},{3,1},{5,7},{7,5},{8,10},{10,8},{12,... | collective-permute-start | bytes 393224 | tf_op jit(solution)/shard_map/ppermute | solution.py:394
  63.5 0.5 collective-permute-start.25
  64.0 0.1 shard_map.119
  64.1 1.3 %collective-permute-start.18 = (bf16[512,128]{1,0:T(8,128)(2,1)S(1)}, bf16[512,128]{1,0:T(8,128)(2,1)S(1)}, u32[]{:S(2)}, u32[]{:S(2)}) collective-permute-start(bf16[512,128]{1,0:T(8,128)(2,1)S(1)} %get-tuple-element.53), channel_id=1, source_target_pairs={{0,2},{2,0},{4,6},{6,4},{1,3},{3,1},{5,7},{7,5},{8,10},{10,8},{12,... | collective-permute-start | bytes 393224 | tf_op jit(solution)/shard_map/ppermute | solution.py:394
  65.4 6.6 %collective-permute-done.13.refs_1_ = bf16[4,2,128,256]{3,2,1,0:T(8,128)(2,1)S(1)} collective-permute-done((bf16[4,2,128,256]{3,2,1,0:T(8,128)(2,1)S(1)}, bf16[4,2,128,256]{3,2,1,0:T(8,128)(2,1)S(1)}, u32[]{:S(2)}, u32[]{:S(2)}) %collective-permute-start.13) | collective-permute-done | bytes 524320 | tf_op jit(solution)/shard_map/ppermute | solution.py:407
  72.0 1.2 %collective-permute-start.19 = (bf16[512,128]{1,0:T(8,128)(2,1)S(1)}, bf16[512,128]{1,0:T(8,128)(2,1)S(1)}, u32[]{:S(2)}, u32[]{:S(2)}) collective-permute-start(bf16[512,128]{1,0:T(8,128)(2,1)S(1)} %get-tuple-element.54), channel_id=1, source_target_pairs={{0,4},{2,6},{4,0},{6,2},{1,5},{3,7},{5,1},{7,3},{8,12},{10,14},{12... | collective-permute-start | bytes 393224 | tf_op jit(solution)/shard_map/ppermute | solution.py:394
  73.2 0.2 shard_map.118
  73.5 1.8 %collective-permute-start.20 = (bf16[512,128]{1,0:T(8,128)(2,1)S(1)}, bf16[512,128]{1,0:T(8,128)(2,1)S(1)}, u32[]{:S(2)}, u32[]{:S(2)}) collective-permute-start(bf16[512,128]{1,0:T(8,128)(2,1)S(1)} %get-tuple-element.55), channel_id=1, source_target_pairs={{0,6},{2,4},{4,2},{6,0},{1,7},{3,5},{5,3},{7,1},{8,14},{10,12},{12... | collective-permute-start | bytes 393224 | tf_op jit(solution)/shard_map/ppermute | solution.py:394
  75.4 0.5 collective-permute-start.14
  75.9 3.7 %collective-permute-start.26 = (bf16[1024,128]{1,0:T(8,128)(2,1)S(1)}, bf16[1024,128]{1,0:T(8,128)(2,1)S(1)}, u32[]{:S(2)}, u32[]{:S(2)}) collective-permute-start(bf16[1024,128]{1,0:T(8,128)(2,1)S(1)} %shard_map.121), channel_id=1, source_target_pairs={{8,0},{16,8},{24,16},{9,1},{17,9},{25,17},{10,2},{18,10},{26,18},{... | collective-permute-start | bytes 786440 | tf_op jit(solution)/shard_map/ppermute | solution.py:407
  79.6 1.3 %collective-permute-start.15 = (bf16[512,128]{1,0:T(8,128)(2,1)S(1)}, bf16[512,128]{1,0:T(8,128)(2,1)S(1)}, u32[]{:S(2)}, u32[]{:S(2)}) collective-permute-start(bf16[512,128]{1,0:T(8,128)(2,1)S(1)} %get-tuple-element.48), channel_id=1, source_target_pairs={{0,4},{2,6},{4,0},{6,2},{1,5},{3,7},{5,1},{7,3},{8,12},{10,14},{12... | collective-permute-start | bytes 393224 | tf_op jit(solution)/shard_map/ppermute | solution.py:394
  80.9 1.8 %collective-permute-start.16 = (bf16[512,128]{1,0:T(8,128)(2,1)S(1)}, bf16[512,128]{1,0:T(8,128)(2,1)S(1)}, u32[]{:S(2)}, u32[]{:S(2)}) collective-permute-start(bf16[512,128]{1,0:T(8,128)(2,1)S(1)} %get-tuple-element.49), channel_id=1, source_target_pairs={{0,6},{2,4},{4,2},{6,0},{1,7},{3,5},{5,3},{7,1},{8,14},{10,12},{12... | collective-permute-start | bytes 393224 | tf_op jit(solution)/shard_map/ppermute | solution.py:394
  82.6 1.2 %collective-permute-start.23 = (bf16[512,128]{1,0:T(8,128)(2,1)S(1)}, bf16[512,128]{1,0:T(8,128)(2,1)S(1)}, u32[]{:S(2)}, u32[]{:S(2)}) collective-permute-start(bf16[512,128]{1,0:T(8,128)(2,1)S(1)} %get-tuple-element.61), channel_id=1, source_target_pairs={{0,6},{2,4},{4,2},{6,0},{1,7},{3,5},{5,3},{7,1},{8,14},{10,12},{12... | collective-permute-start | bytes 393224 | tf_op jit(solution)/shard_map/ppermute | solution.py:394
  83.8 5.4 %collective-permute-done.15.refs_2_ = bf16[512,128]{1,0:T(8,128)(2,1)S(1)} collective-permute-done((bf16[512,128]{1,0:T(8,128)(2,1)S(1)}, bf16[512,128]{1,0:T(8,128)(2,1)S(1)}, u32[]{:S(2)}, u32[]{:S(2)}) %collective-permute-start.15) | collective-permute-done | bytes 131104 | tf_op jit(solution)/shard_map/ppermute | solution.py:394
  89.2 1.2 %shard_map.122 = (bf16[128,2048]{1,0:T(8,128)(2,1)}, bf16[128,1024]{1,0:T(8,128)(2,1)}, bf16[128,1024]{1,0:T(8,128)(2,1)}) custom-call(bf16[512,128]{1,0:T(8,128)(2,1)S(1)} %get-tuple-element.46.refs_0_, bf16[512,128]{1,0:T(8,128)(2,1)S(1)} %collective-permute-done.14.refs_1_, bf16[512,128]{1,0:T(8,128)(2,1)S(1)} %collective-permute-done.15.refs_2_, ...), custom_call_target="tpu_custom_call" | custom-call | bytes 4194304 | tf_op jit(solution)/shard_map/pallas_call | solution.py:543
  (28 shorter events, 0.3 us)
Async XLA Ops:
  0.6 11.0 %collective-permute-start = (f32[4,512]{1,0:T(4,128)}, f32[4,512]{1,0:T(4,128)S(1)}, u32[]{:S(2)}, u32[]{:S(2)}) collective-permute-start(f32[4,512]{1,0:T(4,128)} %param.14), channel_id=1, source_target_pairs={{0,4},{4,0},{1,5},{5,1},{2,6},{6,2},{3,7},{7,3},{8,12},{12,8},{9,1... | collective-permute-start | bytes 24584 | tf_op jit(solution)/shard_map/ppermute | solution.py:417
  2.2 20.4 %collective-permute-start.7 = (bf16[128,2048]{1,0:T(8,128)(2,1)}, bf16[128,2048]{1,0:T(8,128)(2,1)S(1)}, u32[]{:S(2)}, u32[]{:S(2)}) collective-permute-start(bf16[128,2048]{1,0:T(8,128)(2,1)} %refs_0_.3), channel_id=1, source_target_pairs={{8,0},{16,8},{24,16},{9,1},{17,9},{25,17},{10,2},{18,10},{26,18},{... | collective-permute-start | bytes 1572872 | tf_op jit(solution)/shard_map/ppermute | solution.py:407
  6.6 9.3 %collective-permute-start.2 = (bf16[1040,128]{1,0:T(8,128)(2,1)S(1)}, bf16[1040,128]{1,0:T(8,128)(2,1)S(1)}, u32[]{:S(2)}, u32[]{:S(2)}) collective-permute-start(bf16[1040,128]{1,0:T(8,128)(2,1)S(1)} %get-tuple-element.33), channel_id=1, source_target_pairs={{0,2},{2,0},{4,6},{6,4},{1,3},{3,1},{5,7},{7,5},{8,10},{10,8},{12,... | collective-permute-start | bytes 798728 | tf_op jit(solution)/shard_map/ppermute | solution.py:394
  8.2 13.0 %collective-permute-start.3 = (bf16[1040,128]{1,0:T(8,128)(2,1)S(1)}, bf16[1040,128]{1,0:T(8,128)(2,1)S(1)}, u32[]{:S(2)}, u32[]{:S(2)}) collective-permute-start(bf16[1040,128]{1,0:T(8,128)(2,1)S(1)} %get-tuple-element.34), channel_id=1, source_target_pairs={{0,4},{2,6},{4,0},{6,2},{1,5},{3,7},{5,1},{7,3},{8,12},{10,14},{12... | collective-permute-start | bytes 798728 | tf_op jit(solution)/shard_map/ppermute | solution.py:394
  8.7 12.5 %collective-permute-start.4 = (bf16[1040,128]{1,0:T(8,128)(2,1)S(1)}, bf16[1040,128]{1,0:T(8,128)(2,1)S(1)}, u32[]{:S(2)}, u32[]{:S(2)}) collective-permute-start(bf16[1040,128]{1,0:T(8,128)(2,1)S(1)} %get-tuple-element.35), channel_id=1, source_target_pairs={{0,6},{2,4},{4,2},{6,0},{1,7},{3,5},{5,3},{7,1},{8,14},{10,12},{12... | collective-permute-start | bytes 798728 | tf_op jit(solution)/shard_map/ppermute | solution.py:394
  12.3 1.2 %collective-permute-start.1 = (f32[2,4,512]{2,1,0:T(4,128)S(1)}, f32[2,4,512]{2,1,0:T(4,128)S(1)}, u32[]{:S(2)}, u32[]{:S(2)}) collective-permute-start(f32[2,4,512]{2,1,0:T(4,128)S(1)} %pad_maximum_fusion), channel_id=1, source_target_pairs={{0,1},{1,0},{2,3},{3,2},{4,5},{5,4},{6,7},{7,6},{8,9},{9,8},{10,11... | collective-permute-start | bytes 49160 | tf_op jit(solution)/shard_map/ppermute | solution.py:402
  21.3 12.9 %collective-permute-start.5 = (bf16[4,512,128]{2,1,0:T(8,128)(2,1)S(1)}, bf16[4,512,128]{2,1,0:T(8,128)(2,1)S(1)}, u32[]{:S(2)}, u32[]{:S(2)}) collective-permute-start(bf16[4,512,128]{2,1,0:T(8,128)(2,1)S(1)} %get-tuple-element.36.refs_1_), channel_id=1, source_target_pairs={{0,8},{8,16},{16,24},{1,9},{9,17},{17,25},{2,10},{10,18},{18,26},{... | collective-permute-start | bytes 1572872 | tf_op jit(solution)/shard_map/ppermute | solution.py:407
  23.8 6.6 %collective-permute-start.8 = (bf16[1024,128]{1,0:T(8,128)(2,1)S(1)}, bf16[1024,128]{1,0:T(8,128)(2,1)S(1)}, u32[]{:S(2)}, u32[]{:S(2)}) collective-permute-start(bf16[1024,128]{1,0:T(8,128)(2,1)S(1)} %get-tuple-element.38), channel_id=1, source_target_pairs={{0,2},{2,0},{4,6},{6,4},{1,3},{3,1},{5,7},{7,5},{8,10},{10,8},{12,... | collective-permute-start | bytes 786440 | tf_op jit(solution)/shard_map/ppermute | solution.py:394
  24.5 18.8 %collective-permute-start.11 = (bf16[4,512,128]{2,1,0:T(8,128)(2,1)S(1)}, bf16[4,512,128]{2,1,0:T(8,128)(2,1)S(1)}, u32[]{:S(2)}, u32[]{:S(2)}) collective-permute-start(bf16[4,512,128]{2,1,0:T(8,128)(2,1)S(1)} %get-tuple-element.36.refs_1_), channel_id=1, source_target_pairs={{0,1},{1,0},{2,3},{3,2},{4,5},{5,4},{6,7},{7,6},{8,9},{9,8},{10,11... | collective-permute-start | bytes 1572872 | tf_op jit(solution)/shard_map/ppermute | solution.py:402
  24.6 24.3 %collective-permute-start.12 = (bf16[4,544,128]{2,1,0:T(8,128)(2,1)S(1)}, bf16[4,544,128]{2,1,0:T(8,128)(2,1)S(1)}, u32[]{:S(2)}, u32[]{:S(2)}) collective-permute-start(bf16[4,544,128]{2,1,0:T(8,128)(2,1)S(1)} %get-tuple-element.41.refs_7_), channel_id=1, source_target_pairs={{8,0},{16,8},{24,16},{9,1},{17,9},{25,17},{10,2},{18,10},{26,18},{... | collective-permute-start | bytes 1671176 | tf_op jit(solution)/shard_map/ppermute | solution.py:407
  29.2 14.1 %collective-permute-start.9 = (bf16[1024,128]{1,0:T(8,128)(2,1)S(1)}, bf16[1024,128]{1,0:T(8,128)(2,1)S(1)}, u32[]{:S(2)}, u32[]{:S(2)}) collective-permute-start(bf16[1024,128]{1,0:T(8,128)(2,1)S(1)} %get-tuple-element.39), channel_id=1, source_target_pairs={{0,4},{2,6},{4,0},{6,2},{1,5},{3,7},{5,1},{7,3},{8,12},{10,14},{12... | collective-permute-start | bytes 786440 | tf_op jit(solution)/shard_map/ppermute | solution.py:394
  30.4 12.9 %collective-permute-start.10 = (bf16[1024,128]{1,0:T(8,128)(2,1)S(1)}, bf16[1024,128]{1,0:T(8,128)(2,1)S(1)}, u32[]{:S(2)}, u32[]{:S(2)}) collective-permute-start(bf16[1024,128]{1,0:T(8,128)(2,1)S(1)} %get-tuple-element.40), channel_id=1, source_target_pairs={{0,6},{2,4},{4,2},{6,0},{1,7},{3,5},{5,3},{7,1},{8,14},{10,12},{12... | collective-permute-start | bytes 786440 | tf_op jit(solution)/shard_map/ppermute | solution.py:394
  34.2 14.7 %collective-permute-start.6 = (bf16[4,512,128]{2,1,0:T(8,128)(2,1)S(1)}, bf16[4,512,128]{2,1,0:T(8,128)(2,1)S(1)}, u32[]{:S(2)}, u32[]{:S(2)}) collective-permute-start(bf16[4,512,128]{2,1,0:T(8,128)(2,1)S(1)} %collective-permute-done.5.refs_1_), channel_id=1, source_target_pairs={{0,1},{1,0},{2,3},{3,2},{4,5},{5,4},{6,7},{7,6},{8,9},{9,8},{10,11... | collective-permute-start | bytes 1572872 | tf_op jit(solution)/shard_map/ppermute | solution.py:402
  54.1 2.0 %collective-permute-start.21 = (bf16[4,512,128]{2,1,0:T(8,128)(2,1)S(1)}, bf16[4,512,128]{2,1,0:T(8,128)(2,1)S(1)}, u32[]{:S(2)}, u32[]{:S(2)}) collective-permute-start(bf16[4,512,128]{2,1,0:T(8,128)(2,1)S(1)} %get-tuple-element.57), channel_id=1, source_target_pairs={{0,1},{1,0},{2,3},{3,2},{4,5},{5,4},{6,7},{7,6},{8,9},{9,8},{10,11... | collective-permute-start | bytes 1572872 | tf_op jit(solution)/shard_map/ppermute | solution.py:402
  54.1 9.9 %collective-permute-start.17 = (bf16[4,512,128]{2,1,0:T(8,128)(2,1)S(1)}, bf16[4,512,128]{2,1,0:T(8,128)(2,1)S(1)}, u32[]{:S(2)}, u32[]{:S(2)}) collective-permute-start(bf16[4,512,128]{2,1,0:T(8,128)(2,1)S(1)} %get-tuple-element.51), channel_id=1, source_target_pairs={{0,1},{1,0},{2,3},{3,2},{4,5},{5,4},{6,7},{7,6},{8,9},{9,8},{10,11... | collective-permute-start | bytes 1572872 | tf_op jit(solution)/shard_map/ppermute | solution.py:402
  54.6 17.4 %collective-permute-start.13 = (bf16[4,2,128,256]{3,2,1,0:T(8,128)(2,1)S(1)}, bf16[4,2,128,256]{3,2,1,0:T(8,128)(2,1)S(1)}, u32[]{:S(2)}, u32[]{:S(2)}) collective-permute-start(bf16[4,2,128,256]{3,2,1,0:T(8,128)(2,1)S(1)} %get-tuple-element.45), channel_id=1, source_target_pairs={{0,8},{8,16},{16,24},{1,9},{9,17},{17,25},{2,10},{10,18},{18,26},{... | collective-permute-start | bytes 1572872 | tf_op jit(solution)/shard_map/ppermute | solution.py:407
  56.2 19.7 %collective-permute-start.22 = (bf16[1024,128]{1,0:T(8,128)(2,1)S(1)}, bf16[1024,128]{1,0:T(8,128)(2,1)S(1)}, u32[]{:S(2)}, u32[]{:S(2)}) collective-permute-start(bf16[1024,128]{1,0:T(8,128)(2,1)S(1)} %get-tuple-element.58), channel_id=1, source_target_pairs={{8,0},{16,8},{24,16},{9,1},{17,9},{25,17},{10,2},{18,10},{26,18},{... | collective-permute-start | bytes 786440 | tf_op jit(solution)/shard_map/ppermute | solution.py:407
  62.0 11.5 %collective-permute-start.24 = (bf16[512,128]{1,0:T(8,128)(2,1)S(1)}, bf16[512,128]{1,0:T(8,128)(2,1)S(1)}, u32[]{:S(2)}, u32[]{:S(2)}) collective-permute-start(bf16[512,128]{1,0:T(8,128)(2,1)S(1)} %get-tuple-element.59), channel_id=1, source_target_pairs={{0,2},{2,0},{4,6},{6,4},{1,3},{3,1},{5,7},{7,5},{8,10},{10,8},{12,... | collective-permute-start | bytes 393224 | tf_op jit(solution)/shard_map/ppermute | solution.py:394
  63.5 11.8 %collective-permute-start.25 = (bf16[512,128]{1,0:T(8,128)(2,1)S(1)}, bf16[512,128]{1,0:T(8,128)(2,1)S(1)}, u32[]{:S(2)}, u32[]{:S(2)}) collective-permute-start(bf16[512,128]{1,0:T(8,128)(2,1)S(1)} %get-tuple-element.60), channel_id=1, source_target_pairs={{0,4},{2,6},{4,0},{6,2},{1,5},{3,7},{5,1},{7,3},{8,12},{10,14},{12... | collective-permute-start | bytes 393224 | tf_op jit(solution)/shard_map/ppermute | solution.py:394
  64.1 15.4 %collective-permute-start.18 = (bf16[512,128]{1,0:T(8,128)(2,1)S(1)}, bf16[512,128]{1,0:T(8,128)(2,1)S(1)}, u32[]{:S(2)}, u32[]{:S(2)}) collective-permute-start(bf16[512,128]{1,0:T(8,128)(2,1)S(1)} %get-tuple-element.53), channel_id=1, source_target_pairs={{0,2},{2,0},{4,6},{6,4},{1,3},{3,1},{5,7},{7,5},{8,10},{10,8},{12,... | collective-permute-start | bytes 393224 | tf_op jit(solution)/shard_map/ppermute | solution.py:394
  72.0 8.8 %collective-permute-start.19 = (bf16[512,128]{1,0:T(8,128)(2,1)S(1)}, bf16[512,128]{1,0:T(8,128)(2,1)S(1)}, u32[]{:S(2)}, u32[]{:S(2)}) collective-permute-start(bf16[512,128]{1,0:T(8,128)(2,1)S(1)} %get-tuple-element.54), channel_id=1, source_target_pairs={{0,4},{2,6},{4,0},{6,2},{1,5},{3,7},{5,1},{7,3},{8,12},{10,14},{12... | collective-permute-start | bytes 393224 | tf_op jit(solution)/shard_map/ppermute | solution.py:394
  73.5 9.1 %collective-permute-start.20 = (bf16[512,128]{1,0:T(8,128)(2,1)S(1)}, bf16[512,128]{1,0:T(8,128)(2,1)S(1)}, u32[]{:S(2)}, u32[]{:S(2)}) collective-permute-start(bf16[512,128]{1,0:T(8,128)(2,1)S(1)} %get-tuple-element.55), channel_id=1, source_target_pairs={{0,6},{2,4},{4,2},{6,0},{1,7},{3,5},{5,3},{7,1},{8,14},{10,12},{12... | collective-permute-start | bytes 393224 | tf_op jit(solution)/shard_map/ppermute | solution.py:394
  75.4 8.4 %collective-permute-start.14 = (bf16[512,128]{1,0:T(8,128)(2,1)S(1)}, bf16[512,128]{1,0:T(8,128)(2,1)S(1)}, u32[]{:S(2)}, u32[]{:S(2)}) collective-permute-start(bf16[512,128]{1,0:T(8,128)(2,1)S(1)} %get-tuple-element.47), channel_id=1, source_target_pairs={{0,2},{2,0},{4,6},{6,4},{1,3},{3,1},{5,7},{7,5},{8,10},{10,8},{12,... | collective-permute-start | bytes 393224 | tf_op jit(solution)/shard_map/ppermute | solution.py:394
  75.9 13.3 %collective-permute-start.26 = (bf16[1024,128]{1,0:T(8,128)(2,1)S(1)}, bf16[1024,128]{1,0:T(8,128)(2,1)S(1)}, u32[]{:S(2)}, u32[]{:S(2)}) collective-permute-start(bf16[1024,128]{1,0:T(8,128)(2,1)S(1)} %shard_map.121), channel_id=1, source_target_pairs={{8,0},{16,8},{24,16},{9,1},{17,9},{25,17},{10,2},{18,10},{26,18},{... | collective-permute-start | bytes 786440 | tf_op jit(solution)/shard_map/ppermute | solution.py:407
  79.6 9.6 %collective-permute-start.15 = (bf16[512,128]{1,0:T(8,128)(2,1)S(1)}, bf16[512,128]{1,0:T(8,128)(2,1)S(1)}, u32[]{:S(2)}, u32[]{:S(2)}) collective-permute-start(bf16[512,128]{1,0:T(8,128)(2,1)S(1)} %get-tuple-element.48), channel_id=1, source_target_pairs={{0,4},{2,6},{4,0},{6,2},{1,5},{3,7},{5,1},{7,3},{8,12},{10,14},{12... | collective-permute-start | bytes 393224 | tf_op jit(solution)/shard_map/ppermute | solution.py:394
  80.9 8.3 %collective-permute-start.16 = (bf16[512,128]{1,0:T(8,128)(2,1)S(1)}, bf16[512,128]{1,0:T(8,128)(2,1)S(1)}, u32[]{:S(2)}, u32[]{:S(2)}) collective-permute-start(bf16[512,128]{1,0:T(8,128)(2,1)S(1)} %get-tuple-element.49), channel_id=1, source_target_pairs={{0,6},{2,4},{4,2},{6,0},{1,7},{3,5},{5,3},{7,1},{8,14},{10,12},{12... | collective-permute-start | bytes 393224 | tf_op jit(solution)/shard_map/ppermute | solution.py:394
  82.6 6.6 %collective-permute-start.23 = (bf16[512,128]{1,0:T(8,128)(2,1)S(1)}, bf16[512,128]{1,0:T(8,128)(2,1)S(1)}, u32[]{:S(2)}, u32[]{:S(2)}) collective-permute-start(bf16[512,128]{1,0:T(8,128)(2,1)S(1)} %get-tuple-element.61), channel_id=1, source_target_pairs={{0,6},{2,4},{4,2},{6,0},{1,7},{3,5},{5,3},{7,1},{8,14},{10,12},{12... | collective-permute-start | bytes 393224 | tf_op jit(solution)/shard_map/ppermute | solution.py:394

commit v6 on v5

--- a/solution.py
+++ b/solution.py
@@ -98,14 +98,14 @@
 def load(arrived, pairs):
     started = []
     for n, (source, target) in enumerate(pairs):
-        half = target.shape[0] // 2
-        halves = []
-        for part in range(2):
-            rows = pl.ds(part * half, half)
+        size = target.shape[0] // 4
+        parts = []
+        for part in range(4):
+            rows = pl.ds(part * size, size)
             copy = pltpu.make_async_copy(source.at[rows], target.at[rows], arrived.at[n, part])
             copy.start()
-            halves.append(copy)
-        started.append(halves)
+            parts.append(copy)
+        started.append(parts)
 
     def wait_for(n):
         for copy in started[n]:
@@ -450,7 +450,7 @@
         [like(plan.q_rows + plan.kv_rows + plan.aux_sent)] * chips,
         [IN_HBM] * len(arrays),
         scratch=[pltpu.VMEM(a.shape, a.dtype) for a in arrays]
-        + [pltpu.VMEM((LANES, LANES), F32), pltpu.SemaphoreType.DMA((len(arrays), 2))],
+        + [pltpu.VMEM((LANES, LANES), F32), pltpu.SemaphoreType.DMA((len(arrays), 4))],
     )(*map(kept, arrays))
     do_own, kv_own = call(
         functools.partial(assemble_kernel, plan),
@@ -469,7 +469,7 @@
             functools.partial(pack_q_kernel, plan),
             [like(len(raw) * plan.q_rows)] * chips,
             [IN_HBM] + [WHOLE] * (len(raw) - 1),
-            scratch=[pltpu.VMEM(queries.shape, BF16), pltpu.SemaphoreType.DMA((1, 2))],
+            scratch=[pltpu.VMEM(queries.shape, BF16), pltpu.SemaphoreType.DMA((1, 4))],
         )(kept(queries), *raw[1:]),
     )
     up = [(kv, swap(kv)) for kv in up]

time: 91.2 us -> 91.5 us (level)
  transfers between devices with their start and end apart: 27 -> 27, of which waited for: 8 -> 8; matrix products, arithmetic and copies ran while one was open for 4% -> 4% of each run, Pallas kernels for 10% -> 11%
where the time goes in v6:
time: 91.5 us; the launch traced here: 90.7 us
  starting transfers between devices  39.4 us (43%)
  waiting for transfers between devices  31 us (34%)
  Pallas kernels  15.9 us (17%)
  other arithmetic  3.45 us (4%)
    ppermute x15, waiting for transfers between devices, send_in_plane(): return lax.ppermute(piece, CROSS, [(i, i ^ mask) for i in range(chips)])  21.2 us
    ppermute x6, starting transfers between devices, along(): return lax.ppermute(value, 'z', pairs)  19 us
    ppermute x15, starting transfers between devices, send_in_plane(): return lax.ppermute(piece, CROSS, [(i, i ^ mask) for i in range(chips)])  18.3 us
    pallas_call x3, Pallas kernels, body(): call(functools.partial(role_kernel, plan, j, has_dq, carried is not None,...  10.7 us
    ppermute x6, waiting for transfers between devices, along(): return lax.ppermute(value, 'z', pairs)  8.51 us
    pallas_call x1, Pallas kernels, body(): call(functools.partial(pack_kernel, plan), [like(plan.q_rows + plan.kv_ro...  2.16 us
  transfers between devices with their start and end apart: 27, of which 8 were waited for; matrix products, arithmetic and copies ran while one was open for 4% of the time, Pallas kernels for 11%

profile of v6, /device:TPU:24, one launch (start us, length us, event | category | flops | bytes accessed | tf_op | source)
XLA Modules:
  0.0 90.7 jit_solution(15704951694150800259)
XLA Ops:
  0.6 1.6 %collective-permute-start = (f32[4,512]{1,0:T(4,128)}, f32[4,512]{1,0:T(4,128)S(1)}, u32[]{:S(2)}, u32[]{:S(2)}) collective-permute-start(f32[4,512]{1,0:T(4,128)} %param.14), channel_id=1, source_target_pairs={{0,4},{4,0},{1,5},{5,1},{2,6},{6,2},{3,7},{7,3},{8,12},{12,8},{9,1... | collective-permute-start | bytes 24584 | tf_op jit(solution)/shard_map/ppermute | solution.py:417
  2.2 2.4 %collective-permute-start.7 = (bf16[128,2048]{1,0:T(8,128)(2,1)}, bf16[128,2048]{1,0:T(8,128)(2,1)S(1)}, u32[]{:S(2)}, u32[]{:S(2)}) collective-permute-start(bf16[128,2048]{1,0:T(8,128)(2,1)} %refs_0_.3), channel_id=1, source_target_pairs={{8,0},{16,8},{24,16},{9,1},{17,9},{25,17},{10,2},{18,10},{26,18},{... | collective-permute-start | bytes 1572872 | tf_op jit(solution)/shard_map/ppermute | solution.py:407
  4.6 2.2 %shard_map.112 = (bf16[1040,128]{1,0:T(8,128)(2,1)S(1)}, bf16[1040,128]{1,0:T(8,128)(2,1)S(1)}, bf16[1040,128]{1,0:T(8,128)(2,1)S(1)}, bf16[1040,128]{1,0:T(8,128)(2,1)S(1)}) custom-call(bf16[128,2048]{1,0:T(8,128)(2,1)} %refs_0_.2, bf16[128,2048]{1,0:T(8,128)(2,1)} %refs_1_.1, bf16[128,1024]{1,0:T(8,128)(2,1)} %refs_2_.1, bf16[128,1024]{1,0:T(8,128)(2,1)} %refs_3_.1), custom_call_target="tpu_custom_call" | custom-call | bytes 4194304 | tf_op jit(solution)/shard_map/pallas_call | solution.py:448
  6.8 1.6 %collective-permute-start.2 = (bf16[1040,128]{1,0:T(8,128)(2,1)S(1)}, bf16[1040,128]{1,0:T(8,128)(2,1)S(1)}, u32[]{:S(2)}, u32[]{:S(2)}) collective-permute-start(bf16[1040,128]{1,0:T(8,128)(2,1)S(1)} %get-tuple-element.33), channel_id=1, source_target_pairs={{0,2},{2,0},{4,6},{6,4},{1,3},{3,1},{5,7},{7,5},{8,10},{10,8},{12,... | collective-permute-start | bytes 798728 | tf_op jit(solution)/shard_map/ppermute | solution.py:394
  8.3 0.5 collective-permute-start.3
  8.8 1.5 %collective-permute-start.4 = (bf16[1040,128]{1,0:T(8,128)(2,1)S(1)}, bf16[1040,128]{1,0:T(8,128)(2,1)S(1)}, u32[]{:S(2)}, u32[]{:S(2)}) collective-permute-start(bf16[1040,128]{1,0:T(8,128)(2,1)S(1)} %get-tuple-element.35), channel_id=1, source_target_pairs={{0,6},{2,4},{4,2},{6,0},{1,7},{3,5},{5,3},{7,1},{8,14},{10,12},{12... | collective-permute-start | bytes 798728 | tf_op jit(solution)/shard_map/ppermute | solution.py:394
  10.3 0.8 add_bitcast_fusion
  11.1 0.7 add_multiply_fusion
  11.8 0.7 pad_maximum_fusion
  12.6 1.1 %collective-permute-done.1 = f32[2,4,512]{2,1,0:T(4,128)S(1)} collective-permute-done((f32[2,4,512]{2,1,0:T(4,128)S(1)}, f32[2,4,512]{2,1,0:T(4,128)S(1)}, u32[]{:S(2)}, u32[]{:S(2)}) %collective-permute-start.1) | collective-permute-done | bytes 16416 | tf_op jit(solution)/shard_map/ppermute | solution.py:402
  13.7 0.8 fusion.1.refs_0_
  14.5 1.6 %collective-permute-done.2.refs_2_ = bf16[1040,128]{1,0:T(8,128)(2,1)S(1)} collective-permute-done((bf16[1040,128]{1,0:T(8,128)(2,1)S(1)}, bf16[1040,128]{1,0:T(8,128)(2,1)S(1)}, u32[]{:S(2)}, u32[]{:S(2)}) %collective-permute-start.2) | collective-permute-done | bytes 266272 | tf_op jit(solution)/shard_map/ppermute | solution.py:394
  16.1 5.2 %collective-permute-done.3.refs_3_ = bf16[1040,128]{1,0:T(8,128)(2,1)S(1)} collective-permute-done((bf16[1040,128]{1,0:T(8,128)(2,1)S(1)}, bf16[1040,128]{1,0:T(8,128)(2,1)S(1)}, u32[]{:S(2)}, u32[]{:S(2)}) %collective-permute-start.3) | collective-permute-done | bytes 266272 | tf_op jit(solution)/shard_map/ppermute | solution.py:394
  21.3 0.1 shard_map.113
  21.4 1.3 %collective-permute-start.5 = (bf16[4,512,128]{2,1,0:T(8,128)(2,1)S(1)}, bf16[4,512,128]{2,1,0:T(8,128)(2,1)S(1)}, u32[]{:S(2)}, u32[]{:S(2)}) collective-permute-start(bf16[4,512,128]{2,1,0:T(8,128)(2,1)S(1)} %get-tuple-element.36.refs_1_), channel_id=1, source_target_pairs={{0,8},{8,16},{16,24},{1,9},{9,17},{17,25},{2,10},{10,18},{18,26},{... | collective-permute-start | bytes 1572872 | tf_op jit(solution)/shard_map/ppermute | solution.py:407
  22.7 0.1 broadcast_compare_fusion
  22.8 1.3 %shard_map.114 = (bf16[1024,128]{1,0:T(8,128)(2,1)S(1)}, bf16[1024,128]{1,0:T(8,128)(2,1)S(1)}, bf16[1024,128]{1,0:T(8,128)(2,1)S(1)}, bf16[1024,128]{1,0:T(8,128)(2,1)S(1)}) custom-call(bf16[128,2048]{1,0:T(8,128)(2,1)} %refs_0_.3, bf16[128,2048]{1,0:T(8,128)(2,1)S(1)} %collective-permute-done.7.refs_1_), custom_call_target="tpu_custom_call" | custom-call | bytes 4194304 | tf_op jit(solution)/shard_map/pallas_call | solution.py:468
  24.1 0.6 collective-permute-start.8
  24.8 0.1 broadcast_compare_fusion.1
  24.8 4.6 %collective-permute-start.12 = (bf16[4,544,128]{2,1,0:T(8,128)(2,1)S(1)}, bf16[4,544,128]{2,1,0:T(8,128)(2,1)S(1)}, u32[]{:S(2)}, u32[]{:S(2)}) collective-permute-start(bf16[4,544,128]{2,1,0:T(8,128)(2,1)S(1)} %get-tuple-element.41.refs_7_), channel_id=1, source_target_pairs={{8,0},{16,8},{24,16},{9,1},{17,9},{25,17},{10,2},{18,10},{26,18},{... | collective-permute-start | bytes 1671176 | tf_op jit(solution)/shard_map/ppermute | solution.py:407
  29.4 1.3 %collective-permute-start.9 = (bf16[1024,128]{1,0:T(8,128)(2,1)S(1)}, bf16[1024,128]{1,0:T(8,128)(2,1)S(1)}, u32[]{:S(2)}, u32[]{:S(2)}) collective-permute-start(bf16[1024,128]{1,0:T(8,128)(2,1)S(1)} %get-tuple-element.39), channel_id=1, source_target_pairs={{0,4},{2,6},{4,0},{6,2},{1,5},{3,7},{5,1},{7,3},{8,12},{10,14},{12... | collective-permute-start | bytes 786440 | tf_op jit(solution)/shard_map/ppermute | solution.py:394
  30.7 1.7 %collective-permute-start.10 = (bf16[1024,128]{1,0:T(8,128)(2,1)S(1)}, bf16[1024,128]{1,0:T(8,128)(2,1)S(1)}, u32[]{:S(2)}, u32[]{:S(2)}) collective-permute-start(bf16[1024,128]{1,0:T(8,128)(2,1)S(1)} %get-tuple-element.40), channel_id=1, source_target_pairs={{0,6},{2,4},{4,2},{6,0},{1,7},{3,5},{5,3},{7,1},{8,14},{10,12},{12... | collective-permute-start | bytes 786440 | tf_op jit(solution)/shard_map/ppermute | solution.py:394
  32.4 1.9 %collective-permute-done.5.refs_1_ = bf16[4,512,128]{2,1,0:T(8,128)(2,1)S(1)} collective-permute-done((bf16[4,512,128]{2,1,0:T(8,128)(2,1)S(1)}, bf16[4,512,128]{2,1,0:T(8,128)(2,1)S(1)}, u32[]{:S(2)}, u32[]{:S(2)}) %collective-permute-start.5) | collective-permute-done | bytes 524320 | tf_op jit(solution)/shard_map/ppermute | solution.py:407
  34.3 0.2 fusion.5
  34.6 9.0 %collective-permute-done.9.refs_5_ = bf16[1024,128]{1,0:T(8,128)(2,1)S(1)} collective-permute-done((bf16[1024,128]{1,0:T(8,128)(2,1)S(1)}, bf16[1024,128]{1,0:T(8,128)(2,1)S(1)}, u32[]{:S(2)}, u32[]{:S(2)}) %collective-permute-start.9) | collective-permute-done | bytes 262176 | tf_op jit(solution)/shard_map/ppermute | solution.py:394
  43.5 5.5 %shard_map.115 = (f32[4,2,128,256]{3,2,1,0:T(8,128)S(1)}, f32[4,512,128]{2,1,0:T(8,128)S(1)}, bf16[4,512,128]{2,1,0:T(8,128)(2,1)S(1)}) custom-call(s32[2,2]{1,0:T(2,128)S(1)} %get-tuple-element.64.refs_0_, bf16[4,512,128]{2,1,0:T(8,128)(2,1)S(1)} %get-tuple-element.36.refs_1_, bf16[4,512,128]{2,1,0:T(8,128)(2,1)S(1)} %collective-permute-done.11.refs_2_, ...), custom_call_target="tpu_custom_call" | custom-call | flops 2684354560 | bytes 4194304 | tf_op jit(solution)/shard_map/pallas_call | solution.py:501
  49.1 1.2 %shard_map.116 = (bf16[4,2,128,256]{3,2,1,0:T(8,128)(2,1)S(1)}, f32[2,4,512,128]{3,2,1,0:T(8,128)S(1)}) custom-call(s32[2,2]{1,0:T(2,128)S(1)} %get-tuple-element.63.refs_0_, bf16[4,512,128]{2,1,0:T(8,128)(2,1)S(1)} %collective-permute-done.5.refs_1_, bf16[4,512,128]{2,1,0:T(8,128)(2,1)S(1)} %collective-permute-done.6.refs_2_, ...), custom_call_target="tpu_custom_call" | custom-call | flops 2684354560 | bytes 4194304 | tf_op jit(solution)/shard_map/pallas_call | solution.py:501
  50.3 4.0 %shard_map.117 = (f32[4,2,128,256]{3,2,1,0:T(8,128)S(1)}, f32[4,512,128]{2,1,0:T(8,128)S(1)}, bf16[4,512,128]{2,1,0:T(8,128)(2,1)S(1)}) custom-call(s32[2,2]{1,0:T(2,128)S(1)} %get-tuple-element.65.refs_0_, bf16[4,512,128]{2,1,0:T(8,128)(2,1)S(1)} %collective-permute-done.5.refs_1_, bf16[4,512,128]{2,1,0:T(8,128)(2,1)S(1)} %collective-permute-done.6.refs_2_, ...), custom_call_target="tpu_custom_call" | custom-call | flops 2684354560 | bytes 4194304 | tf_op jit(solution)/shard_map/pallas_call | solution.py:501
  54.4 0.5 collective-permute-start.17
  54.9 1.3 %collective-permute-start.13 = (bf16[4,2,128,256]{3,2,1,0:T(8,128)(2,1)S(1)}, bf16[4,2,128,256]{3,2,1,0:T(8,128)(2,1)S(1)}, u32[]{:S(2)}, u32[]{:S(2)}) collective-permute-start(bf16[4,2,128,256]{3,2,1,0:T(8,128)(2,1)S(1)} %get-tuple-element.45), channel_id=1, source_target_pairs={{0,8},{8,16},{16,24},{1,9},{9,17},{17,25},{2,10},{10,18},{18,26},{... | collective-permute-start | bytes 1572872 | tf_op jit(solution)/shard_map/ppermute | solution.py:407
  56.2 0.1 collective-permute-done.21.refs_1_
  56.3 0.1 shard_map.120
  56.4 5.8 %collective-permute-start.22 = (bf16[1024,128]{1,0:T(8,128)(2,1)S(1)}, bf16[1024,128]{1,0:T(8,128)(2,1)S(1)}, u32[]{:S(2)}, u32[]{:S(2)}) collective-permute-start(bf16[1024,128]{1,0:T(8,128)(2,1)S(1)} %get-tuple-element.58), channel_id=1, source_target_pairs={{8,0},{16,8},{24,16},{9,1},{17,9},{25,17},{10,2},{18,10},{26,18},{... | collective-permute-start | bytes 786440 | tf_op jit(solution)/shard_map/ppermute | solution.py:407
  62.2 1.6 %collective-permute-start.24 = (bf16[512,128]{1,0:T(8,128)(2,1)S(1)}, bf16[512,128]{1,0:T(8,128)(2,1)S(1)}, u32[]{:S(2)}, u32[]{:S(2)}) collective-permute-start(bf16[512,128]{1,0:T(8,128)(2,1)S(1)} %get-tuple-element.59), channel_id=1, source_target_pairs={{0,2},{2,0},{4,6},{6,4},{1,3},{3,1},{5,7},{7,5},{8,10},{10,8},{12,... | collective-permute-start | bytes 393224 | tf_op jit(solution)/shard_map/ppermute | solution.py:394
  63.8 0.5 collective-permute-start.25
  64.3 0.1 shard_map.119
  64.4 1.3 %collective-permute-start.18 = (bf16[512,128]{1,0:T(8,128)(2,1)S(1)}, bf16[512,128]{1,0:T(8,128)(2,1)S(1)}, u32[]{:S(2)}, u32[]{:S(2)}) collective-permute-start(bf16[512,128]{1,0:T(8,128)(2,1)S(1)} %get-tuple-element.53), channel_id=1, source_target_pairs={{0,2},{2,0},{4,6},{6,4},{1,3},{3,1},{5,7},{7,5},{8,10},{10,8},{12,... | collective-permute-start | bytes 393224 | tf_op jit(solution)/shard_map/ppermute | solution.py:394
  65.7 6.6 %collective-permute-done.13.refs_1_ = bf16[4,2,128,256]{3,2,1,0:T(8,128)(2,1)S(1)} collective-permute-done((bf16[4,2,128,256]{3,2,1,0:T(8,128)(2,1)S(1)}, bf16[4,2,128,256]{3,2,1,0:T(8,128)(2,1)S(1)}, u32[]{:S(2)}, u32[]{:S(2)}) %collective-permute-start.13) | collective-permute-done | bytes 524320 | tf_op jit(solution)/shard_map/ppermute | solution.py:407
  72.3 1.2 %collective-permute-start.19 = (bf16[512,128]{1,0:T(8,128)(2,1)S(1)}, bf16[512,128]{1,0:T(8,128)(2,1)S(1)}, u32[]{:S(2)}, u32[]{:S(2)}) collective-permute-start(bf16[512,128]{1,0:T(8,128)(2,1)S(1)} %get-tuple-element.54), channel_id=1, source_target_pairs={{0,4},{2,6},{4,0},{6,2},{1,5},{3,7},{5,1},{7,3},{8,12},{10,14},{12... | collective-permute-start | bytes 393224 | tf_op jit(solution)/shard_map/ppermute | solution.py:394
  73.5 0.2 shard_map.118
  73.8 1.8 %collective-permute-start.20 = (bf16[512,128]{1,0:T(8,128)(2,1)S(1)}, bf16[512,128]{1,0:T(8,128)(2,1)S(1)}, u32[]{:S(2)}, u32[]{:S(2)}) collective-permute-start(bf16[512,128]{1,0:T(8,128)(2,1)S(1)} %get-tuple-element.55), channel_id=1, source_target_pairs={{0,6},{2,4},{4,2},{6,0},{1,7},{3,5},{5,3},{7,1},{8,14},{10,12},{12... | collective-permute-start | bytes 393224 | tf_op jit(solution)/shard_map/ppermute | solution.py:394
  75.6 0.5 collective-permute-start.14
  76.1 3.7 %collective-permute-start.26 = (bf16[1024,128]{1,0:T(8,128)(2,1)S(1)}, bf16[1024,128]{1,0:T(8,128)(2,1)S(1)}, u32[]{:S(2)}, u32[]{:S(2)}) collective-permute-start(bf16[1024,128]{1,0:T(8,128)(2,1)S(1)} %shard_map.121), channel_id=1, source_target_pairs={{8,0},{16,8},{24,16},{9,1},{17,9},{25,17},{10,2},{18,10},{26,18},{... | collective-permute-start | bytes 786440 | tf_op jit(solution)/shard_map/ppermute | solution.py:407
  79.8 1.3 %collective-permute-start.15 = (bf16[512,128]{1,0:T(8,128)(2,1)S(1)}, bf16[512,128]{1,0:T(8,128)(2,1)S(1)}, u32[]{:S(2)}, u32[]{:S(2)}) collective-permute-start(bf16[512,128]{1,0:T(8,128)(2,1)S(1)} %get-tuple-element.48), channel_id=1, source_target_pairs={{0,4},{2,6},{4,0},{6,2},{1,5},{3,7},{5,1},{7,3},{8,12},{10,14},{12... | collective-permute-start | bytes 393224 | tf_op jit(solution)/shard_map/ppermute | solution.py:394
  81.1 1.8 %collective-permute-start.16 = (bf16[512,128]{1,0:T(8,128)(2,1)S(1)}, bf16[512,128]{1,0:T(8,128)(2,1)S(1)}, u32[]{:S(2)}, u32[]{:S(2)}) collective-permute-start(bf16[512,128]{1,0:T(8,128)(2,1)S(1)} %get-tuple-element.49), channel_id=1, source_target_pairs={{0,6},{2,4},{4,2},{6,0},{1,7},{3,5},{5,3},{7,1},{8,14},{10,12},{12... | collective-permute-start | bytes 393224 | tf_op jit(solution)/shard_map/ppermute | solution.py:394
  82.9 1.2 %collective-permute-start.23 = (bf16[512,128]{1,0:T(8,128)(2,1)S(1)}, bf16[512,128]{1,0:T(8,128)(2,1)S(1)}, u32[]{:S(2)}, u32[]{:S(2)}) collective-permute-start(bf16[512,128]{1,0:T(8,128)(2,1)S(1)} %get-tuple-element.61), channel_id=1, source_target_pairs={{0,6},{2,4},{4,2},{6,0},{1,7},{3,5},{5,3},{7,1},{8,14},{10,12},{12... | collective-permute-start | bytes 393224 | tf_op jit(solution)/shard_map/ppermute | solution.py:394
  84.1 5.4 %collective-permute-done.15.refs_2_ = bf16[512,128]{1,0:T(8,128)(2,1)S(1)} collective-permute-done((bf16[512,128]{1,0:T(8,128)(2,1)S(1)}, bf16[512,128]{1,0:T(8,128)(2,1)S(1)}, u32[]{:S(2)}, u32[]{:S(2)}) %collective-permute-start.15) | collective-permute-done | bytes 131104 | tf_op jit(solution)/shard_map/ppermute | solution.py:394
  89.5 1.2 %shard_map.122 = (bf16[128,2048]{1,0:T(8,128)(2,1)}, bf16[128,1024]{1,0:T(8,128)(2,1)}, bf16[128,1024]{1,0:T(8,128)(2,1)}) custom-call(bf16[512,128]{1,0:T(8,128)(2,1)S(1)} %get-tuple-element.46.refs_0_, bf16[512,128]{1,0:T(8,128)(2,1)S(1)} %collective-permute-done.14.refs_1_, bf16[512,128]{1,0:T(8,128)(2,1)S(1)} %collective-permute-done.15.refs_2_, ...), custom_call_target="tpu_custom_call" | custom-call | bytes 4194304 | tf_op jit(solution)/shard_map/pallas_call | solution.py:543
  (28 shorter events, 0.3 us)
Async XLA Ops:
  0.6 11.2 %collective-permute-start = (f32[4,512]{1,0:T(4,128)}, f32[4,512]{1,0:T(4,128)S(1)}, u32[]{:S(2)}, u32[]{:S(2)}) collective-permute-start(f32[4,512]{1,0:T(4,128)} %param.14), channel_id=1, source_target_pairs={{0,4},{4,0},{1,5},{5,1},{2,6},{6,2},{3,7},{7,3},{8,12},{12,8},{9,1... | collective-permute-start | bytes 24584 | tf_op jit(solution)/shard_map/ppermute | solution.py:417
  2.2 20.6 %collective-permute-start.7 = (bf16[128,2048]{1,0:T(8,128)(2,1)}, bf16[128,2048]{1,0:T(8,128)(2,1)S(1)}, u32[]{:S(2)}, u32[]{:S(2)}) collective-permute-start(bf16[128,2048]{1,0:T(8,128)(2,1)} %refs_0_.3), channel_id=1, source_target_pairs={{8,0},{16,8},{24,16},{9,1},{17,9},{25,17},{10,2},{18,10},{26,18},{... | collective-permute-start | bytes 1572872 | tf_op jit(solution)/shard_map/ppermute | solution.py:407
  6.8 9.3 %collective-permute-start.2 = (bf16[1040,128]{1,0:T(8,128)(2,1)S(1)}, bf16[1040,128]{1,0:T(8,128)(2,1)S(1)}, u32[]{:S(2)}, u32[]{:S(2)}) collective-permute-start(bf16[1040,128]{1,0:T(8,128)(2,1)S(1)} %get-tuple-element.33), channel_id=1, source_target_pairs={{0,2},{2,0},{4,6},{6,4},{1,3},{3,1},{5,7},{7,5},{8,10},{10,8},{12,... | collective-permute-start | bytes 798728 | tf_op jit(solution)/shard_map/ppermute | solution.py:394
  8.3 13.0 %collective-permute-start.3 = (bf16[1040,128]{1,0:T(8,128)(2,1)S(1)}, bf16[1040,128]{1,0:T(8,128)(2,1)S(1)}, u32[]{:S(2)}, u32[]{:S(2)}) collective-permute-start(bf16[1040,128]{1,0:T(8,128)(2,1)S(1)} %get-tuple-element.34), channel_id=1, source_target_pairs={{0,4},{2,6},{4,0},{6,2},{1,5},{3,7},{5,1},{7,3},{8,12},{10,14},{12... | collective-permute-start | bytes 798728 | tf_op jit(solution)/shard_map/ppermute | solution.py:394
  8.8 12.5 %collective-permute-start.4 = (bf16[1040,128]{1,0:T(8,128)(2,1)S(1)}, bf16[1040,128]{1,0:T(8,128)(2,1)S(1)}, u32[]{:S(2)}, u32[]{:S(2)}) collective-permute-start(bf16[1040,128]{1,0:T(8,128)(2,1)S(1)} %get-tuple-element.35), channel_id=1, source_target_pairs={{0,6},{2,4},{4,2},{6,0},{1,7},{3,5},{5,3},{7,1},{8,14},{10,12},{12... | collective-permute-start | bytes 798728 | tf_op jit(solution)/shard_map/ppermute | solution.py:394
  12.5 1.2 %collective-permute-start.1 = (f32[2,4,512]{2,1,0:T(4,128)S(1)}, f32[2,4,512]{2,1,0:T(4,128)S(1)}, u32[]{:S(2)}, u32[]{:S(2)}) collective-permute-start(f32[2,4,512]{2,1,0:T(4,128)S(1)} %pad_maximum_fusion), channel_id=1, source_target_pairs={{0,1},{1,0},{2,3},{3,2},{4,5},{5,4},{6,7},{7,6},{8,9},{9,8},{10,11... | collective-permute-start | bytes 49160 | tf_op jit(solution)/shard_map/ppermute | solution.py:402
  21.4 12.9 %collective-permute-start.5 = (bf16[4,512,128]{2,1,0:T(8,128)(2,1)S(1)}, bf16[4,512,128]{2,1,0:T(8,128)(2,1)S(1)}, u32[]{:S(2)}, u32[]{:S(2)}) collective-permute-start(bf16[4,512,128]{2,1,0:T(8,128)(2,1)S(1)} %get-tuple-element.36.refs_1_), channel_id=1, source_target_pairs={{0,8},{8,16},{16,24},{1,9},{9,17},{17,25},{2,10},{10,18},{18,26},{... | collective-permute-start | bytes 1572872 | tf_op jit(solution)/shard_map/ppermute | solution.py:407
  24.1 6.6 %collective-permute-start.8 = (bf16[1024,128]{1,0:T(8,128)(2,1)S(1)}, bf16[1024,128]{1,0:T(8,128)(2,1)S(1)}, u32[]{:S(2)}, u32[]{:S(2)}) collective-permute-start(bf16[1024,128]{1,0:T(8,128)(2,1)S(1)} %get-tuple-element.38), channel_id=1, source_target_pairs={{0,2},{2,0},{4,6},{6,4},{1,3},{3,1},{5,7},{7,5},{8,10},{10,8},{12,... | collective-permute-start | bytes 786440 | tf_op jit(solution)/shard_map/ppermute | solution.py:394
  24.8 18.8 %collective-permute-start.11 = (bf16[4,512,128]{2,1,0:T(8,128)(2,1)S(1)}, bf16[4,512,128]{2,1,0:T(8,128)(2,1)S(1)}, u32[]{:S(2)}, u32[]{:S(2)}) collective-permute-start(bf16[4,512,128]{2,1,0:T(8,128)(2,1)S(1)} %get-tuple-element.36.refs_1_), channel_id=1, source_target_pairs={{0,1},{1,0},{2,3},{3,2},{4,5},{5,4},{6,7},{7,6},{8,9},{9,8},{10,11... | collective-permute-start | bytes 1572872 | tf_op jit(solution)/shard_map/ppermute | solution.py:402
  24.8 24.3 %collective-permute-start.12 = (bf16[4,544,128]{2,1,0:T(8,128)(2,1)S(1)}, bf16[4,544,128]{2,1,0:T(8,128)(2,1)S(1)}, u32[]{:S(2)}, u32[]{:S(2)}) collective-permute-start(bf16[4,544,128]{2,1,0:T(8,128)(2,1)S(1)} %get-tuple-element.41.refs_7_), channel_id=1, source_target_pairs={{8,0},{16,8},{24,16},{9,1},{17,9},{25,17},{10,2},{18,10},{26,18},{... | collective-permute-start | bytes 1671176 | tf_op jit(solution)/shard_map/ppermute | solution.py:407
  29.4 14.1 %collective-permute-start.9 = (bf16[1024,128]{1,0:T(8,128)(2,1)S(1)}, bf16[1024,128]{1,0:T(8,128)(2,1)S(1)}, u32[]{:S(2)}, u32[]{:S(2)}) collective-permute-start(bf16[1024,128]{1,0:T(8,128)(2,1)S(1)} %get-tuple-element.39), channel_id=1, source_target_pairs={{0,4},{2,6},{4,0},{6,2},{1,5},{3,7},{5,1},{7,3},{8,12},{10,14},{12... | collective-permute-start | bytes 786440 | tf_op jit(solution)/shard_map/ppermute | solution.py:394
  30.7 12.9 %collective-permute-start.10 = (bf16[1024,128]{1,0:T(8,128)(2,1)S(1)}, bf16[1024,128]{1,0:T(8,128)(2,1)S(1)}, u32[]{:S(2)}, u32[]{:S(2)}) collective-permute-start(bf16[1024,128]{1,0:T(8,128)(2,1)S(1)} %get-tuple-element.40), channel_id=1, source_target_pairs={{0,6},{2,4},{4,2},{6,0},{1,7},{3,5},{5,3},{7,1},{8,14},{10,12},{12... | collective-permute-start | bytes 786440 | tf_op jit(solution)/shard_map/ppermute | solution.py:394
  34.3 14.8 %collective-permute-start.6 = (bf16[4,512,128]{2,1,0:T(8,128)(2,1)S(1)}, bf16[4,512,128]{2,1,0:T(8,128)(2,1)S(1)}, u32[]{:S(2)}, u32[]{:S(2)}) collective-permute-start(bf16[4,512,128]{2,1,0:T(8,128)(2,1)S(1)} %collective-permute-done.5.refs_1_), channel_id=1, source_target_pairs={{0,1},{1,0},{2,3},{3,2},{4,5},{5,4},{6,7},{7,6},{8,9},{9,8},{10,11... | collective-permute-start | bytes 1572872 | tf_op jit(solution)/shard_map/ppermute | solution.py:402
  54.3 2.0 %collective-permute-start.21 = (bf16[4,512,128]{2,1,0:T(8,128)(2,1)S(1)}, bf16[4,512,128]{2,1,0:T(8,128)(2,1)S(1)}, u32[]{:S(2)}, u32[]{:S(2)}) collective-permute-start(bf16[4,512,128]{2,1,0:T(8,128)(2,1)S(1)} %get-tuple-element.57), channel_id=1, source_target_pairs={{0,1},{1,0},{2,3},{3,2},{4,5},{5,4},{6,7},{7,6},{8,9},{9,8},{10,11... | collective-permute-start | bytes 1572872 | tf_op jit(solution)/shard_map/ppermute | solution.py:402
  54.4 9.9 %collective-permute-start.17 = (bf16[4,512,128]{2,1,0:T(8,128)(2,1)S(1)}, bf16[4,512,128]{2,1,0:T(8,128)(2,1)S(1)}, u32[]{:S(2)}, u32[]{:S(2)}) collective-permute-start(bf16[4,512,128]{2,1,0:T(8,128)(2,1)S(1)} %get-tuple-element.51), channel_id=1, source_target_pairs={{0,1},{1,0},{2,3},{3,2},{4,5},{5,4},{6,7},{7,6},{8,9},{9,8},{10,11... | collective-permute-start | bytes 1572872 | tf_op jit(solution)/shard_map/ppermute | solution.py:402
  54.9 17.4 %collective-permute-start.13 = (bf16[4,2,128,256]{3,2,1,0:T(8,128)(2,1)S(1)}, bf16[4,2,128,256]{3,2,1,0:T(8,128)(2,1)S(1)}, u32[]{:S(2)}, u32[]{:S(2)}) collective-permute-start(bf16[4,2,128,256]{3,2,1,0:T(8,128)(2,1)S(1)} %get-tuple-element.45), channel_id=1, source_target_pairs={{0,8},{8,16},{16,24},{1,9},{9,17},{17,25},{2,10},{10,18},{18,26},{... | collective-permute-start | bytes 1572872 | tf_op jit(solution)/shard_map/ppermute | solution.py:407
  56.4 19.7 %collective-permute-start.22 = (bf16[1024,128]{1,0:T(8,128)(2,1)S(1)}, bf16[1024,128]{1,0:T(8,128)(2,1)S(1)}, u32[]{:S(2)}, u32[]{:S(2)}) collective-permute-start(bf16[1024,128]{1,0:T(8,128)(2,1)S(1)} %get-tuple-element.58), channel_id=1, source_target_pairs={{8,0},{16,8},{24,16},{9,1},{17,9},{25,17},{10,2},{18,10},{26,18},{... | collective-permute-start | bytes 786440 | tf_op jit(solution)/shard_map/ppermute | solution.py:407
  62.2 11.5 %collective-permute-start.24 = (bf16[512,128]{1,0:T(8,128)(2,1)S(1)}, bf16[512,128]{1,0:T(8,128)(2,1)S(1)}, u32[]{:S(2)}, u32[]{:S(2)}) collective-permute-start(bf16[512,128]{1,0:T(8,128)(2,1)S(1)} %get-tuple-element.59), channel_id=1, source_target_pairs={{0,2},{2,0},{4,6},{6,4},{1,3},{3,1},{5,7},{7,5},{8,10},{10,8},{12,... | collective-permute-start | bytes 393224 | tf_op jit(solution)/shard_map/ppermute | solution.py:394
  63.8 11.8 %collective-permute-start.25 = (bf16[512,128]{1,0:T(8,128)(2,1)S(1)}, bf16[512,128]{1,0:T(8,128)(2,1)S(1)}, u32[]{:S(2)}, u32[]{:S(2)}) collective-permute-start(bf16[512,128]{1,0:T(8,128)(2,1)S(1)} %get-tuple-element.60), channel_id=1, source_target_pairs={{0,4},{2,6},{4,0},{6,2},{1,5},{3,7},{5,1},{7,3},{8,12},{10,14},{12... | collective-permute-start | bytes 393224 | tf_op jit(solution)/shard_map/ppermute | solution.py:394
  64.4 15.4 %collective-permute-start.18 = (bf16[512,128]{1,0:T(8,128)(2,1)S(1)}, bf16[512,128]{1,0:T(8,128)(2,1)S(1)}, u32[]{:S(2)}, u32[]{:S(2)}) collective-permute-start(bf16[512,128]{1,0:T(8,128)(2,1)S(1)} %get-tuple-element.53), channel_id=1, source_target_pairs={{0,2},{2,0},{4,6},{6,4},{1,3},{3,1},{5,7},{7,5},{8,10},{10,8},{12,... | collective-permute-start | bytes 393224 | tf_op jit(solution)/shard_map/ppermute | solution.py:394
  72.3 8.8 %collective-permute-start.19 = (bf16[512,128]{1,0:T(8,128)(2,1)S(1)}, bf16[512,128]{1,0:T(8,128)(2,1)S(1)}, u32[]{:S(2)}, u32[]{:S(2)}) collective-permute-start(bf16[512,128]{1,0:T(8,128)(2,1)S(1)} %get-tuple-element.54), channel_id=1, source_target_pairs={{0,4},{2,6},{4,0},{6,2},{1,5},{3,7},{5,1},{7,3},{8,12},{10,14},{12... | collective-permute-start | bytes 393224 | tf_op jit(solution)/shard_map/ppermute | solution.py:394
  73.8 9.1 %collective-permute-start.20 = (bf16[512,128]{1,0:T(8,128)(2,1)S(1)}, bf16[512,128]{1,0:T(8,128)(2,1)S(1)}, u32[]{:S(2)}, u32[]{:S(2)}) collective-permute-start(bf16[512,128]{1,0:T(8,128)(2,1)S(1)} %get-tuple-element.55), channel_id=1, source_target_pairs={{0,6},{2,4},{4,2},{6,0},{1,7},{3,5},{5,3},{7,1},{8,14},{10,12},{12... | collective-permute-start | bytes 393224 | tf_op jit(solution)/shard_map/ppermute | solution.py:394
  75.6 8.4 %collective-permute-start.14 = (bf16[512,128]{1,0:T(8,128)(2,1)S(1)}, bf16[512,128]{1,0:T(8,128)(2,1)S(1)}, u32[]{:S(2)}, u32[]{:S(2)}) collective-permute-start(bf16[512,128]{1,0:T(8,128)(2,1)S(1)} %get-tuple-element.47), channel_id=1, source_target_pairs={{0,2},{2,0},{4,6},{6,4},{1,3},{3,1},{5,7},{7,5},{8,10},{10,8},{12,... | collective-permute-start | bytes 393224 | tf_op jit(solution)/shard_map/ppermute | solution.py:394
  76.1 13.3 %collective-permute-start.26 = (bf16[1024,128]{1,0:T(8,128)(2,1)S(1)}, bf16[1024,128]{1,0:T(8,128)(2,1)S(1)}, u32[]{:S(2)}, u32[]{:S(2)}) collective-permute-start(bf16[1024,128]{1,0:T(8,128)(2,1)S(1)} %shard_map.121), channel_id=1, source_target_pairs={{8,0},{16,8},{24,16},{9,1},{17,9},{25,17},{10,2},{18,10},{26,18},{... | collective-permute-start | bytes 786440 | tf_op jit(solution)/shard_map/ppermute | solution.py:407
  79.8 9.6 %collective-permute-start.15 = (bf16[512,128]{1,0:T(8,128)(2,1)S(1)}, bf16[512,128]{1,0:T(8,128)(2,1)S(1)}, u32[]{:S(2)}, u32[]{:S(2)}) collective-permute-start(bf16[512,128]{1,0:T(8,128)(2,1)S(1)} %get-tuple-element.48), channel_id=1, source_target_pairs={{0,4},{2,6},{4,0},{6,2},{1,5},{3,7},{5,1},{7,3},{8,12},{10,14},{12... | collective-permute-start | bytes 393224 | tf_op jit(solution)/shard_map/ppermute | solution.py:394
  81.1 8.3 %collective-permute-start.16 = (bf16[512,128]{1,0:T(8,128)(2,1)S(1)}, bf16[512,128]{1,0:T(8,128)(2,1)S(1)}, u32[]{:S(2)}, u32[]{:S(2)}) collective-permute-start(bf16[512,128]{1,0:T(8,128)(2,1)S(1)} %get-tuple-element.49), channel_id=1, source_target_pairs={{0,6},{2,4},{4,2},{6,0},{1,7},{3,5},{5,3},{7,1},{8,14},{10,12},{12... | collective-permute-start | bytes 393224 | tf_op jit(solution)/shard_map/ppermute | solution.py:394
  82.9 6.6 %collective-permute-start.23 = (bf16[512,128]{1,0:T(8,128)(2,1)S(1)}, bf16[512,128]{1,0:T(8,128)(2,1)S(1)}, u32[]{:S(2)}, u32[]{:S(2)}) collective-permute-start(bf16[512,128]{1,0:T(8,128)(2,1)S(1)} %get-tuple-element.61), channel_id=1, source_target_pairs={{0,6},{2,4},{4,2},{6,0},{1,7},{3,5},{5,3},{7,1},{8,14},{10,12},{12... | collective-permute-start | bytes 393224 | tf_op jit(solution)/shard_map/ppermute | solution.py:394
